TPU v7x, 512 devices: a whole 4x8x8 slice. The times are simulated.
512 devices in a mesh: dom: 128 (over z, y, core), wa: 4 (over x).
Axes of the slice: x: 4, y: 8, z: 8, core: 2. Of those that a mesh axis runs over, the one named last changes fastest.
Arguments:
- bond_feats: bfloat16 [32768, 256], P('dom'), may hold values from -6 to 6
- cotangent: bfloat16 [32768, 256], P('dom', 'wa'), may hold values from -6 to 6
- bond_count: int32 [128], P('dom'), may hold values from 128 to 256, as said below
- source: int32 [393216], P('dom'), may hold values from 0 to 319, as said below
- cosine: float32 [393216], P('dom'), may hold values from -1 to 1
- w_source: bfloat16 [256, 256], P(None, 'wa'), may hold values from -0.375 to 0.375
- w_target: bfloat16 [256, 256], P(None, 'wa'), may hold values from -0.375 to 0.375
- w_message: bfloat16 [256, 256], P(None, 'wa'), may hold values from -0.375 to 0.375
- w_self: bfloat16 [256, 256], P(None, 'wa'), may hold values from -0.375 to 0.375
- gate_angle: float32 [256], P('wa'), may hold values from -4 to 4
Outputs:
- bond_grad: bfloat16 [32768, 256], P('dom', 'wa')
- grad_source: float32 [256, 256], P('dom', 'wa')
- grad_target: float32 [256, 256], P('dom', 'wa')
- grad_message: float32 [256, 256], P('dom', 'wa')
- grad_self: float32 [256, 256], P('dom', 'wa')
- grad_gate: float32 [256], P('wa')
Inputs may be any that keep to these rules, and one draw needn't show every extreme that they name: `bond_count`: every domain has 128 or more live bonds; some domain has all 256 live. `source`: each angle's other bond is a live row of the extended block of its domain: a ghost row (below 32 or at 288 or above) or 32 plus a live own row.
All inputs are finite; a program needn't handle non-finite values.
Results may differ from a plain program's by a relative error of at most 0.0085.
Values may be sent and summed in bfloat16 or wider, within the bound.
No kernel may reach another device: no remote copies, remote signals or barrier semaphores. Data moves between devices by JAX's collectives and lax.ppermute only.
A program may use at most 64 MiB of HBM per device.

v0:
```python
import jax
import jax.numpy as jnp
from jax import lax
from jax.sharding import Mesh
from jax.sharding import PartitionSpec as P

ARITY = 12
GHOST = 32
DOM = ("dom_0", "dom_1", "dom_2")


epsilon = 1e-06


def padded(block, sides, width):
    for axis, dim in sides:
        count = lax.axis_size(axis)
        forward = [(i, i + 1) for i in range(count - 1)]
        forward.append((count - 1, 0))
        backward = [(target, source) for source, target in forward]
        low = lax.ppermute(
            lax.slice_in_dim(block, block.shape[dim] - width, None, axis=dim), axis, forward
        )
        high = lax.ppermute(lax.slice_in_dim(block, 0, width, axis=dim), axis, backward)
        block = jnp.concatenate([low, block, high], axis=dim)
    return block


def split_up(array, dim, peers):
    shape = array.shape
    tiles = array.reshape(*shape[:dim], peers, shape[dim] // peers, *shape[dim + 1 :])
    return jnp.moveaxis(tiles, dim, 0)


def sum_at_owner(array, axis, dim):
    tiles = split_up(array, dim, lax.axis_size(axis))
    arrived = lax.all_to_all(tiles, axis, split_axis=0, concat_axis=0, tiled=True)
    return arrived.astype(jnp.float32).sum(axis=0)


def shifted(block, axis, distance):
    devices = range(lax.axis_size(axis))
    route = [((i - distance) % len(devices), i) for i in devices]
    return lax.ppermute(block, axis, route)


def sent_and_summed(array, axis, dim):
    peers = lax.axis_size(axis)
    tiles = lax.all_to_all(split_up(array, dim, peers), axis, 0, 0, tiled=True)
    return jnp.sum(tiles, axis=0)


def summed_rows(array, axes, dim):
    far, near = axes
    tiles = split_up(array, dim, lax.axis_size(far))
    nearer = sent_and_summed(tiles, near, dim + 1)
    arrived = lax.all_to_all(nearer, far, split_axis=0, concat_axis=0, tiled=True)
    return arrived.sum(axis=0)


def side_by_side(arrays, axis, dim, along):
    both = jnp.concatenate(arrays, axis=along)
    out, at, gathered = (summed_rows(both, axis, dim), 0, [])
    for a in arrays:
        gathered.append(lax.slice_in_dim(out, at, at + a.shape[along], axis=along))
        at += a.shape[along]
    return tuple(gathered)


def copy_for_each(array, axis):
    copies = jnp.broadcast_to(array, (lax.axis_size(axis), *array.shape))
    return lax.all_to_all(copies, axis, split_axis=0, concat_axis=0, tiled=True)


def over_copies(array, axis):
    return copy_for_each(array, axis).sum(axis=0)


def by_axis(array, axes):
    far, near = axes
    return over_copies(over_copies(array, near), far)


def silu_slope(values):
    sigma = jax.nn.sigmoid(values)
    return sigma * (1.0 + values * (1.0 - sigma))


def per_device(
    bond_feats,
    cotangent,
    bond_count,
    source,
    cosine,
    w_source,
    w_target,
    w_message,
    w_self,
    gate_angle,
):
    capacity = bond_feats.shape[0]
    ext_rows = capacity + 2 * GHOST
    extended = padded(bond_feats, ((DOM, 0),), GHOST)

    def spread(values):
        return jnp.broadcast_to(values[:, None, :], (capacity, ARITY, values.shape[1])).reshape(
            ARITY * capacity, values.shape[1]
        )

    def per_bond(values):
        return values.reshape(capacity, ARITY, values.shape[1]).sum(axis=1)

    rows = jnp.arange(capacity, dtype=jnp.int32)
    count = bond_count[0]
    live = ((rows < count - GHOST) | (rows >= capacity - GHOST)).astype(jnp.float32)
    alive = jnp.broadcast_to(live[:, None], (capacity, ARITY)).reshape(ARITY * capacity)[:, None]
    proj_source = jnp.dot(extended, w_source, preferred_element_type=jnp.float32)
    proj_message = jnp.dot(extended, w_message, preferred_element_type=jnp.float32)
    proj_target = jnp.dot(bond_feats, w_target, preferred_element_type=jnp.float32)
    base = jnp.dot(bond_feats, w_self, preferred_element_type=jnp.float32)
    picked_source = jnp.take(proj_source, source, axis=0)
    picked_message = jnp.take(proj_message, source, axis=0)
    pre = picked_source + spread(proj_target) + cosine[:, None] * gate_angle[None, :]
    sigma = jax.nn.sigmoid(pre)
    gated = sigma * alive
    numer = per_bond(gated * picked_message)
    denom = per_bond(gated) + epsilon
    aggregate = numer / denom
    hidden = base + aggregate
    cot_live = cotangent.astype(jnp.float32) * live[:, None]
    dhidden = cot_live * silu_slope(hidden)
    dnumer = dhidden / denom
    ddenom = -dhidden * aggregate / denom
    dgate = spread(dnumer) * picked_message + spread(ddenom)
    dmessage = gated * spread(dnumer)
    dpre = dgate * sigma * (1.0 - sigma) * alive
    dsource = jax.ops.segment_sum(dpre, source, num_segments=ext_rows)
    dmsg_rows = jax.ops.segment_sum(dmessage, source, num_segments=ext_rows)
    dtarget = per_bond(dpre)
    gate_term = jnp.sum(cosine[:, None] * dpre, axis=0)
    round_source = dsource.astype(jnp.bfloat16)
    round_message = dmsg_rows.astype(jnp.bfloat16)
    round_target = dtarget.astype(jnp.bfloat16)
    round_hidden = dhidden.astype(jnp.bfloat16)
    grad_one = jnp.dot(extended.T, round_source, preferred_element_type=jnp.float32)
    grad_two = jnp.dot(bond_feats.T, round_target, preferred_element_type=jnp.float32)
    grad_four = jnp.dot(extended.T, round_message, preferred_element_type=jnp.float32)
    grad_five = jnp.dot(bond_feats.T, round_hidden, preferred_element_type=jnp.float32)
    dext = jnp.dot(round_source, w_source.T, preferred_element_type=jnp.float32) + jnp.dot(
        round_message, w_message.T, preferred_element_type=jnp.float32
    )
    down = jnp.dot(round_target, w_target.T, preferred_element_type=jnp.float32) + jnp.dot(
        round_hidden, w_self.T, preferred_element_type=jnp.float32
    )
    whole = dext.at[GHOST : GHOST + capacity].add(down)
    summed = sum_at_owner(whole.astype(jnp.bfloat16), "wa", 1)
    own_part = summed[GHOST : GHOST + capacity]
    next_part = shifted(summed[:GHOST], DOM, -1)
    prev_part = shifted(summed[GHOST + capacity :], DOM, 1)
    own_part = own_part.at[capacity - GHOST :].add(next_part)
    own_part = own_part.at[:GHOST].add(prev_part)
    bond_grad = (own_part + cot_live).astype(jnp.bfloat16)
    sums_one, sums_two, sums_four, sums_five = side_by_side(
        (grad_one, grad_two, grad_four, grad_five), (("dom_0", "dom_1"), "dom_2"), 0, 1
    )
    grad_gate = by_axis(gate_term, (("dom_0", "dom_1"), "dom_2"))
    return (bond_grad, sums_one, sums_two, sums_four, sums_five, grad_gate)


def solution(mesh):
    finer = Mesh(mesh.devices.reshape(8, 8, 2, mesh.shape["wa"]), ("dom_0", "dom_1", "dom_2", "wa"))
    return jax.shard_map(
        per_device,
        mesh=finer,
        in_specs=(
            P(DOM, None),
            P(DOM, "wa"),
            P(DOM),
            P(DOM),
            P(DOM),
            P(None, "wa"),
            P(None, "wa"),
            P(None, "wa"),
            P(None, "wa"),
            P("wa"),
        ),
        out_specs=(P(DOM, "wa"), P(DOM, "wa"), P(DOM, "wa"), P(DOM, "wa"), P(DOM, "wa"), P("wa")),
        check_vma=False,
    )
```

profile of v0, /device:TPU:1, one launch (start us, length us, event | category | flops | bytes accessed | tf_op | source)
XLA Modules:
  0.0 177.4 jit_solution(12169592979365900583)
XLA Ops:
  1.4 4.6 %collective-permute-start = (bf16[32,256]{1,0:T(8,128)(2,1)S(1)}, bf16[32,256]{1,0:T(8,128)(2,1)S(1)}, u32[]{:S(2)}, u32[]{:S(2)}) collective-permute-start(bf16[32,256]{1,0:T(8,128)(2,1)S(1)} %get-tuple-element.50), channel_id=1, source_target_pairs={{0,4},{4,8},{8,12},{12,16},{16,20},{20,24},{24,28},{28,32},{32,36}... | collective-permute-start | bytes 49160 | tf_op jit(solution)/shard_map/ppermute | solution.py:21
  6.0 6.1 %collective-permute-start.1 = (bf16[32,256]{1,0:T(8,128)(2,1)S(1)}, bf16[32,256]{1,0:T(8,128)(2,1)S(1)}, u32[]{:S(2)}, u32[]{:S(2)}) collective-permute-start(bf16[32,256]{1,0:T(8,128)(2,1)S(1)} %get-tuple-element.49), channel_id=1, source_target_pairs={{4,0},{8,4},{12,8},{16,12},{20,16},{24,20},{28,24},{32,28},{36,32}... | collective-permute-start | bytes 49160 | tf_op jit(solution)/shard_map/ppermute | solution.py:24
  12.1 1.3 fusion.24
  16.1 1.5 broadcast_in_dim.24
  17.5 1.6 reshape.135
  20.1 9.6 %gather_fusion = f32[3072,64]{1,0:T(8,128)S(1)} fusion(f32[320,64]{1,0:T(8,128)S(1)} %fusion.28, s32[3072]{0:T(1024)} %fusion.24), kind=kCustom, calls=%fused_computation.clone | custom fusion | bytes 1585152 | tf_op jit(solution)/shard_map/jit(_take)/gather | solution.py:121
  29.8 12.1 %gather_fusion.1 = f32[3072,64]{1,0:T(8,128)} fusion(f32[320,64]{1,0:T(8,128)S(1)} %fusion.30, s32[3072]{0:T(1024)} %fusion.24), kind=kCustom, calls=%fused_computation.1.clone | custom fusion | bytes 1585152 | tf_op jit(solution)/shard_map/jit(_take)/gather | solution.py:122
  41.8 5.1 %select_multiply_fusion = (f32[3072,64]{1,0:T(8,128)}, f32[3072,64]{1,0:T(8,128)}) fusion(f32[3072,64]{1,0:T(8,128)} %gather_fusion.1, pred[3072]{0:T(1024)(128)(4,1)S(1)} %compare_and_fusion, f32[3072]{0:T(1024)S(1)} %mul.75, f32[64]{0:T(128)S(1)} %copy-done.21, f32[3072]{0:T(1024)S(1)} %copy-done.15, f32[3072,64]{1,0:T(8,128)S(1)} %reshape.135, ...), kind=kLoop, calls=%fused_computation.14 | loop fusion | flops 1966080 | bytes 3960064 | tf_op jit(solution)/shard_map/mul | solution.py:126
  46.9 2.6 %reshape.137 = f32[256,12,64]{2,1,0:T(8,128)} reshape(f32[3072,64]{1,0:T(8,128)} %get-tuple-element.46) | data formatting | bytes 1572864 | tf_op jit(solution)/shard_map/reshape | solution.py:111
  49.6 2.2 %reduce_sum.82 = f32[256,64]{1,0:T(8,128)S(1)} reduce(f32[256,12,64]{2,1,0:T(8,128)} %reshape.137, f32[]{:T(128)} %constant.100.clone.1), dimensions={1}, to_apply=%region_1.3 | reduce | flops 180224 | bytes 851972 | tf_op jit(solution)/shard_map/reduce_sum | solution.py:111
  52.4 1.5 reshape.136
  53.9 2.1 %reduce_sum.81 = f32[256,64]{1,0:T(8,128)S(1)} reduce(f32[256,12,64]{2,1,0:T(8,128)} %reshape.136, f32[]{:T(128)} %constant.100.clone.1), dimensions={1}, to_apply=%region_0.0 | reduce | flops 180224 | bytes 851972 | tf_op jit(solution)/shard_map/reduce_sum | solution.py:111
  57.1 1.5 broadcast_in_dim.26
  58.6 1.6 reshape.138
  61.1 1.5 broadcast_in_dim.27
  62.6 2.5 %reshape.139 = f32[3072,64]{1,0:T(8,128)} reshape(f32[256,12,64]{2,1,0:T(8,128)} %broadcast_in_dim.27) | data formatting | bytes 1572864 | tf_op jit(solution)/shard_map/reshape | solution.py:106
  65.2 5.9 %multiply_reduce_fusion = (f32[64]{0:T(128)}, f32[3072,64]{1,0:T(8,128)}) fusion(f32[3072]{0:T(1024)S(1)} %copy-done.15, f32[3072]{0:T(1024)S(1)} %mul.75, f32[64]{0:T(128)S(1)} %copy-done.21, f32[3072,64]{1,0:T(8,128)S(1)} %reshape.135, f32[3072,64]{1,0:T(8,128)} %copy-done.1, f32[3072,64]{1,0:T(8,128)} %reshape.139, f32[3072,64]{1,0:T(8,128)S(1)} %reshape.138, ...), kind=kLoop, calls=%fused_computation.10 | loop fusion | flops 3145664 | bytes 4746752 | tf_op jit(solution)/shard_map/reduce_sum | solution.py:140
  71.0 17.9 %scatter_custom_fusion = f32[320,64]{1,0:T(8,128)} fusion(s32[3072]{0:T(1024)} %param.21, f32[3072,64]{1,0:T(8,128)} %get-tuple-element.44, f32[]{:T(128)} %constant.100.clone.1), kind=kCustom, calls=%fused_computation.26 | custom fusion | flops 196608 | bytes 82432 | tf_op jit(solution)/shard_map/scatter-add | solution.py:137
  88.9 2.7 %reshape.140 = f32[256,12,64]{2,1,0:T(8,128)} reshape(f32[3072,64]{1,0:T(8,128)} %get-tuple-element.44) | data formatting | bytes 1572864 | tf_op jit(solution)/shard_map/reshape | solution.py:111
  91.6 17.9 %scatter_custom_fusion.1 = f32[320,64]{1,0:T(8,128)} fusion(s32[3072]{0:T(1024)} %param.21, f32[3072,64]{1,0:T(8,128)S(1)} %copy-done.2, f32[3072,64]{1,0:T(8,128)S(1)} %reshape.138, f32[]{:T(128)} %constant.100.clone.1), kind=kCustom, calls=%fused_computation.11 | custom fusion | flops 393216 | bytes 1655296 | tf_op jit(solution)/shard_map/scatter-add | solution.py:138
  111.8 2.1 %reduce_sum.83 = bf16[256,64]{1,0:T(8,128)(2,1)S(1)} reduce(f32[256,12,64]{2,1,0:T(8,128)} %reshape.140, f32[]{:T(128)} %constant.100.clone.1), dimensions={1}, to_apply=%region_4.6 | reduce | flops 180224 | bytes 819204 | tf_op jit(solution)/shard_map/reduce_sum | solution.py:111
  115.7 9.4 %all_to_all.27 = f32[2,1,64]{2,1,0:T(1,128)S(1)} all-to-all(f32[2,1,64]{2,1,0:T(1,128)S(1)} %broadcast_in_dim.28), channel_id=1, replica_groups=mesh['dom_0'=8,'dom_1'=8,'dom_2'=2,'wa'=4] {'dom_2'}, dimensions={0} | all-to-all | bytes 1024 | tf_op jit(solution)/shard_map/all_to_all | solution.py:72
  125.1 4.0 %all-to-all-start = ((bf16[4,320,64]{1,2,0:T(8,128)(2,1)}), bf16[4,320,64]{1,2,0:T(8,128)(2,1)S(1)}, u32[]{:S(2)}, u32[]{:S(2)}) async-start(bf16[4,320,64]{1,2,0:T(8,128)(2,1)} %bitcast.2), calls=%async_computation | async-start | bytes 393216 | tf_op jit(solution)/shard_map/all_to_all | solution.py:37
  130.4 4.0 %all-to-all-done = bf16[4,320,64]{1,2,0:T(8,128)(2,1)S(1)} async-done(((bf16[4,320,64]{1,2,0:T(8,128)(2,1)}), bf16[4,320,64]{1,2,0:T(8,128)(2,1)S(1)}, u32[]{:S(2)}, u32[]{:S(2)}) %all-to-all-start) | async-done | bytes 163872 | tf_op jit(solution)/shard_map/all_to_all | solution.py:37
  134.3 5.2 %all-to-all-start.1 = ((f32[2,64,2,256]{3,2,1,0:T(2,128)}), f32[2,64,2,256]{3,2,1,0:T(2,128)S(1)}, u32[]{:S(2)}, u32[]{:S(2)}) async-start(f32[2,64,2,256]{3,2,1,0:T(2,128)} %copy.57), calls=%async_computation.1 | async-start | bytes 524288 | tf_op jit(solution)/shard_map/all_to_all | solution.py:49
  139.5 1.2 all-to-all-done.1
  141.3 7.9 %all-to-all-start.4 = ((f32[64,1,64]{2,1,0:T(1,128)}), f32[64,1,64]{2,1,0:T(1,128)S(1)}, u32[]{:S(2)}, u32[]{:S(2)}) async-start(f32[64,1,64]{2,1,0:T(1,128)} %broadcast_in_dim.29), calls=%async_computation.4 | async-start | bytes 65536 | tf_op jit(solution)/shard_map/all_to_all | solution.py:72
  149.3 2.5 %collective-permute-start.2 = (f32[32,64]{0,1:T(8,128)S(1)}, f32[32,64]{0,1:T(8,128)S(1)}, u32[]{:S(2)}, u32[]{:S(2)}) collective-permute-start(f32[32,64]{0,1:T(8,128)S(1)} %get-tuple-element.52), channel_id=1, source_target_pairs={{4,0},{8,4},{12,8},{16,12},{20,16},{24,20},{28,24},{32,28},{36,32}... | collective-permute-start | bytes 24584 | tf_op jit(solution)/shard_map/ppermute | solution.py:44
  152.7 7.3 %all-to-all-done.4 = f32[64,1,64]{2,1,0:T(1,128)S(1)} async-done(((f32[64,1,64]{2,1,0:T(1,128)}), f32[64,1,64]{2,1,0:T(1,128)S(1)}, u32[]{:S(2)}, u32[]{:S(2)}) %all-to-all-start.4) | async-done | bytes 16416 | tf_op jit(solution)/shard_map/all_to_all | solution.py:72
  160.0 5.1 %all-to-all-start.2 = ((f32[64,2,256]{2,1,0:T(2,128)}), f32[64,2,256]{2,1,0:T(2,128)S(1)}, u32[]{:S(2)}, u32[]{:S(2)}) async-start(f32[64,2,256]{2,1,0:T(2,128)} %reduce_sum.85), calls=%async_computation.2 | async-start | bytes 262144 | tf_op jit(solution)/shard_map/all_to_all | solution.py:57
  165.7 4.3 %collective-permute-start.3 = (f32[32,64]{0,1:T(8,128)S(1)}, f32[32,64]{0,1:T(8,128)S(1)}, u32[]{:S(2)}, u32[]{:S(2)}) collective-permute-start(f32[32,64]{0,1:T(8,128)S(1)} %get-tuple-element.51), channel_id=1, source_target_pairs={{508,0},{0,4},{4,8},{8,12},{12,16},{16,20},{20,24},{24,28},{28,32}... | collective-permute-start | bytes 24584 | tf_op jit(solution)/shard_map/ppermute | solution.py:44
  172.1 4.6 %all-to-all-done.2 = f32[64,2,256]{2,1,0:T(2,128)S(1)} async-done(((f32[64,2,256]{2,1,0:T(2,128)}), f32[64,2,256]{2,1,0:T(2,128)S(1)}, u32[]{:S(2)}, u32[]{:S(2)}) %all-to-all-start.2) | async-done | bytes 131104 | tf_op jit(solution)/shard_map/all_to_all | solution.py:57
  (95 shorter events, 16.5 us)
Async XLA Ops:
  0.6 55.4 %copy-start = (bf16[256,64]{0,1:T(8,128)(2,1)S(1)}, bf16[256,64]{0,1:T(8,128)(2,1)}, u32[]{:S(2)}) copy-start(bf16[256,64]{0,1:T(8,128)(2,1)} %param.26) | copy-start | bytes 98308
  1.4 17.8 %collective-permute-start = (bf16[32,256]{1,0:T(8,128)(2,1)S(1)}, bf16[32,256]{1,0:T(8,128)(2,1)S(1)}, u32[]{:S(2)}, u32[]{:S(2)}) collective-permute-start(bf16[32,256]{1,0:T(8,128)(2,1)S(1)} %get-tuple-element.50), channel_id=1, source_target_pairs={{0,4},{4,8},{8,12},{12,16},{16,20},{20,24},{24,28},{28,32},{32,36}... | collective-permute-start | bytes 49160 | tf_op jit(solution)/shard_map/ppermute | solution.py:21
  6.0 13.3 %collective-permute-start.1 = (bf16[32,256]{1,0:T(8,128)(2,1)S(1)}, bf16[32,256]{1,0:T(8,128)(2,1)S(1)}, u32[]{:S(2)}, u32[]{:S(2)}) collective-permute-start(bf16[32,256]{1,0:T(8,128)(2,1)S(1)} %get-tuple-element.49), channel_id=1, source_target_pairs={{4,0},{8,4},{12,8},{16,12},{20,16},{24,20},{28,24},{32,28},{36,32}... | collective-permute-start | bytes 49160 | tf_op jit(solution)/shard_map/ppermute | solution.py:24
  15.8 3.4 %copy-start.18 = (f32[256]{0:T(256)}, f32[256]{0:T(256)S(1)}, u32[]{:S(2)}) copy-start(f32[256]{0:T(256)S(1)} %or_convert_fusion) | copy-start | bytes 3076
  17.5 1.7 copy-start.6
  17.5 1.7 copy-start.9
  17.5 2.4 %copy-start.12 = (bf16[256,64]{0,1:T(8,128)(2,1)S(1)}, bf16[256,64]{0,1:T(8,128)(2,1)}, u32[]{:S(2)}) copy-start(bf16[256,64]{0,1:T(8,128)(2,1)} %param.25) | copy-start | bytes 98308
  19.3 0.7 copy-start.4
  29.7 12.1 %copy-start.1 = (f32[3072,64]{1,0:T(8,128)}, f32[3072,64]{1,0:T(8,128)S(1)}, u32[]{:S(2)}) copy-start(f32[3072,64]{1,0:T(8,128)S(1)} %gather_fusion) | copy-start | bytes 2359300
  29.7 12.1 %copy-start.15 = (f32[3072]{0:T(1024)S(1)}, f32[3072]{0:T(1024)}, u32[]{:S(2)}) copy-start(f32[3072]{0:T(1024)} %param.22) | copy-start | bytes 36868
  29.8 12.1 %copy-start.21 = (f32[64]{0:T(128)S(1)}, f32[64]{0:T(128)}, u32[]{:S(2)}) copy-start(f32[64]{0:T(128)} %param.27) | copy-start | bytes 772
  49.6 2.9 %copy-start.3 = (f32[3072,64]{1,0:T(8,128)S(1)}, f32[3072,64]{1,0:T(8,128)}, u32[]{:S(2)}) copy-start(f32[3072,64]{1,0:T(8,128)} %get-tuple-element.45) | copy-start | bytes 2359300
  53.9 2.2 %copy-start.7 = (bf16[256,256]{1,0:T(8,128)(2,1)S(1)}, bf16[256,256]{1,0:T(8,128)(2,1)}, u32[]{:S(2)}) copy-start(bf16[256,256]{1,0:T(8,128)(2,1)} %param.18) | copy-start | bytes 393220
  53.9 2.2 %copy-start.14 = (f32[256,64]{0,1:T(8,128)S(1)}, f32[256,64]{0,1:T(8,128)}, u32[]{:S(2)}) copy-start(f32[256,64]{0,1:T(8,128)} %copy.51) | copy-start | bytes 196612
  53.9 2.2 %copy-start.16 = (bf16[256,64]{0,1:T(8,128)(2,1)S(1)}, bf16[256,64]{0,1:T(8,128)(2,1)}, u32[]{:S(2)}) copy-start(bf16[256,64]{0,1:T(8,128)(2,1)} %param.19) | copy-start | bytes 98308
  53.9 2.2 %copy-start.19 = (f32[256]{0:T(256)S(1)}, f32[256]{0:T(256)}, u32[]{:S(2)}) copy-start(f32[256]{0:T(256)} %copy-done.18) | copy-start | bytes 3076
  88.9 2.7 %copy-start.2 = (f32[3072,64]{1,0:T(8,128)S(1)}, f32[3072,64]{1,0:T(8,128)}, u32[]{:S(2)}) copy-start(f32[3072,64]{1,0:T(8,128)} %get-tuple-element.46) | copy-start | bytes 2359300
  91.6 17.9 %copy-start.5 = (bf16[320,256]{1,0:T(8,128)(2,1)S(1)}, bf16[320,256]{1,0:T(8,128)(2,1)}, u32[]{:S(2)}) copy-start(bf16[320,256]{1,0:T(8,128)(2,1)} %copy-done.4) | copy-start | bytes 491524
  110.6 3.4 %copy-start.10 = (bf16[256,64]{0,1:T(8,128)(2,1)S(1)}, bf16[256,64]{0,1:T(8,128)(2,1)}, u32[]{:S(2)}) copy-start(bf16[256,64]{0,1:T(8,128)(2,1)} %param.24) | copy-start | bytes 98308
  110.6 3.6 %copy-start.8 = (f32[320,64]{1,0:T(8,128)S(1)}, f32[320,64]{1,0:T(8,128)}, u32[]{:S(2)}) copy-start(f32[320,64]{1,0:T(8,128)} %scatter_custom_fusion.1) | copy-start | bytes 245764
  111.8 2.7 %copy-start.13 = (bf16[256,64]{0,1:T(8,128)(2,1)S(1)}, bf16[256,64]{0,1:T(8,128)(2,1)}, u32[]{:S(2)}) copy-start(bf16[256,64]{0,1:T(8,128)(2,1)} %param.25) | copy-start | bytes 98308
  111.8 2.8 %copy-start.11 = (bf16[256,64]{0,1:T(8,128)(2,1)S(1)}, bf16[256,64]{0,1:T(8,128)(2,1)}, u32[]{:S(2)}) copy-start(bf16[256,64]{0,1:T(8,128)(2,1)} %get-tuple-element.57) | copy-start | bytes 98308
  114.0 1.7 copy-start.22
  125.1 9.2 %all-to-all-start = ((bf16[4,320,64]{1,2,0:T(8,128)(2,1)}), bf16[4,320,64]{1,2,0:T(8,128)(2,1)S(1)}, u32[]{:S(2)}, u32[]{:S(2)}) async-start(bf16[4,320,64]{1,2,0:T(8,128)(2,1)} %bitcast.2), calls=%async_computation | async-start | bytes 393216 | tf_op jit(solution)/shard_map/all_to_all | solution.py:37
  129.4 42.0 %copy-start.17 = (bf16[256,64]{0,1:T(8,128)(2,1)S(1)}, bf16[256,64]{0,1:T(8,128)(2,1)}, u32[]{:S(2)}) copy-start(bf16[256,64]{0,1:T(8,128)(2,1)} %param.19) | copy-start | bytes 98308
  129.4 42.0 %copy-start.20 = (f32[256]{0:T(256)S(1)}, f32[256]{0:T(256)}, u32[]{:S(2)}) copy-start(f32[256]{0:T(256)} %copy-done.18) | copy-start | bytes 3076
  134.3 6.4 %all-to-all-start.1 = ((f32[2,64,2,256]{3,2,1,0:T(2,128)}), f32[2,64,2,256]{3,2,1,0:T(2,128)S(1)}, u32[]{:S(2)}, u32[]{:S(2)}) async-start(f32[2,64,2,256]{3,2,1,0:T(2,128)} %copy.57), calls=%async_computation.1 | async-start | bytes 524288 | tf_op jit(solution)/shard_map/all_to_all | solution.py:49
  141.3 18.7 %all-to-all-start.4 = ((f32[64,1,64]{2,1,0:T(1,128)}), f32[64,1,64]{2,1,0:T(1,128)S(1)}, u32[]{:S(2)}, u32[]{:S(2)}) async-start(f32[64,1,64]{2,1,0:T(1,128)} %broadcast_in_dim.29), calls=%async_computation.4 | async-start | bytes 65536 | tf_op jit(solution)/shard_map/all_to_all | solution.py:72
  149.3 20.7 %collective-permute-start.2 = (f32[32,64]{0,1:T(8,128)S(1)}, f32[32,64]{0,1:T(8,128)S(1)}, u32[]{:S(2)}, u32[]{:S(2)}) collective-permute-start(f32[32,64]{0,1:T(8,128)S(1)} %get-tuple-element.52), channel_id=1, source_target_pairs={{4,0},{8,4},{12,8},{16,12},{20,16},{24,20},{28,24},{32,28},{36,32}... | collective-permute-start | bytes 24584 | tf_op jit(solution)/shard_map/ppermute | solution.py:44
  160.0 16.6 %all-to-all-start.2 = ((f32[64,2,256]{2,1,0:T(2,128)}), f32[64,2,256]{2,1,0:T(2,128)S(1)}, u32[]{:S(2)}, u32[]{:S(2)}) async-start(f32[64,2,256]{2,1,0:T(2,128)} %reduce_sum.85), calls=%async_computation.2 | async-start | bytes 262144 | tf_op jit(solution)/shard_map/all_to_all | solution.py:57
  165.7 5.3 %collective-permute-start.3 = (f32[32,64]{0,1:T(8,128)S(1)}, f32[32,64]{0,1:T(8,128)S(1)}, u32[]{:S(2)}, u32[]{:S(2)}) collective-permute-start(f32[32,64]{0,1:T(8,128)S(1)} %get-tuple-element.51), channel_id=1, source_target_pairs={{508,0},{0,4},{4,8},{8,12},{12,16},{16,20},{20,24},{24,28},{28,32}... | collective-permute-start | bytes 24584 | tf_op jit(solution)/shard_map/ppermute | solution.py:44
where the time goes:
time: 179 us; the launch traced here: 177 us
  other arithmetic  57.2 us (32%)
  local copies, waits for them, and re-layouts  46.2 us (26%)
  starting transfers between devices  39.6 us (22%)
  waiting for transfers between devices  17.5 us (10%)
  blocking collectives  9.37 us (5%)
  matrix products  5.6 us (3%)
  between operations  1.8 us (1%)
    scatter-add x1, other arithmetic, per_device(): dmsg_rows = jax.ops.segment_sum(dmessage, source, num_segments=ext_rows)  17.9 us
    scatter-add x1, other arithmetic, per_device(): dsource = jax.ops.segment_sum(dpre, source, num_segments=ext_rows)  17.9 us
    gather x1, local copies, waits for them, and re-layouts, per_device(): picked_message = jnp.take(proj_message, source, axis=0)  12.1 us
    gather x1, local copies, waits for them, and re-layouts, per_device(): picked_source = jnp.take(proj_source, source, axis=0)  9.58 us
    all_to_all x1, blocking collectives, copy_for_each(): return lax.all_to_all(copies, axis, split_axis=0, concat_axis=0, tiled=True)  9.37 us
    all_to_all x1, starting transfers between devices, copy_for_each(): return lax.all_to_all(copies, axis, split_axis=0, concat_axis=0, tiled=True)  7.87 us
    all_to_all x1, waiting for transfers between devices, copy_for_each(): return lax.all_to_all(copies, axis, split_axis=0, concat_axis=0, tiled=True)  7.34 us
    ppermute x2, starting transfers between devices, shifted(): return lax.ppermute(block, axis, route)  6.84 us
  transfers between devices with their start and end apart: 8, of which 5 were waited for; matrix products, arithmetic and copies ran while one was open for 6% of the time, Pallas kernels for 0%

commit v1 on v0

v1 whole, which is shorter than its diff:
```python
import jax
import jax.numpy as jnp
from jax import lax
from jax.experimental import pallas as pl
from jax.experimental.pallas import tpu as pltpu
from jax.sharding import Mesh
from jax.sharding import PartitionSpec as P

ARITY = 12
GHOST = 32
CAP = 256
EXT = CAP + 2 * GHOST
DOM = ("dom_0", "dom_1", "dom_2")
NDOM = 128
EPS = 1e-06
F32 = jnp.float32
BF16 = jnp.bfloat16


def dot(a, b, ca=1, cb=0):
    return lax.dot_general(a, b, (((ca,), (cb,)), ((), ())), preferred_element_type=F32)


def sigmoid(v):
    return 1.0 / (1.0 + jnp.exp(-v))


def angle_kernel(
    meta,
    h_ref,
    ga_ref,
    gb_ref,
    cot_ref,
    src_ref,
    cos_ref,
    ws_ref,
    wm_ref,
    wt_ref,
    wf_ref,
    gate_w_ref,
    whole_ref,
    grads_ref,
    gate_ref,
    hot_ref,
    sig_ref,
    msg_ref,
):
    count = meta[0]
    odd = meta[1]
    h = h_ref[...]
    gh = jnp.concatenate([ga_ref[...], gb_ref[...]], axis=0)
    h_t = h.T
    gh_t = gh.T
    w_t = jnp.concatenate([ws_ref[...], wm_ref[...], wt_ref[...], wf_ref[...]], axis=0)
    own = dot(w_t, h_t)
    far = dot(w_t[:128], gh_t)
    own_hi = own[:128].astype(BF16)
    own_lo = (own[:128] - own_hi.astype(F32)).astype(BF16)
    far_hi = far.astype(BF16)
    far_lo = (far - far_hi.astype(F32)).astype(BF16)
    table_own = jnp.concatenate([own_hi, own_lo], axis=0)
    table_far = jnp.concatenate([far_hi, far_lo], axis=0)
    q2 = own[128:192]
    base = own[192:256]

    bond = lax.broadcasted_iota(jnp.int32, (1, CAP), 1)
    live = ((bond < count - GHOST) | (bond >= CAP - GHOST)).astype(F32)
    src = src_ref[...]
    low_base = jnp.where(odd == 1, CAP, CAP + GHOST)
    high_base = jnp.where(odd == 1, CAP + GHOST, CAP)
    row = jnp.where(
        src < GHOST,
        src + low_base,
        jnp.where(src >= CAP + GHOST, src - (CAP + GHOST) + high_base, src - GHOST),
    )
    row_id = lax.broadcasted_iota(jnp.int32, (EXT, CAP), 0)
    gate_w = gate_w_ref[...]

    num = jnp.zeros((64, CAP), F32)
    den = jnp.zeros((64, CAP), F32)
    for k in range(ARITY):
        hot = (row_id == row[k : k + 1]).astype(F32).astype(BF16)
        hot_ref[k] = hot
        picked = dot(table_own, hot[:CAP]) + dot(table_far, hot[CAP:])
        p1 = picked[0:64] + picked[128:192]
        p4 = picked[64:128] + picked[192:256]
        sig = sigmoid(p1 + q2 + gate_w * cos_ref[k : k + 1])
        gate = sig * live
        num += gate * p4
        den += gate
        sig_ref[k] = sig
        msg_ref[k] = p4
    den = den + EPS
    agg = num / den
    z = base + agg
    s = sigmoid(z)
    dz = cot_ref[...].astype(F32) * live * (s * (1.0 + z * (1.0 - s)))
    dnum = dz / den
    dden = -(dnum * agg)

    dq2 = jnp.zeros((64, CAP), F32)
    dgw = jnp.zeros((64, CAP), F32)
    acc = jnp.zeros((EXT, 128), F32)
    for k in range(ARITY):
        sig = sig_ref[k]
        gate = sig * live
        dgate = dnum * msg_ref[k] + dden
        dmsg = gate * dnum
        dpre = dgate * gate * (1.0 - sig)
        dq2 += dpre
        dgw += dpre * cos_ref[k : k + 1]
        both = jnp.concatenate([dpre, dmsg], axis=0).astype(BF16)
        acc += dot(hot_ref[k], both, 1, 1)
    edge = acc.astype(BF16)
    bonds = jnp.concatenate([dq2, dz], axis=0).astype(BF16).T
    full = jnp.concatenate([edge[:CAP], bonds], axis=1)
    edge_far = edge[CAP:]
    whole_ref[:, :CAP] = dot(full, w_t).astype(BF16).T
    whole_ref[:, CAP:] = dot(edge_far, w_t[:128]).astype(BF16).T
    grads = dot(h_t, full)
    extra = dot(gh_t, edge_far)
    grads_ref[:, :128] = (grads[:, :128] + extra).astype(BF16)
    grads_ref[:, 128:] = grads[:, 128:].astype(BF16)
    gate_ref[...] = jnp.sum(dgw, axis=1, keepdims=True)


def angle_stage(meta, h, ga, gb, cot_t, src, cos, ws, wm, wt, wf, gate_w):
    vmem = pl.BlockSpec(memory_space=pltpu.VMEM)
    return pl.pallas_call(
        angle_kernel,
        out_shape=(
            jax.ShapeDtypeStruct((256, EXT), BF16),
            jax.ShapeDtypeStruct((256, 256), BF16),
            jax.ShapeDtypeStruct((64, 1), F32),
        ),
        in_specs=[pl.BlockSpec(memory_space=pltpu.SMEM)] + [vmem] * 11,
        out_specs=(vmem, vmem, vmem),
        scratch_shapes=[
            pltpu.VMEM((ARITY, EXT, CAP), BF16),
            pltpu.VMEM((ARITY, 64, CAP), F32),
            pltpu.VMEM((ARITY, 64, CAP), F32),
        ],
        name="angle_stage",
    )(meta, h, ga, gb, cot_t, src, cos, ws, wm, wt, wf, gate_w)


def swap_core(x):
    return lax.ppermute(x, DOM, [(i, i ^ 1) for i in range(NDOM)])


def swap_chip(x):
    return lax.ppermute(x, DOM, [(i, (i + 1) % NDOM if i % 2 else (i - 1) % NDOM) for i in range(NDOM)])


def per_device(
    bond_feats,
    cotangent,
    bond_count,
    source,
    cosine,
    w_source,
    w_target,
    w_message,
    w_self,
    gate_angle,
):
    odd = lax.axis_index("dom_2")
    first, last = bond_feats[:GHOST], bond_feats[CAP - GHOST :]
    is_odd = odd == 1
    ghost_a = swap_core(jnp.where(is_odd, first, last))
    ghost_b = swap_chip(jnp.where(is_odd, last, first))
    meta = jnp.stack([bond_count[0], odd.astype(jnp.int32)])
    src = source.reshape(CAP, ARITY).T
    cos = cosine.reshape(CAP, ARITY).T
    cot_t = cotangent.T
    whole, grads, gate_term = angle_stage(
        meta,
        bond_feats,
        ghost_a,
        ghost_b,
        cot_t,
        src,
        cos,
        w_source.T,
        w_message.T,
        w_target.T,
        w_self.T,
        gate_angle[:, None],
    )
    tiles = lax.all_to_all(whole.reshape(4, 64, EXT), "wa", 0, 0, tiled=True)
    summed = tiles.astype(F32).sum(axis=0)
    back_a = swap_core(summed[:, CAP : CAP + GHOST])
    back_b = swap_chip(summed[:, CAP + GHOST :])
    gate_row = gate_term[:, 0]
    gate_hi = gate_row.astype(BF16)
    gate_lo = (gate_row - gate_hi.astype(F32)).astype(BF16)
    gate_slot = jnp.concatenate([gate_hi, gate_lo, jnp.zeros((128,), BF16)])
    slots = jnp.concatenate(
        [grads.reshape(NDOM, 256 // NDOM, 256), jnp.broadcast_to(gate_slot[None, None], (NDOM, 1, 256))], axis=1
    )
    arrived = lax.all_to_all(slots, DOM, 0, 0, tiled=True).astype(F32).sum(axis=0)
    grad_gate = arrived[-1, :64] + arrived[-1, 64:128]

    bond = jnp.arange(CAP, dtype=jnp.int32)
    count = bond_count[0]
    live = ((bond < count - GHOST) | (bond >= CAP - GHOST)).astype(F32)
    total = summed[:, :CAP] + cot_t.astype(F32) * live[None, :]
    to_first = jnp.where(is_odd, back_a, back_b)
    to_last = jnp.where(is_odd, back_b, back_a)
    added = jnp.concatenate([to_first, jnp.zeros((64, CAP - 2 * GHOST), F32), to_last], axis=1)
    bond_grad = (total + added).astype(BF16).T
    return (
        bond_grad,
        arrived[:-1, 0:64],
        arrived[:-1, 128:192],
        arrived[:-1, 64:128],
        arrived[:-1, 192:256],
        grad_gate,
    )


def solution(mesh):
    finer = Mesh(mesh.devices.reshape(8, 8, 2, mesh.shape["wa"]), ("dom_0", "dom_1", "dom_2", "wa"))
    return jax.shard_map(
        per_device,
        mesh=finer,
        in_specs=(
            P(DOM, None),
            P(DOM, "wa"),
            P(DOM),
            P(DOM),
            P(DOM),
            P(None, "wa"),
            P(None, "wa"),
            P(None, "wa"),
            P(None, "wa"),
            P("wa"),
        ),
        out_specs=(P(DOM, "wa"), P(DOM, "wa"), P(DOM, "wa"), P(DOM, "wa"), P(DOM, "wa"), P("wa")),
        check_vma=False,
    )
```

time: 179 us -> 69.6 us (0.39)
  other arithmetic: 57.2 us -> 3.98 us
  local copies, waits for them, and re-layouts: 46.2 us -> 5.26 us
  blocking collectives: 9.37 us -> 0 us
  matrix products: 5.6 us -> 0 us
  starting transfers between devices: 39.6 us -> 34.8 us
  Pallas kernels: 0 us -> 4.49 us
    scatter-add x2 -> x0, other arithmetic: 35.7 us -> none  [the longest x1 17.9 us: per_device(): dmsg_rows = jax.ops.segment_sum(dmessage, source, num_segments=ext_rows)]
    gather x2 -> x0, local copies, waits for them, and re-layouts: 21.7 us -> none  [the longest x1 12.1 us: per_device(): picked_message = jnp.take(proj_message, source, axis=0)]
    reduce_sum x9 -> x2, other arithmetic: 13.7 us -> 0.2 us  [the longest x1 0.17 us: per_device(): lax.all_to_all(slots, DOM, 0, 0, tiled=True).astype(F32).sum(axis=0)]
    reshape x6 -> x5, local copies, waits for them, and re-layouts: 12.6 us -> 1.69 us  [the longest x2 0.82 us: per_device(): src = source.reshape(CAP, ARITY).T]
    all_to_all x1 -> x0, blocking collectives: 9.37 us -> none  [copy_for_each(): return lax.all_to_all(copies, axis, split_axis=0, concat_axis=0, tiled=True)]
    all_to_all x4 -> x2, starting transfers between devices: 22.1 us -> 12.8 us  [the longest x1 8.68 us: per_device(): lax.all_to_all(slots, DOM, 0, 0, tiled=True).astype(F32).sum(axis=0)]
    dot_general x12 -> x0, matrix products: 5.6 us -> none  [the longest x1 1.13 us: per_device(): jnp.dot(round_source, w_source.T, preferred_element_type=jnp.float32)]
    mul x1 -> x0, other arithmetic: 5.1 us -> none  [per_device(): numer = per_bond(gated * picked_message)]
  transfers between devices with their start and end apart: 8 -> 6, of which waited for: 5 -> 2; matrix products, arithmetic and copies ran while one was open for 6% -> 7% of each run, Pallas kernels for 0% -> 0%
where the time goes in v1:
time: 69.6 us; the launch traced here: 68.9 us
  starting transfers between devices  34.8 us (50%)
  waiting for transfers between devices  19 us (27%)
  local copies, waits for them, and re-layouts  5.26 us (8%)
  Pallas kernels  4.49 us (6%)
  other arithmetic  3.98 us (6%)
  between operations  1.45 us (2%)
    ppermute x2, starting transfers between devices, swap_core(): return lax.ppermute(x, DOM, [(i, i ^ 1) for i in range(NDOM)])  15.5 us
    all_to_all x1, waiting for transfers between devices, per_device(): lax.all_to_all(slots, DOM, 0, 0, tiled=True).astype(F32).sum(axis=0)  13.8 us
    all_to_all x1, starting transfers between devices, per_device(): lax.all_to_all(slots, DOM, 0, 0, tiled=True).astype(F32).sum(axis=0)  8.68 us
    ppermute x2, starting transfers between devices, swap_chip(): lax.ppermute(x, DOM, [(i, (i + 1) % NDOM if i % 2 else (i - 1) % NDOM) fo...  6.49 us
    all_to_all x1, waiting for transfers between devices, per_device(): tiles = lax.all_to_all(whole.reshape(4, 64, EXT), 'wa', 0, 0, tiled=True)  5.19 us
    pallas_call x1, Pallas kernels, angle_stage(): pl.pallas_call(angle_kernel, out_shape=(jax.ShapeDtypeStruct((256, EXT),...  4.49 us
    all_to_all x1, starting transfers between devices, per_device(): tiles = lax.all_to_all(whole.reshape(4, 64, EXT), 'wa', 0, 0, tiled=True)  4.15 us
    unnamed x16, local copies, waits for them, and re-layouts  2 us
  transfers between devices with their start and end apart: 6, of which 2 were waited for; matrix products, arithmetic and copies ran while one was open for 7% of the time, Pallas kernels for 0%

profile of v1, /device:TPU:1, one launch (start us, length us, event | category | flops | bytes accessed | tf_op | source)
XLA Modules:
  0.0 68.9 jit_solution(2802188006737610899)
XLA Ops:
  0.6 0.7 %broadcast_select_fusion.2 = (bf16[32,256]{1,0:T(8,128)(2,1)S(1)}, bf16[32,256]{1,0:T(8,128)(2,1)S(1)}) fusion(pred[]{:T(512)S(6)} %eq.3, bf16[256,256]{1,0:T(8,128)(2,1)} %h_ref.1), kind=kLoop, calls=%fused_computation.9 | loop fusion | flops 16384 | bytes 65537 | tf_op jit(solution)/shard_map/jit(_where)/select_n | solution.py:171
  1.4 4.6 %collective-permute-start.1 = (bf16[32,256]{1,0:T(8,128)(2,1)S(1)}, bf16[32,256]{1,0:T(8,128)(2,1)S(1)}, u32[]{:S(2)}, u32[]{:S(2)}) collective-permute-start(bf16[32,256]{1,0:T(8,128)(2,1)S(1)} %get-tuple-element.12), channel_id=1, source_target_pairs={{0,508},{4,8},{8,4},{12,16},{16,12},{20,24},{24,20},{28,32},{32,28... | collective-permute-start | bytes 49160 | tf_op jit(solution)/shard_map/ppermute | solution.py:152
  6.0 12.1 %collective-permute-start = (bf16[32,256]{1,0:T(8,128)(2,1)S(1)}, bf16[32,256]{1,0:T(8,128)(2,1)S(1)}, u32[]{:S(2)}, u32[]{:S(2)}) collective-permute-start(bf16[32,256]{1,0:T(8,128)(2,1)S(1)} %get-tuple-element.13), channel_id=1, source_target_pairs={{0,4},{4,0},{8,12},{12,8},{16,20},{20,16},{24,28},{28,24},{32,36},... | collective-permute-start | bytes 49160 | tf_op jit(solution)/shard_map/ppermute | solution.py:148
  18.7 0.6 pad_add_fusion.meta
  19.3 0.7 copy-done.7
  20.0 0.7 %copy.19.gate_w_ref = f32[64,1]{1,0:T(8,128)} copy(f32[64,1]{0,1:T(1,128)S(1)} %bitcast.24) | data formatting | bytes 512 | tf_op jit(solution)/shard_map/broadcast_in_dim | solution.py:188
  20.7 0.1 reshape.38
  20.8 0.0 copy-start.6
  20.9 0.7 copy.17
  21.5 0.0 copy-done.6
  21.6 0.1 reshape.39
  21.7 0.7 copy.18
  22.4 0.1 pad.6.clone
  22.5 0.6 copy-done.3
  23.1 4.5 %angle_stage.1 = (bf16[256,320]{1,0:T(8,128)(2,1)}, bf16[256,256]{1,0:T(8,128)(2,1)}, f32[64,1]{1,0:T(8,128)}) custom-call(s32[2]{0:T(128)} %pad_add_fusion.meta, bf16[256,256]{1,0:T(8,128)(2,1)} %h_ref.1, bf16[32,256]{1,0:T(8,128)(2,1)} %copy-done.4, bf16[32,256]{1,0:T(8,128)(2,1)} %copy-done.3, bf16[64,256]{1,0:T(8,128)(2,1)} %bitcast.17, ...), custom_call_target="tpu_custom_call" | custom-call | tf_op jit(solution)/shard_map/angle_stage/pallas_call | solution.py:129
  27.6 4.1 %all-to-all-start = ((bf16[4,64,320]{2,1,0:T(8,128)(2,1)}), bf16[4,64,320]{2,1,0:T(8,128)(2,1)S(1)}, u32[]{:S(2)}, u32[]{:S(2)}) async-start(bf16[4,64,320]{2,1,0:T(8,128)(2,1)} %bitcast.16), calls=%async_computation | async-start | bytes 393216 | tf_op jit(solution)/shard_map/all_to_all | solution.py:190
  31.7 0.1 reduce
  31.8 0.1 reshape.41
  31.9 0.1 pad_maximum_fusion.1
  32.0 5.2 %all-to-all-done = bf16[4,64,320]{2,1,0:T(8,128)(2,1)S(1)} async-done(((bf16[4,64,320]{2,1,0:T(8,128)(2,1)}), bf16[4,64,320]{2,1,0:T(8,128)(2,1)S(1)}, u32[]{:S(2)}, u32[]{:S(2)}) %all-to-all-start) | async-done | bytes 163872 | tf_op jit(solution)/shard_map/all_to_all | solution.py:190
  37.2 0.1 fusion.4
  37.3 3.4 %collective-permute-start.2 = (f32[64,32]{1,0:T(8,128)S(1)}, f32[64,32]{1,0:T(8,128)S(1)}, u32[]{:S(2)}, u32[]{:S(2)}) collective-permute-start(f32[64,32]{1,0:T(8,128)S(1)} %get-tuple-element.14), channel_id=1, source_target_pairs={{0,4},{4,0},{8,12},{12,8},{16,20},{20,16},{24,28},{28,24},{32,36},... | collective-permute-start | bytes 24584 | tf_op jit(solution)/shard_map/ppermute | solution.py:148
  40.6 1.9 %collective-permute-start.3 = (f32[64,32]{1,0:T(8,128)S(1)}, f32[64,32]{1,0:T(8,128)S(1)}, u32[]{:S(2)}, u32[]{:S(2)}) collective-permute-start(f32[64,32]{1,0:T(8,128)S(1)} %get-tuple-element.15), channel_id=1, source_target_pairs={{0,508},{4,8},{8,4},{12,16},{16,12},{20,24},{24,20},{28,32},{32,28... | collective-permute-start | bytes 24584 | tf_op jit(solution)/shard_map/ppermute | solution.py:152
  42.6 0.1 broadcast_in_dim.19
  42.7 1.0 %pad_maximum_fusion = bf16[128,3,256]{2,1,0:T(4,128)(2,1)} fusion(bf16[128,1,256]{2,1,0:T(2,128)(2,1)S(1)} %broadcast_in_dim.19, bf16[128,2,256]{2,1,0:T(2,128)(2,1)S(1)} %reshape.41), kind=kLoop, calls=%fused_computation.2 | loop fusion | flops 393216 | bytes 393216 | tf_op jit(solution)/shard_map/concatenate | solution.py:198
  43.6 8.7 %all-to-all-start.1 = ((bf16[128,3,256]{2,1,0:T(4,128)(2,1)}), bf16[128,3,256]{2,1,0:T(4,128)(2,1)S(1)}, u32[]{:S(2)}, u32[]{:S(2)}) async-start(bf16[128,3,256]{2,1,0:T(4,128)(2,1)} %pad_maximum_fusion), calls=%async_computation.1 | async-start | bytes 524288 | tf_op jit(solution)/shard_map/all_to_all | solution.py:201
  52.4 0.7 %copy-done = bf16[256,64]{0,1:T(8,128)(2,1)S(1)} copy-done((bf16[256,64]{0,1:T(8,128)(2,1)S(1)}, bf16[256,64]{0,1:T(8,128)(2,1)}, u32[]{:S(2)}) %copy-start) | copy-done | bytes 32792
  53.1 0.7 %fusion.2 = bf16[256,64]{0,1:T(8,128)(2,1)} fusion(f32[64,32]{1,0:T(8,128)S(1)} %get-tuple-element.17, f32[64,32]{1,0:T(8,128)S(1)} %get-tuple-element.16, f32[64,320]{1,0:T(8,128)S(1)} %convert_reduce_fusion.1, f32[256]{0:T(256)S(1)} %pad.6.clone, f32[256]{0:T(256)S(1)} %or_convert_fusion, bf16[256,64]{0,1:T(8,128)(2,1)S(1)} %copy-done), kind=kLoop, calls=%fused_computation.6 | loop fusion | flops 114688 | bytes 149504 | tf_op jit(solution)/shard_map/transpose | solution.py:211
  53.8 13.8 %all-to-all-done.1 = bf16[128,3,256]{2,1,0:T(4,128)(2,1)S(1)} async-done(((bf16[128,3,256]{2,1,0:T(4,128)(2,1)}), bf16[128,3,256]{2,1,0:T(4,128)(2,1)S(1)}, u32[]{:S(2)}, u32[]{:S(2)}) %all-to-all-start.1) | async-done | bytes 196640 | tf_op jit(solution)/shard_map/all_to_all | solution.py:201
  67.6 0.2 convert_reduce_fusion
  67.7 0.6 fusion.3
  68.3 0.6 fusion.5
  (21 shorter events, 0.1 us)
Async XLA Ops:
  1.4 21.1 %collective-permute-start.1 = (bf16[32,256]{1,0:T(8,128)(2,1)S(1)}, bf16[32,256]{1,0:T(8,128)(2,1)S(1)}, u32[]{:S(2)}, u32[]{:S(2)}) collective-permute-start(bf16[32,256]{1,0:T(8,128)(2,1)S(1)} %get-tuple-element.12), channel_id=1, source_target_pairs={{0,508},{4,8},{8,4},{12,16},{16,12},{20,24},{24,20},{28,32},{32,28... | collective-permute-start | bytes 49160 | tf_op jit(solution)/shard_map/ppermute | solution.py:152
  6.0 16.5 %collective-permute-start = (bf16[32,256]{1,0:T(8,128)(2,1)S(1)}, bf16[32,256]{1,0:T(8,128)(2,1)S(1)}, u32[]{:S(2)}, u32[]{:S(2)}) collective-permute-start(bf16[32,256]{1,0:T(8,128)(2,1)S(1)} %get-tuple-element.13), channel_id=1, source_target_pairs={{0,4},{4,0},{8,12},{12,8},{16,20},{20,16},{24,28},{28,24},{32,36},... | collective-permute-start | bytes 49160 | tf_op jit(solution)/shard_map/ppermute | solution.py:148
  19.3 0.7 copy-start.7
  20.0 0.7 %copy-start.5 = (s32[3072]{0:T(1024)S(1)}, s32[3072]{0:T(1024)}, u32[]{:S(2)}) copy-start(s32[3072]{0:T(1024)} %param.13) | copy-start | bytes 36868
  20.8 0.7 %copy-start.6 = (f32[3072]{0:T(1024)S(1)}, f32[3072]{0:T(1024)}, u32[]{:S(2)}) copy-start(f32[3072]{0:T(1024)} %param.14) | copy-start | bytes 36868
  22.5 0.6 copy-start.3
  22.5 0.6 copy-start.4
  27.6 4.2 %copy-start.2 = (f32[64,1]{1,0:T(8,128)S(1)}, f32[64,1]{1,0:T(8,128)}, u32[]{:S(2)}) copy-start(f32[64,1]{1,0:T(8,128)} %get-tuple-element.11) | copy-start | bytes 772
  27.6 4.3 %copy-start.1 = (bf16[256,256]{1,0:T(8,128)(2,1)S(1)}, bf16[256,256]{1,0:T(8,128)(2,1)}, u32[]{:S(2)}) copy-start(bf16[256,256]{1,0:T(8,128)(2,1)} %get-tuple-element.10) | copy-start | bytes 393220
  27.6 9.6 %all-to-all-start = ((bf16[4,64,320]{2,1,0:T(8,128)(2,1)}), bf16[4,64,320]{2,1,0:T(8,128)(2,1)S(1)}, u32[]{:S(2)}, u32[]{:S(2)}) async-start(bf16[4,64,320]{2,1,0:T(8,128)(2,1)} %bitcast.16), calls=%async_computation | async-start | bytes 393216 | tf_op jit(solution)/shard_map/all_to_all | solution.py:190
  37.3 15.0 %collective-permute-start.2 = (f32[64,32]{1,0:T(8,128)S(1)}, f32[64,32]{1,0:T(8,128)S(1)}, u32[]{:S(2)}, u32[]{:S(2)}) collective-permute-start(f32[64,32]{1,0:T(8,128)S(1)} %get-tuple-element.14), channel_id=1, source_target_pairs={{0,4},{4,0},{8,12},{12,8},{16,20},{20,16},{24,28},{28,24},{32,36},... | collective-permute-start | bytes 24584 | tf_op jit(solution)/shard_map/ppermute | solution.py:148
  40.6 11.7 %collective-permute-start.3 = (f32[64,32]{1,0:T(8,128)S(1)}, f32[64,32]{1,0:T(8,128)S(1)}, u32[]{:S(2)}, u32[]{:S(2)}) collective-permute-start(f32[64,32]{1,0:T(8,128)S(1)} %get-tuple-element.15), channel_id=1, source_target_pairs={{0,508},{4,8},{8,4},{12,16},{16,12},{20,24},{24,20},{28,32},{32,28... | collective-permute-start | bytes 24584 | tf_op jit(solution)/shard_map/ppermute | solution.py:152
  43.6 23.9 %all-to-all-start.1 = ((bf16[128,3,256]{2,1,0:T(4,128)(2,1)}), bf16[128,3,256]{2,1,0:T(4,128)(2,1)S(1)}, u32[]{:S(2)}, u32[]{:S(2)}) async-start(bf16[128,3,256]{2,1,0:T(4,128)(2,1)} %pad_maximum_fusion), calls=%async_computation.1 | async-start | bytes 524288 | tf_op jit(solution)/shard_map/all_to_all | solution.py:201
  52.3 0.8 %copy-start = (bf16[256,64]{0,1:T(8,128)(2,1)S(1)}, bf16[256,64]{0,1:T(8,128)(2,1)}, u32[]{:S(2)}) copy-start(bf16[256,64]{0,1:T(8,128)(2,1)} %param.11) | copy-start | bytes 98308

commit v2 on v1

v2 whole, which is shorter than its diff:
```python
import jax
import jax.numpy as jnp
from jax import lax
from jax.experimental import pallas as pl
from jax.experimental.pallas import tpu as pltpu
from jax.sharding import Mesh
from jax.sharding import PartitionSpec as P


ARITY = 12
GHOST = 32
CAP = 256
EXT = CAP + 2 * GHOST
DOM = ("dom_0", "dom_1", "dom_2")
CHIP = ("dom_0", "dom_1")
NDOM = 128
EPS = 1e-06
F32 = jnp.float32
BF16 = jnp.bfloat16
VMEM = pl.BlockSpec(memory_space=pltpu.VMEM)
SMEM = pl.BlockSpec(memory_space=pltpu.SMEM)
HBM = pl.BlockSpec(memory_space=pltpu.HBM)


def dot(a, b, ca=1, cb=0):
    return lax.dot_general(a, b, (((ca,), (cb,)), ((), ())), preferred_element_type=F32)


def sigmoid(v):
    return 1.0 / (1.0 + jnp.exp(-v))


def two_parts(v):
    high = v.astype(BF16)
    return high, (v - high.astype(F32)).astype(BF16)


def in_vmem(x):
    return pltpu.with_memory_space_constraint(x, pltpu.VMEM)


def in_hbm(x):
    return pltpu.with_memory_space_constraint(x, pltpu.HBM)


def stay(shape, dtype):
    return pltpu.VMEM(shape, dtype)


def live_row(count):
    bond = lax.broadcasted_iota(jnp.int32, (1, CAP), 1)
    return ((bond < count - GHOST) | (bond >= CAP - GHOST)).astype(F32)


def prep_kernel(
    odd_ref, count_ref, src_ref, cos_ref, h_hbm, ws_hbm, wm_hbm, wt_hbm, wf_hbm, gate_w_hbm, cot_hbm,
    hp_ref, w_ref, perm_ref, own_ref, hot_ref, part_ref, cot_live_ref,
    h_ref, gate_w_ref, cot_ref, sems,
):
    copies = [
        pltpu.make_async_copy(ref, w_ref.at[pl.ds(64 * n, 64)], sems.at[n])
        for n, ref in enumerate((ws_hbm, wm_hbm, wt_hbm, wf_hbm))
    ]
    copies.append(pltpu.make_async_copy(h_hbm, h_ref, sems.at[4]))
    copies.append(pltpu.make_async_copy(gate_w_hbm, gate_w_ref, sems.at[5]))
    copies.append(pltpu.make_async_copy(cot_hbm, cot_ref, sems.at[6]))
    for copy in copies:
        copy.start()
    odd = odd_ref[0]
    rows = 256 // NDOM
    m = lax.broadcasted_iota(jnp.int32, (256, 256), 0)
    i = lax.broadcasted_iota(jnp.int32, (256, 256), 1)
    half = jnp.where(m < 128, 1 - odd, odd)
    m = m & 127
    want = (m // rows) * (2 * rows) + rows * half + m % rows
    perm = (i == want).astype(F32).astype(BF16)
    perm_ref[...] = perm
    src = src_ref[...].T
    cos = cos_ref[...].T
    low_base = jnp.where(odd == 1, CAP, CAP + GHOST)
    high_base = jnp.where(odd == 1, CAP + GHOST, CAP)
    row = jnp.where(
        src < GHOST,
        src + low_base,
        jnp.where(src >= CAP + GHOST, src - (CAP + GHOST) + high_base, src - GHOST),
    )
    row_id = lax.broadcasted_iota(jnp.int32, (EXT, CAP), 0)
    for k in range(ARITY):
        hot_ref[k] = (row_id == row[k : k + 1]).astype(F32).astype(BF16)
    for copy in copies:
        copy.wait()
    cot_live_ref[...] = cot_ref[...].astype(F32) * live_row(count_ref[0])
    h_t = h_ref[...].T
    w_t = w_ref[...]
    hp_ref[...] = dot(perm, h_t).astype(BF16)
    own = dot(w_t, h_t)
    own_ref[...] = own[128:]
    high, low = two_parts(own[:128])
    table = jnp.concatenate([high, low], axis=0)
    eye = lax.broadcasted_iota(jnp.int32, (64, 64), 0) == lax.broadcasted_iota(jnp.int32, (64, 64), 1)
    gate_w = jnp.sum(jnp.where(eye, gate_w_ref[...], 0.0), axis=1, keepdims=True)
    for k in range(ARITY):
        picked = dot(table, hot_ref[k, :CAP])
        part_ref[k, 0:64] = picked[0:64] + picked[128:192] + (own[128:192] + gate_w * cos[k : k + 1])
        part_ref[k, 64:128] = picked[64:128] + picked[192:256]


def prep_stage(odd, count, src, cos, *held):
    return pl.pallas_call(
        prep_kernel,
        out_shape=(
            stay((256, CAP), BF16),
            stay((256, 256), BF16),
            stay((256, 256), BF16),
            stay((128, CAP), F32),
            stay((ARITY, EXT, CAP), BF16),
            stay((ARITY, 128, CAP), F32),
            stay((64, CAP), F32),
        ),
        in_specs=[SMEM, SMEM, VMEM, VMEM] + [HBM] * 7,
        out_specs=(VMEM,) * 7,
        scratch_shapes=[
            pltpu.VMEM((CAP, 256), BF16),
            pltpu.VMEM((1, 64), F32),
            pltpu.VMEM((64, CAP), BF16),
            pltpu.SemaphoreType.DMA((7,)),
        ],
        compiler_params=pltpu.CompilerParams(vmem_limit_bytes=24 << 20),
        name="prep_stage",
    )(odd, count, src, cos, *(in_hbm(x) for x in held))


def angle_kernel(
    count_ref, ga_ref, gb_ref, cos_ref, hp_ref, w_ref, perm_ref, own_ref, hot_ref, part_ref, cot_live_ref,
    whole_ref, send_ref, keep_ref,
    sig_ref, msg_ref,
):
    w_t = w_ref[...]
    gh_t = jnp.concatenate([ga_ref[...], gb_ref[...]], axis=0).T
    high, low = two_parts(dot(w_t[:128], gh_t))
    table = jnp.concatenate([high, low], axis=1)
    gh_p = dot(perm_ref[...], gh_t).astype(BF16)
    cos = cos_ref[...].T

    live = live_row(count_ref[0])
    num = jnp.zeros((64, CAP), F32)
    den = jnp.zeros((64, CAP), F32)
    for k in range(ARITY):
        far = hot_ref[k, CAP:]
        picked = dot(table, jnp.concatenate([far, far], axis=0)) + part_ref[k]
        p4 = picked[64:128]
        sig = sigmoid(picked[0:64])
        gate = sig * live
        num += gate * p4
        den += gate
        sig_ref[k] = sig
        msg_ref[k] = p4
    den = den + EPS
    agg = num / den
    z = own_ref[64:128] + agg
    s = sigmoid(z)
    dz = cot_live_ref[...] * (s * (1.0 + z * (1.0 - s)))
    dnum = dz / den
    dden = -(dnum * agg)

    dq2 = jnp.zeros((64, CAP), F32)
    dgw = jnp.zeros((64, CAP), F32)
    acc = jnp.zeros((EXT, 128), F32)
    for k in range(ARITY):
        sig = sig_ref[k]
        gate = sig * live
        dgate = dnum * msg_ref[k] + dden
        dmsg = gate * dnum
        dpre = dgate * gate * (1.0 - sig)
        dq2 += dpre
        dgw += dpre * cos[k : k + 1]
        both = jnp.concatenate([dpre, dmsg], axis=0).astype(BF16)
        acc += dot(hot_ref[k], both, 1, 1)
    edge = acc.astype(BF16)
    bonds = jnp.concatenate([dq2, dz], axis=0).astype(BF16).T
    full = jnp.concatenate([edge[:CAP], bonds], axis=1)
    edge_far = edge[CAP:]
    whole_ref[:, :CAP] = dot(full, w_t).astype(BF16).T
    whole_ref[:, CAP:] = dot(edge_far, w_t[:128]).astype(BF16).T
    grads = dot(hp_ref[...], full)
    grads = jnp.concatenate([grads[:, :128] + dot(gh_p, edge_far), grads[:, 128:]], axis=1)
    ones = jnp.ones((8, CAP), BF16)
    dgw_high, dgw_low = two_parts(dgw)
    gate = dot(ones, dgw_high, 1, 1) + dot(ones, dgw_low, 1, 1)
    keep_ref[0:128] = grads[128:256]
    keep_ref[128:136] = jnp.concatenate([gate, jnp.zeros((8, 192), F32)], axis=1)
    send_ref[0:128] = grads[0:128].astype(BF16)
    gate_high, gate_low = two_parts(gate)
    row = jnp.concatenate([gate_high, gate_low, jnp.zeros((8, 128), BF16)], axis=1)
    send_ref[128:144] = jnp.concatenate([row, row], axis=0)


def angle_stage(count, ga, gb, cos, prepared):
    return pl.pallas_call(
        angle_kernel,
        out_shape=(
            jax.ShapeDtypeStruct((256, EXT), BF16),
            jax.ShapeDtypeStruct((144, 256), BF16),
            stay((136, 256), F32),
        ),
        in_specs=[SMEM] + [VMEM] * 10,
        out_specs=(VMEM, VMEM, VMEM),
        scratch_shapes=[
            pltpu.VMEM((ARITY, 64, CAP), F32),
            pltpu.VMEM((ARITY, 64, CAP), F32),
        ],
        compiler_params=pltpu.CompilerParams(vmem_limit_bytes=24 << 20),
        name="angle_stage",
    )(count, in_vmem(ga), in_vmem(gb), cos, *prepared)


def pair_kernel(keep_ref, recv_ref, out_ref):
    out_ref[:, :256] = (keep_ref[0:128] + recv_ref[0:128].astype(F32)).astype(BF16)
    row = recv_ref[128:144].astype(F32)[0:8]
    gate = keep_ref[128:136][:, 0:64] + row[:, 0:64] + row[:, 64:128]
    high, low = two_parts(gate)
    out_ref[:, 256:] = jnp.broadcast_to(jnp.concatenate([high, low], axis=1)[0:1], (128, 128))


def pair_stage(keep, recv):
    return pl.pallas_call(
        pair_kernel,
        out_shape=jax.ShapeDtypeStruct((128, 384), BF16),
        in_specs=[VMEM, VMEM],
        out_specs=VMEM,
        compiler_params=pltpu.CompilerParams(vmem_limit_bytes=24 << 20),
        name="pair_stage",
    )(keep, in_vmem(recv))


def last_kernel(slots_ref, source_ref, target_ref, message_ref, self_ref, gate_ref):
    total = jnp.sum(slots_ref[...].astype(F32), axis=0)
    source_ref[...] = total[:, 0:64]
    message_ref[...] = total[:, 64:128]
    target_ref[...] = total[:, 128:192]
    self_ref[...] = total[:, 192:256]
    gate_ref[...] = total[0:1, 256:320] + total[0:1, 320:384]


def last_stage(slots):
    rows = slots.shape[1]
    square = jax.ShapeDtypeStruct((rows, 64), F32)
    return pl.pallas_call(
        last_kernel,
        out_shape=(square, square, square, square, jax.ShapeDtypeStruct((1, 64), F32)),
        in_specs=[VMEM],
        out_specs=(VMEM,) * 5,
        compiler_params=pltpu.CompilerParams(vmem_limit_bytes=24 << 20),
        name="last_stage",
    )(in_vmem(slots))


def swap_core(x):
    return lax.ppermute(x, DOM, [(i, i ^ 1) for i in range(NDOM)])


def swap_chip(x):
    return lax.ppermute(x, DOM, [(i, (i + 1) % NDOM if i % 2 else (i - 1) % NDOM) for i in range(NDOM)])


def per_device(
    bond_feats,
    cotangent,
    bond_count,
    source,
    cosine,
    w_source,
    w_target,
    w_message,
    w_self,
    gate_angle,
):
    odd = lax.axis_index("dom_2").astype(jnp.int32)
    is_odd = odd == 1
    first, last = bond_feats[:GHOST], bond_feats[CAP - GHOST :]
    ghost_b = swap_chip(jnp.where(is_odd, last, first))
    ghost_a = swap_core(jnp.where(is_odd, first, last))
    src = source.reshape(CAP, ARITY)
    cos = cosine.reshape(CAP, ARITY)
    prepared = prep_stage(
        odd.reshape(1),
        bond_count,
        src,
        cos,
        bond_feats,
        w_source.T,
        w_message.T,
        w_target.T,
        w_self.T,
        gate_angle[None, :],
        cotangent.T,
    )
    whole, send, keep = angle_stage(bond_count, ghost_a, ghost_b, cos, prepared)
    tiles = lax.all_to_all(whole.reshape(4, 64, EXT), "wa", 0, 0, tiled=True)
    recv = swap_core(send)
    slots = pair_stage(keep, recv).reshape(NDOM // 2, 256 // NDOM, 384)
    slots = lax.all_to_all(slots, CHIP, 0, 0, tiled=True)
    summed = tiles.astype(F32).sum(axis=0)
    back_b = swap_chip(summed[:, CAP + GHOST :])
    back_a = swap_core(summed[:, CAP : CAP + GHOST])
    g_source, g_target, g_message, g_self, g_gate = last_stage(slots)

    total = summed[:, :CAP] + prepared[-1]
    to_first = jnp.where(is_odd, back_a, back_b)
    to_last = jnp.where(is_odd, back_b, back_a)
    added = jnp.concatenate([to_first, jnp.zeros((64, CAP - 2 * GHOST), F32), to_last], axis=1)
    bond_grad = (total + added).astype(BF16).T
    return (bond_grad, g_source, g_target, g_message, g_self, g_gate[0])


def solution(mesh):
    finer = Mesh(mesh.devices.reshape(8, 8, 2, mesh.shape["wa"]), ("dom_0", "dom_1", "dom_2", "wa"))
    return jax.shard_map(
        per_device,
        mesh=finer,
        in_specs=(
            P(DOM, None),
            P(DOM, "wa"),
            P(DOM),
            P(DOM),
            P(DOM),
            P(None, "wa"),
            P(None, "wa"),
            P(None, "wa"),
            P(None, "wa"),
            P("wa"),
        ),
        out_specs=(P(DOM, "wa"), P(DOM, "wa"), P(DOM, "wa"), P(DOM, "wa"), P(DOM, "wa"), P("wa")),
        check_vma=False,
    )
```

time: 69.6 us -> 61 us (0.88)
  waiting for transfers between devices: 19 us -> 10.7 us
  starting transfers between devices: 34.8 us -> 38.7 us
  local copies, waits for them, and re-layouts: 5.26 us -> 2.52 us
  other arithmetic: 3.98 us -> 1.49 us
  Pallas kernels: 4.49 us -> 5.57 us
    ppermute x2 -> x3, starting transfers between devices: 15.5 us -> 24.6 us  [swap_core(): return lax.ppermute(x, DOM, [(i, i ^ 1) for i in range(NDOM)])]
    all_to_all x1, waiting for transfers between devices: 5.19 us -> 0.01 us  [per_device(): tiles = lax.all_to_all(whole.reshape(4, 64, EXT), 'wa', 0, 0, tiled=True)]
    all_to_all x1, waiting for transfers between devices: 13.8 us -> 10.7 us  [per_device(): slots = lax.all_to_all(slots, CHIP, 0, 0, tiled=True)]
    pallas_call x0 -> x3, Pallas kernels: none -> 2.79 us  [the longest x1 1.89 us: prep_stage(): pl.pallas_call(prep_kernel, out_shape=(stay((256, CAP), BF16), stay((256,...]
    ppermute x2, starting transfers between devices: 6.49 us -> 3.84 us  [swap_chip(): lax.ppermute(x, DOM, [(i, (i + 1) % NDOM if i % 2 else (i - 1) % NDOM) fo...]
    unnamed x16 -> x0, local copies, waits for them, and re-layouts: 2 us -> none
    all_to_all x1, starting transfers between devices: 8.68 us -> 6.96 us  [per_device(): slots = lax.all_to_all(slots, CHIP, 0, 0, tiled=True)]
    pallas_call x1, Pallas kernels: 4.49 us -> 2.78 us  [angle_stage(): pl.pallas_call(angle_kernel, out_shape=(jax.ShapeDtypeStruct((256, EXT),...]
  transfers between devices with their start and end apart: 6 -> 7, of which waited for: 2 -> 1; matrix products, arithmetic and copies ran while one was open for 7% -> 5% of each run, Pallas kernels for 0% -> 3%
where the time goes in v2:
time: 61 us; the launch traced here: 60.4 us
  starting transfers between devices  38.7 us (63%)
  waiting for transfers between devices  10.7 us (18%)
  Pallas kernels  5.57 us (9%)
  local copies, waits for them, and re-layouts  2.52 us (4%)
  other arithmetic  1.49 us (2%)
  between operations  1.43 us (2%)
    ppermute x3, starting transfers between devices, swap_core(): return lax.ppermute(x, DOM, [(i, i ^ 1) for i in range(NDOM)])  24.6 us
    all_to_all x1, waiting for transfers between devices, per_device(): slots = lax.all_to_all(slots, CHIP, 0, 0, tiled=True)  10.7 us
    all_to_all x1, starting transfers between devices, per_device(): slots = lax.all_to_all(slots, CHIP, 0, 0, tiled=True)  6.96 us
    ppermute x2, starting transfers between devices, swap_chip(): lax.ppermute(x, DOM, [(i, (i + 1) % NDOM if i % 2 else (i - 1) % NDOM) fo...  3.84 us
    all_to_all x1, starting transfers between devices, per_device(): tiles = lax.all_to_all(whole.reshape(4, 64, EXT), 'wa', 0, 0, tiled=True)  3.36 us
    pallas_call x1, Pallas kernels, angle_stage(): pl.pallas_call(angle_kernel, out_shape=(jax.ShapeDtypeStruct((256, EXT),...  2.78 us
    pallas_call x1, Pallas kernels, prep_stage(): pl.pallas_call(prep_kernel, out_shape=(stay((256, CAP), BF16), stay((256,...  1.89 us
  transfers between devices with their start and end apart: 7, of which 1 were waited for; matrix products, arithmetic and copies ran while one was open for 5% of the time, Pallas kernels for 3%

profile of v2, /device:TPU:1, one launch (start us, length us, event | category | flops | bytes accessed | tf_op | source)
XLA Modules:
  0.0 60.4 jit_solution(9784892075107852352)
XLA Ops:
  0.6 0.7 %broadcast_select_fusion.2 = (bf16[32,256]{1,0:T(8,128)(2,1)S(1)}, bf16[32,256]{1,0:T(8,128)(2,1)S(1)}) fusion(pred[]{:T(512)S(6)} %eq.3, bf16[256,256]{1,0:T(8,128)(2,1)} %h_hbm.1), kind=kLoop, calls=%fused_computation.7 | loop fusion | flops 16384 | bytes 65537 | tf_op jit(solution)/shard_map/jit(_where)/select_n | solution.py:281
  1.4 8.7 %collective-permute-start = (bf16[32,256]{1,0:T(8,128)(2,1)S(1)}, bf16[32,256]{1,0:T(8,128)(2,1)S(1)}, u32[]{:S(2)}, u32[]{:S(2)}) collective-permute-start(bf16[32,256]{1,0:T(8,128)(2,1)S(1)} %get-tuple-element.37), channel_id=1, source_target_pairs={{0,4},{4,0},{8,12},{12,8},{16,20},{20,16},{24,28},{28,24},{32,36},... | collective-permute-start | bytes 49160 | tf_op jit(solution)/shard_map/ppermute | solution.py:259
  10.1 1.9 %collective-permute-start.1 = (bf16[32,256]{1,0:T(8,128)(2,1)S(1)}, bf16[32,256]{1,0:T(8,128)(2,1)S(1)}, u32[]{:S(2)}, u32[]{:S(2)}) collective-permute-start(bf16[32,256]{1,0:T(8,128)(2,1)S(1)} %get-tuple-element.36), channel_id=1, source_target_pairs={{0,508},{4,8},{8,4},{12,16},{16,12},{20,24},{24,20},{28,32},{32,28... | collective-permute-start | bytes 49160 | tf_op jit(solution)/shard_map/ppermute | solution.py:263
  12.1 0.8 %reshape.27.cos_ref = f32[256,12]{1,0:T(8,128)S(1)} reshape(f32[3072]{0:T(1024)} %param.14) | data formatting | bytes 24576 | tf_op jit(solution)/shard_map/reshape | solution.py:284
  13.6 0.8 %reshape.29.src_ref = s32[256,12]{1,0:T(8,128)S(1)} reshape(s32[3072]{0:T(1024)} %param.13) | data formatting | bytes 24576 | tf_op jit(solution)/shard_map/reshape | solution.py:283
  14.4 1.9 %prep_stage.1 = (bf16[256,256]{1,0:T(8,128)(2,1)S(1)}, bf16[256,256]{1,0:T(8,128)(2,1)S(1)}, bf16[256,256]{1,0:T(8,128)(2,1)S(1)}, f32[128,256]{1,0:T(8,128)S(1)...) custom-call(s32[1]{0:T(128)} %bitcast.odd_ref, s32[1]{0:T(128)S(6)} %copy.16.count_ref, ...), custom_call_target="tpu_custom_call" | custom-call | tf_op jit(solution)/shard_map/prep_stage/pallas_call | solution.py:109
  16.3 0.0 collective-permute-done.ga_ref
  16.3 0.0 collective-permute-done.1.gb_ref
  16.3 2.8 %angle_stage.1 = (bf16[256,320]{1,0:T(8,128)(2,1)}, bf16[144,256]{1,0:T(8,128)(2,1)S(1)}, f32[136,256]{1,0:T(8,128)S(1)}) custom-call(s32[1]{0:T(128)S(6)} %copy.16.count_ref, bf16[32,256]{1,0:T(8,128)(2,1)S(1)} %collective-permute-done.ga_ref, bf16[32,256]{1,0:T(8,128)(2,1)S(1)} %collective-permute-done.1.gb_ref, f32[256,12]{1,0:T(8,128)S(1)} %reshape.27.cos_ref, ...), custom_call_target="tpu_custom_call" | custom-call | tf_op jit(solution)/shard_map/angle_stage/pallas_call | solution.py:199
  19.1 3.4 %all-to-all-start = ((bf16[4,64,320]{2,1,0:T(8,128)(2,1)}), bf16[4,64,320]{2,1,0:T(8,128)(2,1)S(1)}, u32[]{:S(2)}, u32[]{:S(2)}) async-start(bf16[4,64,320]{2,1,0:T(8,128)(2,1)} %bitcast.7), calls=%async_computation | async-start | bytes 393216 | tf_op jit(solution)/shard_map/all_to_all | solution.py:299
  22.5 9.5 %collective-permute-start.4 = (bf16[144,256]{1,0:T(8,128)(2,1)S(1)}, bf16[144,256]{1,0:T(8,128)(2,1)S(1)}, u32[]{:S(2)}, u32[]{:S(2)}) collective-permute-start(bf16[144,256]{1,0:T(8,128)(2,1)S(1)} %get-tuple-element.30), channel_id=1, source_target_pairs={{0,4},{4,0},{8,12},{12,8},{16,20},{20,16},{24,28},{28,24},{32,36},... | collective-permute-start | bytes 221192 | tf_op jit(solution)/shard_map/ppermute | solution.py:259
  32.0 0.0 all-to-all-done
  32.1 0.1 fusion.3
  32.1 6.3 %collective-permute-start.2 = (f32[64,32]{1,0:T(8,128)S(1)}, f32[64,32]{1,0:T(8,128)S(1)}, u32[]{:S(2)}, u32[]{:S(2)}) collective-permute-start(f32[64,32]{1,0:T(8,128)S(1)} %get-tuple-element.38), channel_id=1, source_target_pairs={{0,4},{4,0},{8,12},{12,8},{16,20},{20,16},{24,28},{28,24},{32,36},... | collective-permute-start | bytes 24584 | tf_op jit(solution)/shard_map/ppermute | solution.py:259
  38.5 1.9 %collective-permute-start.3 = (f32[64,32]{1,0:T(8,128)S(1)}, f32[64,32]{1,0:T(8,128)S(1)}, u32[]{:S(2)}, u32[]{:S(2)}) collective-permute-start(f32[64,32]{1,0:T(8,128)S(1)} %get-tuple-element.39), channel_id=1, source_target_pairs={{0,508},{4,8},{8,4},{12,16},{16,12},{20,24},{24,20},{28,32},{32,28... | collective-permute-start | bytes 24584 | tf_op jit(solution)/shard_map/ppermute | solution.py:263
  40.4 0.1 pad.1.clone
  40.5 0.0 collective-permute-done.4.recv_ref
  40.5 0.2 pair_stage.1
  40.6 0.7 %reshape.31 = bf16[64,2,384]{2,1,0:T(2,128)(2,1)} reshape(bf16[128,384]{1,0:T(8,128)(2,1)S(1)} %pair_stage.1) | data formatting | bytes 196608 | tf_op jit(solution)/shard_map/reshape | solution.py:301
  41.3 7.0 %all-to-all-start.1 = ((bf16[64,2,384]{2,1,0:T(2,128)(2,1)}), bf16[64,2,384]{2,1,0:T(2,128)(2,1)S(1)}, u32[]{:S(2)}, u32[]{:S(2)}) async-start(bf16[64,2,384]{2,1,0:T(2,128)(2,1)} %reshape.31), calls=%async_computation.1 | async-start | bytes 196608 | tf_op jit(solution)/shard_map/all_to_all | solution.py:302
  48.3 0.0 collective-permute-done.2
  48.3 0.0 collective-permute-done.3
  48.3 0.7 %fusion.2 = bf16[256,64]{0,1:T(8,128)(2,1)} fusion(f32[64,32]{1,0:T(8,128)S(1)} %get-tuple-element.41, f32[64,32]{1,0:T(8,128)S(1)} %get-tuple-element.40, f32[64,256]{1,0:T(8,128)S(1)} %get-tuple-element.27.cot_live_ref, f32[64,320]{1,0:T(8,128)S(1)} %convert_reduce_fusion, f32[256]{0:T(256)S(1)} %pad.1.clone), kind=kLoop, calls=%fused_computation.4 | loop fusion | flops 81920 | bytes 181248 | tf_op jit(solution)/shard_map/transpose | solution.py:312
  49.0 10.7 %all-to-all-done.1.slots_ref = bf16[64,2,384]{2,1,0:T(2,128)(2,1)S(1)} async-done(((bf16[64,2,384]{2,1,0:T(2,128)(2,1)}), bf16[64,2,384]{2,1,0:T(2,128)(2,1)S(1)}, u32[]{:S(2)}, u32[]{:S(2)}) %all-to-all-start.1) | async-done | bytes 98336 | tf_op jit(solution)/shard_map/all_to_all | solution.py:302
  59.7 0.7 %last_stage.1 = (f32[2,64]{1,0:T(2,128)}, f32[2,64]{1,0:T(2,128)}, f32[2,64]{1,0:T(2,128)}, f32[2,64]{1,0:T(2,128)}, f32[1,64]{1,0:T(1,128)}) custom-call(bf16[64,2,384]{2,1,0:T(2,128)(2,1)S(1)} %all-to-all-done.1.slots_ref), custom_call_target="tpu_custom_call" | custom-call | tf_op jit(solution)/shard_map/last_stage/pallas_call | solution.py:248
  (3 shorter events, 0.0 us)
Async XLA Ops:
  1.4 14.9 %collective-permute-start = (bf16[32,256]{1,0:T(8,128)(2,1)S(1)}, bf16[32,256]{1,0:T(8,128)(2,1)S(1)}, u32[]{:S(2)}, u32[]{:S(2)}) collective-permute-start(bf16[32,256]{1,0:T(8,128)(2,1)S(1)} %get-tuple-element.37), channel_id=1, source_target_pairs={{0,4},{4,0},{8,12},{12,8},{16,20},{20,16},{24,28},{28,24},{32,36},... | collective-permute-start | bytes 49160 | tf_op jit(solution)/shard_map/ppermute | solution.py:259
  10.1 6.2 %collective-permute-start.1 = (bf16[32,256]{1,0:T(8,128)(2,1)S(1)}, bf16[32,256]{1,0:T(8,128)(2,1)S(1)}, u32[]{:S(2)}, u32[]{:S(2)}) collective-permute-start(bf16[32,256]{1,0:T(8,128)(2,1)S(1)} %get-tuple-element.36), channel_id=1, source_target_pairs={{0,508},{4,8},{8,4},{12,16},{16,12},{20,24},{24,20},{28,32},{32,28... | collective-permute-start | bytes 49160 | tf_op jit(solution)/shard_map/ppermute | solution.py:263
  19.1 12.9 %all-to-all-start = ((bf16[4,64,320]{2,1,0:T(8,128)(2,1)}), bf16[4,64,320]{2,1,0:T(8,128)(2,1)S(1)}, u32[]{:S(2)}, u32[]{:S(2)}) async-start(bf16[4,64,320]{2,1,0:T(8,128)(2,1)} %bitcast.7), calls=%async_computation | async-start | bytes 393216 | tf_op jit(solution)/shard_map/all_to_all | solution.py:299
  22.5 18.0 %collective-permute-start.4 = (bf16[144,256]{1,0:T(8,128)(2,1)S(1)}, bf16[144,256]{1,0:T(8,128)(2,1)S(1)}, u32[]{:S(2)}, u32[]{:S(2)}) collective-permute-start(bf16[144,256]{1,0:T(8,128)(2,1)S(1)} %get-tuple-element.30), channel_id=1, source_target_pairs={{0,4},{4,0},{8,12},{12,8},{16,20},{20,16},{24,28},{28,24},{32,36},... | collective-permute-start | bytes 221192 | tf_op jit(solution)/shard_map/ppermute | solution.py:259
  32.1 16.1 %collective-permute-start.2 = (f32[64,32]{1,0:T(8,128)S(1)}, f32[64,32]{1,0:T(8,128)S(1)}, u32[]{:S(2)}, u32[]{:S(2)}) collective-permute-start(f32[64,32]{1,0:T(8,128)S(1)} %get-tuple-element.38), channel_id=1, source_target_pairs={{0,4},{4,0},{8,12},{12,8},{16,20},{20,16},{24,28},{28,24},{32,36},... | collective-permute-start | bytes 24584 | tf_op jit(solution)/shard_map/ppermute | solution.py:259
  38.5 9.8 %collective-permute-start.3 = (f32[64,32]{1,0:T(8,128)S(1)}, f32[64,32]{1,0:T(8,128)S(1)}, u32[]{:S(2)}, u32[]{:S(2)}) collective-permute-start(f32[64,32]{1,0:T(8,128)S(1)} %get-tuple-element.39), channel_id=1, source_target_pairs={{0,508},{4,8},{8,4},{12,16},{16,12},{20,24},{24,20},{28,32},{32,28... | collective-permute-start | bytes 24584 | tf_op jit(solution)/shard_map/ppermute | solution.py:263
  41.3 18.4 %all-to-all-start.1 = ((bf16[64,2,384]{2,1,0:T(2,128)(2,1)}), bf16[64,2,384]{2,1,0:T(2,128)(2,1)S(1)}, u32[]{:S(2)}, u32[]{:S(2)}) async-start(bf16[64,2,384]{2,1,0:T(2,128)(2,1)} %reshape.31), calls=%async_computation.1 | async-start | bytes 196608 | tf_op jit(solution)/shard_map/all_to_all | solution.py:302

commit v3 on v2

--- a/solution.py
+++ b/solution.py
@@ -8,6 +8,7 @@
 
 
 ARITY = 12
+CHUNK = 3
 GHOST = 32
 CAP = 256
 EXT = CAP + 2 * GHOST
@@ -52,11 +53,39 @@
     return ((bond < count - GHOST) | (bond >= CAP - GHOST)).astype(F32)
 
 
+def by_slot(src_ref, cos_ref):
+    def grouped(ref):
+        return jnp.concatenate([ref[pl.ds(t, 8, stride=3), :] for t in range(3)], axis=1)
+
+    cos = grouped(cos_ref)
+    one = cos.astype(BF16)
+    rest = cos - one.astype(F32)
+    two = rest.astype(BF16)
+    three = (rest - two.astype(F32)).astype(BF16)
+    middle = EXT // 2
+    src = (grouped(src_ref) - middle).astype(F32)
+    parts = jnp.concatenate([src, one.astype(F32), two.astype(F32), three.astype(F32)], axis=0).astype(BF16)
+    spot = lax.broadcasted_iota(jnp.int32, (384, CAP), 0)
+    start = (lax.broadcasted_iota(jnp.int32, (1, CAP), 1) & 31) * ARITY
+    inside = (spot >= start) & (spot < start + ARITY)
+    slot = lax.broadcasted_iota(jnp.int32, (16, 384), 1) % ARITY
+    slot = (slot == lax.broadcasted_iota(jnp.int32, (16, 384), 0)).astype(F32).astype(BF16)
+    group = lax.broadcasted_iota(jnp.int32, (32, CAP), 0)
+    wanted = lax.broadcasted_iota(jnp.int32, (32, CAP), 1) >> 5
+    rows = []
+    for n in range(4):
+        pick = (group == wanted + 8 * n).astype(F32).astype(BF16)
+        spread = jnp.where(inside, dot(parts, pick, 0, 0), 0.0).astype(BF16)
+        rows.append(dot(slot, spread))
+    return rows[0].astype(jnp.int32) + middle, rows[1] + rows[2] + rows[3]
+
+
 def prep_kernel(
-    odd_ref, count_ref, src_ref, cos_ref, h_hbm, ws_hbm, wm_hbm, wt_hbm, wf_hbm, gate_w_hbm, cot_hbm,
-    hp_ref, w_ref, perm_ref, own_ref, hot_ref, part_ref, cot_live_ref,
-    h_ref, gate_w_ref, cot_ref, sems,
+    odd_ref, count_hbm, src_hbm, cos_hbm, h_hbm, ws_hbm, wm_hbm, wt_hbm, wf_hbm, gate_w_hbm, cot_hbm,
+    hp_ref, w_ref, perm_ref, own_ref, hot_ref, part_ref, live_ref, cot_live_ref, cos_t_ref,
+    h_ref, gate_w_ref, cot_ref, count_ref, src_ref, cos_ref, sems,
 ):
+    first = [pltpu.make_async_copy(src_hbm, src_ref, sems.at[8]), pltpu.make_async_copy(cos_hbm, cos_ref, sems.at[9])]
     copies = [
         pltpu.make_async_copy(ref, w_ref.at[pl.ds(64 * n, 64)], sems.at[n])
         for n, ref in enumerate((ws_hbm, wm_hbm, wt_hbm, wf_hbm))
@@ -64,19 +93,22 @@
     copies.append(pltpu.make_async_copy(h_hbm, h_ref, sems.at[4]))
     copies.append(pltpu.make_async_copy(gate_w_hbm, gate_w_ref, sems.at[5]))
     copies.append(pltpu.make_async_copy(cot_hbm, cot_ref, sems.at[6]))
-    for copy in copies:
+    copies.append(pltpu.make_async_copy(count_hbm, count_ref, sems.at[7]))
+    for copy in first + copies:
         copy.start()
     odd = odd_ref[0]
     rows = 256 // NDOM
-    m = lax.broadcasted_iota(jnp.int32, (256, 256), 0)
+    m = lax.broadcasted_iota(jnp.int32, (256, 1), 0)
     i = lax.broadcasted_iota(jnp.int32, (256, 256), 1)
     half = jnp.where(m < 128, 1 - odd, odd)
     m = m & 127
     want = (m // rows) * (2 * rows) + rows * half + m % rows
     perm = (i == want).astype(F32).astype(BF16)
     perm_ref[...] = perm
-    src = src_ref[...].T
-    cos = cos_ref[...].T
+    for copy in first:
+        copy.wait()
+    src, cos = by_slot(src_ref, cos_ref)
+    cos_t_ref[...] = cos
     low_base = jnp.where(odd == 1, CAP, CAP + GHOST)
     high_base = jnp.where(odd == 1, CAP + GHOST, CAP)
     row = jnp.where(
@@ -84,12 +116,20 @@
         src + low_base,
         jnp.where(src >= CAP + GHOST, src - (CAP + GHOST) + high_base, src - GHOST),
     )
-    row_id = lax.broadcasted_iota(jnp.int32, (EXT, CAP), 0)
+    near_row = row.astype(F32).astype(BF16)
+    far_row = (row - CAP).astype(F32).astype(BF16)
+    near_id = lax.broadcasted_iota(jnp.int32, (CAP, CAP), 0).astype(F32).astype(BF16)
+    far_id = lax.broadcasted_iota(jnp.int32, (2 * GHOST, CAP), 0).astype(F32).astype(BF16)
+    one, zero = jnp.ones((), BF16), jnp.zeros((), BF16)
     for k in range(ARITY):
-        hot_ref[k] = (row_id == row[k : k + 1]).astype(F32).astype(BF16)
+        at = slice(k * CAP, (k + 1) * CAP)
+        hot_ref[:CAP, at] = jnp.where(near_id == near_row[k : k + 1], one, zero)
+        hot_ref[CAP:, at] = jnp.where(far_id == far_row[k : k + 1], one, zero)
     for copy in copies:
         copy.wait()
-    cot_live_ref[...] = cot_ref[...].astype(F32) * live_row(count_ref[0])
+    live = live_row(count_ref[0])
+    live_ref[...] = jnp.broadcast_to(live, (8, CAP))
+    cot_live_ref[...] = cot_ref[...].astype(F32) * live
     h_t = h_ref[...].T
     w_t = w_ref[...]
     hp_ref[...] = dot(perm, h_t).astype(BF16)
@@ -100,12 +140,12 @@
     eye = lax.broadcasted_iota(jnp.int32, (64, 64), 0) == lax.broadcasted_iota(jnp.int32, (64, 64), 1)
     gate_w = jnp.sum(jnp.where(eye, gate_w_ref[...], 0.0), axis=1, keepdims=True)
     for k in range(ARITY):
-        picked = dot(table, hot_ref[k, :CAP])
+        picked = dot(table, hot_ref[:CAP, k * CAP : (k + 1) * CAP])
         part_ref[k, 0:64] = picked[0:64] + picked[128:192] + (own[128:192] + gate_w * cos[k : k + 1])
         part_ref[k, 64:128] = picked[64:128] + picked[192:256]
 
 
-def prep_stage(odd, count, src, cos, *held):
+def prep_stage(odd, count, *held):
     return pl.pallas_call(
         prep_kernel,
         out_shape=(
@@ -113,71 +153,87 @@
             stay((256, 256), BF16),
             stay((256, 256), BF16),
             stay((128, CAP), F32),
-            stay((ARITY, EXT, CAP), BF16),
+            stay((EXT, ARITY * CAP), BF16),
             stay((ARITY, 128, CAP), F32),
+            stay((8, CAP), F32),
             stay((64, CAP), F32),
+            stay((16, CAP), F32),
         ),
-        in_specs=[SMEM, SMEM, VMEM, VMEM] + [HBM] * 7,
-        out_specs=(VMEM,) * 7,
+        in_specs=[SMEM] + [HBM] * 10,
+        out_specs=(VMEM,) * 9,
         scratch_shapes=[
             pltpu.VMEM((CAP, 256), BF16),
             pltpu.VMEM((1, 64), F32),
             pltpu.VMEM((64, CAP), BF16),
-            pltpu.SemaphoreType.DMA((7,)),
+            pltpu.SMEM((1,), jnp.int32),
+            pltpu.VMEM((24, 128), jnp.int32),
+            pltpu.VMEM((24, 128), F32),
+            pltpu.SemaphoreType.DMA((10,)),
         ],
         compiler_params=pltpu.CompilerParams(vmem_limit_bytes=24 << 20),
         name="prep_stage",
-    )(odd, count, src, cos, *(in_hbm(x) for x in held))
+    )(odd, count, *(in_hbm(x) for x in held))
 
 
 def angle_kernel(
-    count_ref, ga_ref, gb_ref, cos_ref, hp_ref, w_ref, perm_ref, own_ref, hot_ref, part_ref, cot_live_ref,
+    ga_ref, gb_ref, hp_ref, w_ref, perm_ref, own_ref, hot_ref, part_ref, live_ref, cot_live_ref, cos_ref,
     whole_ref, send_ref, keep_ref,
-    sig_ref, msg_ref,
+    pick_ref, sig_ref, both_ref, bonds_ref, slope_ref,
 ):
     w_t = w_ref[...]
     gh_t = jnp.concatenate([ga_ref[...], gb_ref[...]], axis=0).T
     high, low = two_parts(dot(w_t[:128], gh_t))
     table = jnp.concatenate([high, low], axis=1)
     gh_p = dot(perm_ref[...], gh_t).astype(BF16)
-    cos = cos_ref[...].T
-
-    live = live_row(count_ref[0])
-    num = jnp.zeros((64, CAP), F32)
-    den = jnp.zeros((64, CAP), F32)
     for k in range(ARITY):
-        far = hot_ref[k, CAP:]
-        picked = dot(table, jnp.concatenate([far, far], axis=0)) + part_ref[k]
-        p4 = picked[64:128]
-        sig = sigmoid(picked[0:64])
-        gate = sig * live
-        num += gate * p4
-        den += gate
-        sig_ref[k] = sig
-        msg_ref[k] = p4
-    den = den + EPS
-    agg = num / den
-    z = own_ref[64:128] + agg
-    s = sigmoid(z)
-    dz = cot_live_ref[...] * (s * (1.0 + z * (1.0 - s)))
-    dnum = dz / den
-    dden = -(dnum * agg)
-
-    dq2 = jnp.zeros((64, CAP), F32)
-    dgw = jnp.zeros((64, CAP), F32)
+        far = hot_ref[CAP:, k * CAP : (k + 1) * CAP]
+        pick_ref[k] = dot(table, jnp.concatenate([far, far], axis=0)) + part_ref[k]
+
+    for at in (slice(0, 128), slice(128, 256)):
+        live = live_ref[0:1, at]
+        num = jnp.zeros((64, 128), F32)
+        den = jnp.zeros((64, 128), F32)
+        for k in range(ARITY):
+            sig = sigmoid(pick_ref[k, 0:64, at])
+            gate = sig * live
+            num += gate * pick_ref[k, 64:128, at]
+            den += gate
+            sig_ref[k, :, at] = sig
+        den = den + EPS
+        agg = num / den
+        z = own_ref[64:128, at] + agg
+        s = sigmoid(z)
+        dz = cot_live_ref[:, at] * (s * (1.0 + z * (1.0 - s)))
+        dnum = dz / den
+        dden = -(dnum * agg)
+        bonds_ref[64:128, at] = dz.astype(BF16)
+        slope_ref[0:64, at] = dnum
+        slope_ref[64:128, at] = dden
+    zero = jnp.zeros((64, 128), F32)
+    dq2, dgw = [zero, zero], [zero, zero]
     acc = jnp.zeros((EXT, 128), F32)
-    for k in range(ARITY):
-        sig = sig_ref[k]
-        gate = sig * live
-        dgate = dnum * msg_ref[k] + dden
-        dmsg = gate * dnum
-        dpre = dgate * gate * (1.0 - sig)
-        dq2 += dpre
-        dgw += dpre * cos[k : k + 1]
-        both = jnp.concatenate([dpre, dmsg], axis=0).astype(BF16)
-        acc += dot(hot_ref[k], both, 1, 1)
+    for first in range(0, ARITY, CHUNK):
+        for n in (0, 1):
+            at = slice(n * 128, (n + 1) * 128)
+            live = live_ref[0:1, at]
+            dnum = slope_ref[0:64, at]
+            dden = slope_ref[64:128, at]
+            for k in range(first, first + CHUNK):
+                sig = sig_ref[k, :, at]
+                gate = sig * live
+                dgate = dnum * pick_ref[k, 64:128, at] + dden
+                dpre = dgate * gate * (1.0 - sig)
+                dq2[n] += dpre
+                dgw[n] += dpre * cos_ref[k : k + 1, at]
+                lane = slice(k * CAP + at.start, k * CAP + at.stop)
+                both_ref[0:64, lane] = dpre.astype(BF16)
+                both_ref[64:128, lane] = (gate * dnum).astype(BF16)
+        lanes = slice(first * CAP, (first + CHUNK) * CAP)
+        acc += dot(hot_ref[:, lanes], both_ref[:, lanes], 1, 1)
+    dgw = jnp.concatenate(dgw, axis=1)
+    bonds_ref[0:64] = jnp.concatenate(dq2, axis=1).astype(BF16)
     edge = acc.astype(BF16)
-    bonds = jnp.concatenate([dq2, dz], axis=0).astype(BF16).T
+    bonds = bonds_ref[...].T
     full = jnp.concatenate([edge[:CAP], bonds], axis=1)
     edge_far = edge[CAP:]
     whole_ref[:, :CAP] = dot(full, w_t).astype(BF16).T
@@ -195,23 +251,26 @@
     send_ref[128:144] = jnp.concatenate([row, row], axis=0)
 
 
-def angle_stage(count, ga, gb, cos, prepared):
+def angle_stage(ga, gb, prepared):
     return pl.pallas_call(
         angle_kernel,
         out_shape=(
-            jax.ShapeDtypeStruct((256, EXT), BF16),
-            jax.ShapeDtypeStruct((144, 256), BF16),
+            stay((256, EXT), BF16),
+            stay((144, 256), BF16),
             stay((136, 256), F32),
         ),
-        in_specs=[SMEM] + [VMEM] * 10,
+        in_specs=[VMEM] * 11,
         out_specs=(VMEM, VMEM, VMEM),
         scratch_shapes=[
+            pltpu.VMEM((ARITY, 128, CAP), F32),
             pltpu.VMEM((ARITY, 64, CAP), F32),
-            pltpu.VMEM((ARITY, 64, CAP), F32),
+            pltpu.VMEM((128, ARITY * CAP), BF16),
+            pltpu.VMEM((128, CAP), BF16),
+            pltpu.VMEM((128, CAP), F32),
         ],
         compiler_params=pltpu.CompilerParams(vmem_limit_bytes=24 << 20),
         name="angle_stage",
-    )(count, in_vmem(ga), in_vmem(gb), cos, *prepared)
+    )(in_vmem(ga), in_vmem(gb), *prepared)
 
 
 def pair_kernel(keep_ref, recv_ref, out_ref):
@@ -278,15 +337,14 @@
     odd = lax.axis_index("dom_2").astype(jnp.int32)
     is_odd = odd == 1
     first, last = bond_feats[:GHOST], bond_feats[CAP - GHOST :]
-    ghost_b = swap_chip(jnp.where(is_odd, last, first))
-    ghost_a = swap_core(jnp.where(is_odd, first, last))
-    src = source.reshape(CAP, ARITY)
-    cos = cosine.reshape(CAP, ARITY)
+    to_b, to_a = jnp.where(is_odd, last, first), jnp.where(is_odd, first, last)
+    ghost_b = swap_chip(to_b)
+    ghost_a = swap_core(to_a)
     prepared = prep_stage(
         odd.reshape(1),
         bond_count,
-        src,
-        cos,
+        source.reshape(24, 128),
+        cosine.reshape(24, 128),
         bond_feats,
         w_source.T,
         w_message.T,
@@ -295,17 +353,18 @@
         gate_angle[None, :],
         cotangent.T,
     )
-    whole, send, keep = angle_stage(bond_count, ghost_a, ghost_b, cos, prepared)
+    whole, send, keep = angle_stage(ghost_a, ghost_b, prepared)
     tiles = lax.all_to_all(whole.reshape(4, 64, EXT), "wa", 0, 0, tiled=True)
     recv = swap_core(send)
     slots = pair_stage(keep, recv).reshape(NDOM // 2, 256 // NDOM, 384)
     slots = lax.all_to_all(slots, CHIP, 0, 0, tiled=True)
     summed = tiles.astype(F32).sum(axis=0)
-    back_b = swap_chip(summed[:, CAP + GHOST :])
-    back_a = swap_core(summed[:, CAP : CAP + GHOST])
+    to_a, to_b = summed[:, CAP : CAP + GHOST], summed[:, CAP + GHOST :]
+    back_b = swap_chip(to_b)
+    back_a = swap_core(to_a)
     g_source, g_target, g_message, g_self, g_gate = last_stage(slots)
 
-    total = summed[:, :CAP] + prepared[-1]
+    total = summed[:, :CAP] + prepared[-2]
     to_first = jnp.where(is_odd, back_a, back_b)
     to_last = jnp.where(is_odd, back_b, back_a)
     added = jnp.concatenate([to_first, jnp.zeros((64, CAP - 2 * GHOST), F32), to_last], axis=1)

time: 61 us -> 61 us (level)
  local copies, waits for them, and re-layouts: 2.52 us -> 0.83 us
  Pallas kernels: 5.57 us -> 6.63 us
    reshape x2 -> x0, local copies, waits for them, and re-layouts: 1.69 us -> none  [the longest x1 0.85 us: per_device(): cos = cosine.reshape(CAP, ARITY)]
    pallas_call x1, Pallas kernels: 1.89 us -> 2.86 us  [prep_stage(): pl.pallas_call(prep_kernel, out_shape=(stay((256, CAP), BF16), stay((256,...]
    all_to_all x1, waiting for transfers between devices: 10.7 us -> 11.3 us  [per_device(): slots = lax.all_to_all(slots, CHIP, 0, 0, tiled=True)]
  transfers between devices with their start and end apart: 7 -> 7, of which waited for: 1 -> 1; matrix products, arithmetic and copies ran while one was open for 5% -> 3% of each run, Pallas kernels for 3% -> 5%
where the time goes in v3:
time: 61 us; the launch traced here: 60.4 us
  starting transfers between devices  38.7 us (63%)
  waiting for transfers between devices  11.3 us (19%)
  Pallas kernels  6.63 us (11%)
  other arithmetic  1.48 us (2%)
  between operations  1.41 us (2%)
  local copies, waits for them, and re-layouts  0.83 us (1%)
    ppermute x3, starting transfers between devices, swap_core(): return lax.ppermute(x, DOM, [(i, i ^ 1) for i in range(NDOM)])  24.6 us
    all_to_all x1, waiting for transfers between devices, per_device(): slots = lax.all_to_all(slots, CHIP, 0, 0, tiled=True)  11.3 us
    all_to_all x1, starting transfers between devices, per_device(): slots = lax.all_to_all(slots, CHIP, 0, 0, tiled=True)  6.96 us
    ppermute x2, starting transfers between devices, swap_chip(): lax.ppermute(x, DOM, [(i, (i + 1) % NDOM if i % 2 else (i - 1) % NDOM) fo...  3.84 us
    all_to_all x1, starting transfers between devices, per_device(): tiles = lax.all_to_all(whole.reshape(4, 64, EXT), 'wa', 0, 0, tiled=True)  3.36 us
    pallas_call x1, Pallas kernels, angle_stage(): pl.pallas_call(angle_kernel, out_shape=(stay((256, EXT), BF16), stay((144...  2.88 us
    pallas_call x1, Pallas kernels, prep_stage(): pl.pallas_call(prep_kernel, out_shape=(stay((256, CAP), BF16), stay((256,...  2.86 us
  transfers between devices with their start and end apart: 7, of which 1 were waited for; matrix products, arithmetic and copies ran while one was open for 3% of the time, Pallas kernels for 5%

profile of v3, /device:TPU:1, one launch (start us, length us, event | category | flops | bytes accessed | tf_op | source)
XLA Modules:
  0.0 60.4 jit_solution(17871794706269265890)
XLA Ops:
  0.6 0.7 %broadcast_select_fusion.2 = (bf16[32,256]{1,0:T(8,128)(2,1)S(1)}, bf16[32,256]{1,0:T(8,128)(2,1)S(1)}) fusion(pred[]{:T(512)S(6)} %eq.3, bf16[256,256]{1,0:T(8,128)(2,1)} %h_hbm.1), kind=kLoop, calls=%fused_computation.7 | loop fusion | flops 16384 | bytes 65537 | tf_op jit(solution)/shard_map/jit(_where)/select_n | solution.py:340
  1.4 8.7 %collective-permute-start = (bf16[32,256]{1,0:T(8,128)(2,1)S(1)}, bf16[32,256]{1,0:T(8,128)(2,1)S(1)}, u32[]{:S(2)}, u32[]{:S(2)}) collective-permute-start(bf16[32,256]{1,0:T(8,128)(2,1)S(1)} %get-tuple-element.41), channel_id=1, source_target_pairs={{0,4},{4,0},{8,12},{12,8},{16,20},{20,16},{24,28},{28,24},{32,36},... | collective-permute-start | bytes 49160 | tf_op jit(solution)/shard_map/ppermute | solution.py:318
  10.1 1.9 %collective-permute-start.1 = (bf16[32,256]{1,0:T(8,128)(2,1)S(1)}, bf16[32,256]{1,0:T(8,128)(2,1)S(1)}, u32[]{:S(2)}, u32[]{:S(2)}) collective-permute-start(bf16[32,256]{1,0:T(8,128)(2,1)S(1)} %get-tuple-element.40), channel_id=1, source_target_pairs={{0,508},{4,8},{8,4},{12,16},{16,12},{20,24},{24,20},{28,32},{32,28... | collective-permute-start | bytes 49160 | tf_op jit(solution)/shard_map/ppermute | solution.py:322
  12.7 2.9 %prep_stage.1 = (bf16[256,256]{1,0:T(8,128)(2,1)S(1)}, bf16[256,256]{1,0:T(8,128)(2,1)S(1)}, bf16[256,256]{1,0:T(8,128)(2,1)S(1)}, f32[128,256]{1,0:T(8,128)S(1)...) custom-call(s32[1]{0:T(128)} %bitcast.odd_ref, ...), custom_call_target="tpu_custom_call" | custom-call | tf_op jit(solution)/shard_map/prep_stage/pallas_call | solution.py:149
  15.6 0.0 collective-permute-done.ga_ref
  15.6 0.0 collective-permute-done.1.gb_ref
  15.6 2.9 %angle_stage.1 = (bf16[256,320]{1,0:T(8,128)(2,1)}, bf16[144,256]{1,0:T(8,128)(2,1)S(1)}, f32[136,256]{1,0:T(8,128)S(1)}) custom-call(bf16[32,256]{1,0:T(8,128)(2,1)S(1)} %collective-permute-done.ga_ref, bf16[32,256]{1,0:T(8,128)(2,1)S(1)} %collective-permute-done.1.gb_ref, bf16[256,256]{1,0:T(8,128)(2,1)S(1)} %get-tuple-element.23.hp_ref, ...), custom_call_target="tpu_custom_call" | custom-call | tf_op jit(solution)/shard_map/angle_stage/pallas_call | solution.py:255
  18.5 3.4 %all-to-all-start = ((bf16[4,64,320]{2,1,0:T(8,128)(2,1)}), bf16[4,64,320]{2,1,0:T(8,128)(2,1)S(1)}, u32[]{:S(2)}, u32[]{:S(2)}) async-start(bf16[4,64,320]{2,1,0:T(8,128)(2,1)} %bitcast.9), calls=%async_computation | async-start | bytes 393216 | tf_op jit(solution)/shard_map/all_to_all | solution.py:357
  21.8 9.5 %collective-permute-start.4 = (bf16[144,256]{1,0:T(8,128)(2,1)S(1)}, bf16[144,256]{1,0:T(8,128)(2,1)S(1)}, u32[]{:S(2)}, u32[]{:S(2)}) collective-permute-start(bf16[144,256]{1,0:T(8,128)(2,1)S(1)} %get-tuple-element.34), channel_id=1, source_target_pairs={{0,4},{4,0},{8,12},{12,8},{16,20},{20,16},{24,28},{28,24},{32,36},... | collective-permute-start | bytes 221192 | tf_op jit(solution)/shard_map/ppermute | solution.py:318
  31.4 0.0 all-to-all-done
  31.4 0.1 fusion.3
  31.5 6.3 %collective-permute-start.2 = (f32[64,32]{1,0:T(8,128)S(1)}, f32[64,32]{1,0:T(8,128)S(1)}, u32[]{:S(2)}, u32[]{:S(2)}) collective-permute-start(f32[64,32]{1,0:T(8,128)S(1)} %get-tuple-element.42), channel_id=1, source_target_pairs={{0,4},{4,0},{8,12},{12,8},{16,20},{20,16},{24,28},{28,24},{32,36},... | collective-permute-start | bytes 24584 | tf_op jit(solution)/shard_map/ppermute | solution.py:318
  37.8 1.9 %collective-permute-start.3 = (f32[64,32]{1,0:T(8,128)S(1)}, f32[64,32]{1,0:T(8,128)S(1)}, u32[]{:S(2)}, u32[]{:S(2)}) collective-permute-start(f32[64,32]{1,0:T(8,128)S(1)} %get-tuple-element.43), channel_id=1, source_target_pairs={{0,508},{4,8},{8,4},{12,16},{16,12},{20,24},{24,20},{28,32},{32,28... | collective-permute-start | bytes 24584 | tf_op jit(solution)/shard_map/ppermute | solution.py:322
  39.7 0.1 pad.1.clone
  39.8 0.0 collective-permute-done.4.recv_ref
  39.8 0.2 pair_stage.1
  40.0 0.7 %reshape.31 = bf16[64,2,384]{2,1,0:T(2,128)(2,1)} reshape(bf16[128,384]{1,0:T(8,128)(2,1)S(1)} %pair_stage.1) | data formatting | bytes 196608 | tf_op jit(solution)/shard_map/reshape | solution.py:359
  40.7 7.0 %all-to-all-start.1 = ((bf16[64,2,384]{2,1,0:T(2,128)(2,1)}), bf16[64,2,384]{2,1,0:T(2,128)(2,1)S(1)}, u32[]{:S(2)}, u32[]{:S(2)}) async-start(bf16[64,2,384]{2,1,0:T(2,128)(2,1)} %reshape.31), calls=%async_computation.1 | async-start | bytes 196608 | tf_op jit(solution)/shard_map/all_to_all | solution.py:360
  47.6 0.0 collective-permute-done.2
  47.6 0.0 collective-permute-done.3
  47.7 0.7 %fusion.2 = bf16[256,64]{0,1:T(8,128)(2,1)} fusion(f32[64,32]{1,0:T(8,128)S(1)} %get-tuple-element.45, f32[64,32]{1,0:T(8,128)S(1)} %get-tuple-element.44, f32[64,256]{1,0:T(8,128)S(1)} %get-tuple-element.30.cot_live_ref, f32[64,320]{1,0:T(8,128)S(1)} %convert_reduce_fusion, f32[256]{0:T(256)S(1)} %pad.1.clone), kind=kLoop, calls=%fused_computation.4 | loop fusion | flops 81920 | bytes 181248 | tf_op jit(solution)/shard_map/transpose | solution.py:371
  48.4 11.3 %all-to-all-done.1.slots_ref = bf16[64,2,384]{2,1,0:T(2,128)(2,1)S(1)} async-done(((bf16[64,2,384]{2,1,0:T(2,128)(2,1)}), bf16[64,2,384]{2,1,0:T(2,128)(2,1)S(1)}, u32[]{:S(2)}, u32[]{:S(2)}) %all-to-all-start.1) | async-done | bytes 98336 | tf_op jit(solution)/shard_map/all_to_all | solution.py:360
  59.6 0.7 %last_stage.1 = (f32[2,64]{1,0:T(2,128)}, f32[2,64]{1,0:T(2,128)}, f32[2,64]{1,0:T(2,128)}, f32[2,64]{1,0:T(2,128)}, f32[1,64]{1,0:T(1,128)}) custom-call(bf16[64,2,384]{2,1,0:T(2,128)(2,1)S(1)} %all-to-all-done.1.slots_ref), custom_call_target="tpu_custom_call" | custom-call | tf_op jit(solution)/shard_map/last_stage/pallas_call | solution.py:307
  (3 shorter events, 0.0 us)
Async XLA Ops:
  1.4 14.2 %collective-permute-start = (bf16[32,256]{1,0:T(8,128)(2,1)S(1)}, bf16[32,256]{1,0:T(8,128)(2,1)S(1)}, u32[]{:S(2)}, u32[]{:S(2)}) collective-permute-start(bf16[32,256]{1,0:T(8,128)(2,1)S(1)} %get-tuple-element.41), channel_id=1, source_target_pairs={{0,4},{4,0},{8,12},{12,8},{16,20},{20,16},{24,28},{28,24},{32,36},... | collective-permute-start | bytes 49160 | tf_op jit(solution)/shard_map/ppermute | solution.py:318
  10.1 5.5 %collective-permute-start.1 = (bf16[32,256]{1,0:T(8,128)(2,1)S(1)}, bf16[32,256]{1,0:T(8,128)(2,1)S(1)}, u32[]{:S(2)}, u32[]{:S(2)}) collective-permute-start(bf16[32,256]{1,0:T(8,128)(2,1)S(1)} %get-tuple-element.40), channel_id=1, source_target_pairs={{0,508},{4,8},{8,4},{12,16},{16,12},{20,24},{24,20},{28,32},{32,28... | collective-permute-start | bytes 49160 | tf_op jit(solution)/shard_map/ppermute | solution.py:322
  18.5 12.9 %all-to-all-start = ((bf16[4,64,320]{2,1,0:T(8,128)(2,1)}), bf16[4,64,320]{2,1,0:T(8,128)(2,1)S(1)}, u32[]{:S(2)}, u32[]{:S(2)}) async-start(bf16[4,64,320]{2,1,0:T(8,128)(2,1)} %bitcast.9), calls=%async_computation | async-start | bytes 393216 | tf_op jit(solution)/shard_map/all_to_all | solution.py:357
  21.8 18.0 %collective-permute-start.4 = (bf16[144,256]{1,0:T(8,128)(2,1)S(1)}, bf16[144,256]{1,0:T(8,128)(2,1)S(1)}, u32[]{:S(2)}, u32[]{:S(2)}) collective-permute-start(bf16[144,256]{1,0:T(8,128)(2,1)S(1)} %get-tuple-element.34), channel_id=1, source_target_pairs={{0,4},{4,0},{8,12},{12,8},{16,20},{20,16},{24,28},{28,24},{32,36},... | collective-permute-start | bytes 221192 | tf_op jit(solution)/shard_map/ppermute | solution.py:318
  31.5 16.1 %collective-permute-start.2 = (f32[64,32]{1,0:T(8,128)S(1)}, f32[64,32]{1,0:T(8,128)S(1)}, u32[]{:S(2)}, u32[]{:S(2)}) collective-permute-start(f32[64,32]{1,0:T(8,128)S(1)} %get-tuple-element.42), channel_id=1, source_target_pairs={{0,4},{4,0},{8,12},{12,8},{16,20},{20,16},{24,28},{28,24},{32,36},... | collective-permute-start | bytes 24584 | tf_op jit(solution)/shard_map/ppermute | solution.py:318
  37.8 9.8 %collective-permute-start.3 = (f32[64,32]{1,0:T(8,128)S(1)}, f32[64,32]{1,0:T(8,128)S(1)}, u32[]{:S(2)}, u32[]{:S(2)}) collective-permute-start(f32[64,32]{1,0:T(8,128)S(1)} %get-tuple-element.43), channel_id=1, source_target_pairs={{0,508},{4,8},{8,4},{12,16},{16,12},{20,24},{24,20},{28,32},{32,28... | collective-permute-start | bytes 24584 | tf_op jit(solution)/shard_map/ppermute | solution.py:322
  40.7 19.0 %all-to-all-start.1 = ((bf16[64,2,384]{2,1,0:T(2,128)(2,1)}), bf16[64,2,384]{2,1,0:T(2,128)(2,1)S(1)}, u32[]{:S(2)}, u32[]{:S(2)}) async-start(bf16[64,2,384]{2,1,0:T(2,128)(2,1)} %reshape.31), calls=%async_computation.1 | async-start | bytes 196608 | tf_op jit(solution)/shard_map/all_to_all | solution.py:360

commit v4 on v3

--- a/solution.py
+++ b/solution.py
@@ -8,7 +8,7 @@
 
 
 ARITY = 12
-CHUNK = 3
+CHUNK = 12
 GHOST = 32
 CAP = 256
 EXT = CAP + 2 * GHOST
@@ -58,13 +58,10 @@
         return jnp.concatenate([ref[pl.ds(t, 8, stride=3), :] for t in range(3)], axis=1)
 
     cos = grouped(cos_ref)
-    one = cos.astype(BF16)
-    rest = cos - one.astype(F32)
-    two = rest.astype(BF16)
-    three = (rest - two.astype(F32)).astype(BF16)
+    one, two = two_parts(cos)
     middle = EXT // 2
     src = (grouped(src_ref) - middle).astype(F32)
-    parts = jnp.concatenate([src, one.astype(F32), two.astype(F32), three.astype(F32)], axis=0).astype(BF16)
+    parts = jnp.concatenate([src, one.astype(F32), two.astype(F32), jnp.zeros((8, 384), F32)], axis=0).astype(BF16)
     spot = lax.broadcasted_iota(jnp.int32, (384, CAP), 0)
     start = (lax.broadcasted_iota(jnp.int32, (1, CAP), 1) & 31) * ARITY
     inside = (spot >= start) & (spot < start + ARITY)
@@ -73,19 +70,19 @@
     group = lax.broadcasted_iota(jnp.int32, (32, CAP), 0)
     wanted = lax.broadcasted_iota(jnp.int32, (32, CAP), 1) >> 5
     rows = []
-    for n in range(4):
+    for n in range(3):
         pick = (group == wanted + 8 * n).astype(F32).astype(BF16)
         spread = jnp.where(inside, dot(parts, pick, 0, 0), 0.0).astype(BF16)
         rows.append(dot(slot, spread))
-    return rows[0].astype(jnp.int32) + middle, rows[1] + rows[2] + rows[3]
+    return rows[0].astype(jnp.int32) + middle, rows[1] + rows[2]
 
 
 def prep_kernel(
-    odd_ref, count_hbm, src_hbm, cos_hbm, h_hbm, ws_hbm, wm_hbm, wt_hbm, wf_hbm, gate_w_hbm, cot_hbm,
-    hp_ref, w_ref, perm_ref, own_ref, hot_ref, part_ref, live_ref, cot_live_ref, cos_t_ref,
-    h_ref, gate_w_ref, cot_ref, count_ref, src_ref, cos_ref, sems,
+    odd_ref, count_ref, src_hbm, cos_hbm, h_hbm, ws_hbm, wm_hbm, wt_hbm, wf_hbm, gate_w_hbm, cot_hbm,
+    h_t_ref, w_ref, own_ref, hot_ref, part_ref, live_ref, cot_live_ref, cos_t_ref,
+    h_ref, gate_w_ref, cot_ref, src_ref, cos_ref, sems,
 ):
-    first = [pltpu.make_async_copy(src_hbm, src_ref, sems.at[8]), pltpu.make_async_copy(cos_hbm, cos_ref, sems.at[9])]
+    first = [pltpu.make_async_copy(src_hbm, src_ref, sems.at[7]), pltpu.make_async_copy(cos_hbm, cos_ref, sems.at[8])]
     copies = [
         pltpu.make_async_copy(ref, w_ref.at[pl.ds(64 * n, 64)], sems.at[n])
         for n, ref in enumerate((ws_hbm, wm_hbm, wt_hbm, wf_hbm))
@@ -93,18 +90,9 @@
     copies.append(pltpu.make_async_copy(h_hbm, h_ref, sems.at[4]))
     copies.append(pltpu.make_async_copy(gate_w_hbm, gate_w_ref, sems.at[5]))
     copies.append(pltpu.make_async_copy(cot_hbm, cot_ref, sems.at[6]))
-    copies.append(pltpu.make_async_copy(count_hbm, count_ref, sems.at[7]))
     for copy in first + copies:
         copy.start()
     odd = odd_ref[0]
-    rows = 256 // NDOM
-    m = lax.broadcasted_iota(jnp.int32, (256, 1), 0)
-    i = lax.broadcasted_iota(jnp.int32, (256, 256), 1)
-    half = jnp.where(m < 128, 1 - odd, odd)
-    m = m & 127
-    want = (m // rows) * (2 * rows) + rows * half + m % rows
-    perm = (i == want).astype(F32).astype(BF16)
-    perm_ref[...] = perm
     for copy in first:
         copy.wait()
     src, cos = by_slot(src_ref, cos_ref)
@@ -121,10 +109,6 @@
     near_id = lax.broadcasted_iota(jnp.int32, (CAP, CAP), 0).astype(F32).astype(BF16)
     far_id = lax.broadcasted_iota(jnp.int32, (2 * GHOST, CAP), 0).astype(F32).astype(BF16)
     one, zero = jnp.ones((), BF16), jnp.zeros((), BF16)
-    for k in range(ARITY):
-        at = slice(k * CAP, (k + 1) * CAP)
-        hot_ref[:CAP, at] = jnp.where(near_id == near_row[k : k + 1], one, zero)
-        hot_ref[CAP:, at] = jnp.where(far_id == far_row[k : k + 1], one, zero)
     for copy in copies:
         copy.wait()
     live = live_row(count_ref[0])
@@ -132,7 +116,7 @@
     cot_live_ref[...] = cot_ref[...].astype(F32) * live
     h_t = h_ref[...].T
     w_t = w_ref[...]
-    hp_ref[...] = dot(perm, h_t).astype(BF16)
+    h_t_ref[...] = h_t
     own = dot(w_t, h_t)
     own_ref[...] = own[128:]
     high, low = two_parts(own[:128])
@@ -140,7 +124,11 @@
     eye = lax.broadcasted_iota(jnp.int32, (64, 64), 0) == lax.broadcasted_iota(jnp.int32, (64, 64), 1)
     gate_w = jnp.sum(jnp.where(eye, gate_w_ref[...], 0.0), axis=1, keepdims=True)
     for k in range(ARITY):
-        picked = dot(table, hot_ref[:CAP, k * CAP : (k + 1) * CAP])
+        at = slice(k * CAP, (k + 1) * CAP)
+        hot = jnp.where(near_id == near_row[k : k + 1], one, zero)
+        hot_ref[:CAP, at] = hot
+        hot_ref[CAP:, at] = jnp.where(far_id == far_row[k : k + 1], one, zero)
+        picked = dot(table, hot)
         part_ref[k, 0:64] = picked[0:64] + picked[128:192] + (own[128:192] + gate_w * cos[k : k + 1])
         part_ref[k, 64:128] = picked[64:128] + picked[192:256]
 
@@ -150,7 +138,6 @@
         prep_kernel,
         out_shape=(
             stay((256, CAP), BF16),
-            stay((256, 256), BF16),
             stay((256, 256), BF16),
             stay((128, CAP), F32),
             stay((EXT, ARITY * CAP), BF16),
@@ -159,16 +146,15 @@
             stay((64, CAP), F32),
             stay((16, CAP), F32),
         ),
-        in_specs=[SMEM] + [HBM] * 10,
-        out_specs=(VMEM,) * 9,
+        in_specs=[SMEM, SMEM] + [HBM] * 9,
+        out_specs=(VMEM,) * 8,
         scratch_shapes=[
             pltpu.VMEM((CAP, 256), BF16),
             pltpu.VMEM((1, 64), F32),
             pltpu.VMEM((64, CAP), BF16),
-            pltpu.SMEM((1,), jnp.int32),
             pltpu.VMEM((24, 128), jnp.int32),
             pltpu.VMEM((24, 128), F32),
-            pltpu.SemaphoreType.DMA((10,)),
+            pltpu.SemaphoreType.DMA((9,)),
         ],
         compiler_params=pltpu.CompilerParams(vmem_limit_bytes=24 << 20),
         name="prep_stage",
@@ -176,15 +162,14 @@
 
 
 def angle_kernel(
-    ga_ref, gb_ref, hp_ref, w_ref, perm_ref, own_ref, hot_ref, part_ref, live_ref, cot_live_ref, cos_ref,
-    whole_ref, send_ref, keep_ref,
-    pick_ref, sig_ref, both_ref, bonds_ref, slope_ref,
+    ga_ref, gb_ref, w_ref, own_ref, hot_ref, part_ref, live_ref, cot_live_ref, cos_ref,
+    whole_ref, full_ref, edge_ref, dgw_ref,
+    pick_ref, sig_ref, bonds_ref, slope_ref,
 ):
     w_t = w_ref[...]
     gh_t = jnp.concatenate([ga_ref[...], gb_ref[...]], axis=0).T
     high, low = two_parts(dot(w_t[:128], gh_t))
     table = jnp.concatenate([high, low], axis=1)
-    gh_p = dot(perm_ref[...], gh_t).astype(BF16)
     for k in range(ARITY):
         far = hot_ref[CAP:, k * CAP : (k + 1) * CAP]
         pick_ref[k] = dot(table, jnp.concatenate([far, far], axis=0)) + part_ref[k]
@@ -213,64 +198,89 @@
     dq2, dgw = [zero, zero], [zero, zero]
     acc = jnp.zeros((EXT, 128), F32)
     for first in range(0, ARITY, CHUNK):
-        for n in (0, 1):
-            at = slice(n * 128, (n + 1) * 128)
-            live = live_ref[0:1, at]
-            dnum = slope_ref[0:64, at]
-            dden = slope_ref[64:128, at]
-            for k in range(first, first + CHUNK):
+        chunk = []
+        for k in range(first, first + CHUNK):
+            dpre, dmsg = [], []
+            for n in (0, 1):
+                at = slice(n * 128, (n + 1) * 128)
+                dnum = slope_ref[0:64, at]
                 sig = sig_ref[k, :, at]
-                gate = sig * live
-                dgate = dnum * pick_ref[k, 64:128, at] + dden
-                dpre = dgate * gate * (1.0 - sig)
-                dq2[n] += dpre
-                dgw[n] += dpre * cos_ref[k : k + 1, at]
-                lane = slice(k * CAP + at.start, k * CAP + at.stop)
-                both_ref[0:64, lane] = dpre.astype(BF16)
-                both_ref[64:128, lane] = (gate * dnum).astype(BF16)
-        lanes = slice(first * CAP, (first + CHUNK) * CAP)
-        acc += dot(hot_ref[:, lanes], both_ref[:, lanes], 1, 1)
-    dgw = jnp.concatenate(dgw, axis=1)
+                gate = sig * live_ref[0:1, at]
+                dgate = dnum * pick_ref[k, 64:128, at] + slope_ref[64:128, at]
+                change = dgate * gate * (1.0 - sig)
+                dq2[n] += change
+                dgw[n] += change * cos_ref[k : k + 1, at]
+                dpre.append(change.astype(BF16))
+                dmsg.append((gate * dnum).astype(BF16))
+            chunk.append(jnp.concatenate([jnp.concatenate(dpre, axis=1), jnp.concatenate(dmsg, axis=1)], axis=0))
+        acc += dot(hot_ref[:, first * CAP : (first + CHUNK) * CAP], jnp.concatenate(chunk, axis=1), 1, 1)
+    dgw_ref[...] = jnp.concatenate(dgw, axis=1)
     bonds_ref[0:64] = jnp.concatenate(dq2, axis=1).astype(BF16)
     edge = acc.astype(BF16)
-    bonds = bonds_ref[...].T
-    full = jnp.concatenate([edge[:CAP], bonds], axis=1)
+    full = jnp.concatenate([edge[:CAP], bonds_ref[...].T], axis=1)
     edge_far = edge[CAP:]
+    full_ref[...] = full
+    edge_ref[...] = edge_far
     whole_ref[:, :CAP] = dot(full, w_t).astype(BF16).T
     whole_ref[:, CAP:] = dot(edge_far, w_t[:128]).astype(BF16).T
-    grads = dot(hp_ref[...], full)
-    grads = jnp.concatenate([grads[:, :128] + dot(gh_p, edge_far), grads[:, 128:]], axis=1)
-    ones = jnp.ones((8, CAP), BF16)
-    dgw_high, dgw_low = two_parts(dgw)
-    gate = dot(ones, dgw_high, 1, 1) + dot(ones, dgw_low, 1, 1)
-    keep_ref[0:128] = grads[128:256]
-    keep_ref[128:136] = jnp.concatenate([gate, jnp.zeros((8, 192), F32)], axis=1)
-    send_ref[0:128] = grads[0:128].astype(BF16)
-    gate_high, gate_low = two_parts(gate)
-    row = jnp.concatenate([gate_high, gate_low, jnp.zeros((8, 128), BF16)], axis=1)
-    send_ref[128:144] = jnp.concatenate([row, row], axis=0)
-
-
-def angle_stage(ga, gb, prepared):
+
+
+def angle_stage(ga, gb, *prepared):
     return pl.pallas_call(
         angle_kernel,
         out_shape=(
             stay((256, EXT), BF16),
-            stay((144, 256), BF16),
-            stay((136, 256), F32),
+            stay((CAP, 256), BF16),
+            stay((2 * GHOST, 128), BF16),
+            stay((64, CAP), F32),
         ),
-        in_specs=[VMEM] * 11,
-        out_specs=(VMEM, VMEM, VMEM),
+        in_specs=[VMEM] * 9,
+        out_specs=(VMEM,) * 4,
         scratch_shapes=[
             pltpu.VMEM((ARITY, 128, CAP), F32),
             pltpu.VMEM((ARITY, 64, CAP), F32),
-            pltpu.VMEM((128, ARITY * CAP), BF16),
             pltpu.VMEM((128, CAP), BF16),
             pltpu.VMEM((128, CAP), F32),
         ],
         compiler_params=pltpu.CompilerParams(vmem_limit_bytes=24 << 20),
         name="angle_stage",
-    )(in_vmem(ga), in_vmem(gb), *prepared)
+    )(in_vmem(ga), in_vmem(gb), *(in_vmem(x) for x in prepared))
+
+
+def grads_kernel(odd_ref, ga_ref, gb_ref, h_t_ref, full_ref, edge_ref, dgw_ref, send_ref, keep_ref):
+    odd = odd_ref[0]
+    rows = 256 // NDOM
+    m = lax.broadcasted_iota(jnp.int32, (256, 1), 0)
+    i = lax.broadcasted_iota(jnp.int32, (256, 256), 1)
+    half = jnp.where(m < 128, 1 - odd, odd)
+    m = m & 127
+    want = (m // rows) * (2 * rows) + rows * half + m % rows
+    perm = (i == want).astype(F32).astype(BF16)
+    full = full_ref[...]
+    gh_t = jnp.concatenate([ga_ref[...], gb_ref[...]], axis=0).T
+    own = dot(h_t_ref[...], full)
+    own = jnp.concatenate([own[:, :128] + dot(gh_t, edge_ref[...]), own[:, 128:]], axis=1)
+    high, low = two_parts(own)
+    send_ref[0:128] = dot(perm[:128], high).astype(BF16)
+    keep_ref[0:128] = dot(perm[128:], high) + dot(perm[128:], low)
+    ones = jnp.ones((8, CAP), BF16)
+    dgw_high, dgw_low = two_parts(dgw_ref[...])
+    gate = dot(ones, dgw_high, 1, 1) + dot(ones, dgw_low, 1, 1)
+    keep_ref[128:136] = jnp.concatenate([gate, jnp.zeros((8, 192), F32)], axis=1)
+    gate_high, gate_low = two_parts(gate)
+    row = jnp.concatenate([gate_high, gate_low, jnp.zeros((8, 128), BF16)], axis=1)
+    send_ref[128:144] = jnp.concatenate([row, row], axis=0)
+
+
+def grads_stage(odd, ga, gb, *found):
+    return pl.pallas_call(
+        grads_kernel,
+        out_shape=(stay((144, 256), BF16), stay((136, 256), F32)),
+        in_specs=[SMEM] + [VMEM] * 6,
+        out_specs=(VMEM, VMEM),
+        compiler_params=pltpu.CompilerParams(vmem_limit_bytes=24 << 20),
+        name="grads_stage",
+    )(odd, in_vmem(ga), in_vmem(gb), *found)
 
 
 def pair_kernel(keep_ref, recv_ref, out_ref):
@@ -340,8 +350,9 @@
     to_b, to_a = jnp.where(is_odd, last, first), jnp.where(is_odd, first, last)
     ghost_b = swap_chip(to_b)
     ghost_a = swap_core(to_a)
-    prepared = prep_stage(
-        odd.reshape(1),
+    odd = odd.reshape(1)
+    h_t, *prepared = prep_stage(
+        odd,
         bond_count,
         source.reshape(24, 128),
         cosine.reshape(24, 128),
@@ -353,8 +364,9 @@
         gate_angle[None, :],
         cotangent.T,
     )
-    whole, send, keep = angle_stage(ghost_a, ghost_b, prepared)
+    whole, *found = angle_stage(ghost_a, ghost_b, *prepared)
     tiles = lax.all_to_all(whole.reshape(4, 64, EXT), "wa", 0, 0, tiled=True)
+    send, keep = grads_stage(odd, ghost_a, ghost_b, h_t, *found)
     recv = swap_core(send)
     slots = pair_stage(keep, recv).reshape(NDOM // 2, 256 // NDOM, 384)
     slots = lax.all_to_all(slots, CHIP, 0, 0, tiled=True)

time: 61 us -> 59.7 us (0.979)
    ppermute x3, starting transfers between devices: 24.6 us -> 23.9 us  [swap_core(): return lax.ppermute(x, DOM, [(i, i ^ 1) for i in range(NDOM)])]
    pallas_call x1, Pallas kernels: 2.86 us -> 2.23 us  [prep_stage(): pl.pallas_call(prep_kernel, out_shape=(stay((256, CAP), BF16), stay((256,...]
    pallas_call x1 -> x2, Pallas kernels: 2.88 us -> 3.02 us  [the longest x1 2.58 us: angle_stage(): pl.pallas_call(angle_kernel, out_shape=(stay((256, EXT), BF16), stay((CAP...]
  transfers between devices with their start and end apart: 7 -> 7, of which waited for: 1 -> 2; matrix products, arithmetic and copies ran while one was open for 3% -> 3% of each run, Pallas kernels for 5% -> 5%
where the time goes in v4:
time: 59.7 us; the launch traced here: 59.2 us
  starting transfers between devices  38.1 us (64%)
  waiting for transfers between devices  11.2 us (19%)
  Pallas kernels  6.15 us (10%)
  other arithmetic  1.48 us (2%)
  between operations  1.41 us (2%)
  local copies, waits for them, and re-layouts  0.82 us (1%)
    ppermute x3, starting transfers between devices, swap_core(): return lax.ppermute(x, DOM, [(i, i ^ 1) for i in range(NDOM)])  23.9 us
    all_to_all x1, waiting for transfers between devices, per_device(): slots = lax.all_to_all(slots, CHIP, 0, 0, tiled=True)  11 us
    all_to_all x1, starting transfers between devices, per_device(): slots = lax.all_to_all(slots, CHIP, 0, 0, tiled=True)  6.96 us
    ppermute x2, starting transfers between devices, swap_chip(): lax.ppermute(x, DOM, [(i, (i + 1) % NDOM if i % 2 else (i - 1) % NDOM) fo...  3.84 us
    all_to_all x1, starting transfers between devices, per_device(): tiles = lax.all_to_all(whole.reshape(4, 64, EXT), 'wa', 0, 0, tiled=True)  3.36 us
    pallas_call x1, Pallas kernels, angle_stage(): pl.pallas_call(angle_kernel, out_shape=(stay((256, EXT), BF16), stay((CAP...  2.58 us
    pallas_call x1, Pallas kernels, prep_stage(): pl.pallas_call(prep_kernel, out_shape=(stay((256, CAP), BF16), stay((256,...  2.23 us
  transfers between devices with their start and end apart: 7, of which 2 were waited for; matrix products, arithmetic and copies ran while one was open for 3% of the time, Pallas kernels for 5%

profile of v4, /device:TPU:1, one launch (start us, length us, event | category | flops | bytes accessed | tf_op | source)
XLA Modules:
  0.0 59.2 jit_solution(11495805009911371072)
XLA Ops:
  0.6 0.7 %broadcast_select_fusion.2 = (bf16[32,256]{1,0:T(8,128)(2,1)S(1)}, bf16[32,256]{1,0:T(8,128)(2,1)S(1)}) fusion(pred[]{:T(512)S(6)} %eq.3, bf16[256,256]{1,0:T(8,128)(2,1)} %h_hbm.1), kind=kLoop, calls=%fused_computation.7 | loop fusion | flops 16384 | bytes 65537 | tf_op jit(solution)/shard_map/jit(_where)/select_n | solution.py:350
  1.4 8.7 %collective-permute-start = (bf16[32,256]{1,0:T(8,128)(2,1)S(1)}, bf16[32,256]{1,0:T(8,128)(2,1)S(1)}, u32[]{:S(2)}, u32[]{:S(2)}) collective-permute-start(bf16[32,256]{1,0:T(8,128)(2,1)S(1)} %get-tuple-element.45), channel_id=1, source_target_pairs={{0,4},{4,0},{8,12},{12,8},{16,20},{20,16},{24,28},{28,24},{32,36},... | collective-permute-start | bytes 49160 | tf_op jit(solution)/shard_map/ppermute | solution.py:328
  10.1 1.9 %collective-permute-start.1 = (bf16[32,256]{1,0:T(8,128)(2,1)S(1)}, bf16[32,256]{1,0:T(8,128)(2,1)S(1)}, u32[]{:S(2)}, u32[]{:S(2)}) collective-permute-start(bf16[32,256]{1,0:T(8,128)(2,1)S(1)} %get-tuple-element.44), channel_id=1, source_target_pairs={{0,508},{4,8},{8,4},{12,16},{16,12},{20,24},{24,20},{28,32},{32,28... | collective-permute-start | bytes 49160 | tf_op jit(solution)/shard_map/ppermute | solution.py:332
  12.7 2.2 %prep_stage.1 = (bf16[256,256]{1,0:T(8,128)(2,1)S(1)}, bf16[256,256]{1,0:T(8,128)(2,1)S(1)}, f32[128,256]{1,0:T(8,128)S(1)}, bf16[320,3072]{1,0:T(8,128)(2,1)S(1...) custom-call(s32[1]{0:T(128)} %bitcast.odd_ref, ...), custom_call_target="tpu_custom_call" | custom-call | tf_op jit(solution)/shard_map/prep_stage/pallas_call | solution.py:137
  14.9 0.0 collective-permute-done.ga_ref
  15.0 0.2 collective-permute-done.1.gb_ref
  15.2 2.6 %angle_stage.1 = (bf16[256,320]{1,0:T(8,128)(2,1)}, bf16[256,256]{1,0:T(8,128)(2,1)S(1)}, bf16[64,128]{1,0:T(8,128)(2,1)S(1)}, f32[64,256]{1,0:T(8,128)S(1)}) custom-call(bf16[32,256]{1,0:T(8,128)(2,1)S(1)} %collective-permute-done.ga_ref, bf16[32,256]{1,0:T(8,128)(2,1)S(1)} %collective-permute-done.1.gb_ref, bf16[256,256]{1,0:T(8,128)(2,1)S(1)} %get-tuple-element.25.w_ref, ...), custom_call_target="tpu_custom_call" | custom-call | tf_op jit(solution)/shard_map/angle_stage/pallas_call | solution.py:229
  17.8 3.4 %all-to-all-start = ((bf16[4,64,320]{2,1,0:T(8,128)(2,1)}), bf16[4,64,320]{2,1,0:T(8,128)(2,1)S(1)}, u32[]{:S(2)}, u32[]{:S(2)}) async-start(bf16[4,64,320]{2,1,0:T(8,128)(2,1)} %bitcast.9), calls=%async_computation | async-start | bytes 393216 | tf_op jit(solution)/shard_map/all_to_all | solution.py:368
  21.1 0.4 grads_stage.1
  21.6 9.3 %collective-permute-start.4 = (bf16[144,256]{1,0:T(8,128)(2,1)S(1)}, bf16[144,256]{1,0:T(8,128)(2,1)S(1)}, u32[]{:S(2)}, u32[]{:S(2)}) collective-permute-start(bf16[144,256]{1,0:T(8,128)(2,1)S(1)} %get-tuple-element.38), channel_id=1, source_target_pairs={{0,4},{4,0},{8,12},{12,8},{16,20},{20,16},{24,28},{28,24},{32,36},... | collective-permute-start | bytes 221192 | tf_op jit(solution)/shard_map/ppermute | solution.py:328
  30.9 0.0 all-to-all-done
  30.9 0.1 fusion.3
  31.0 5.9 %collective-permute-start.2 = (f32[64,32]{1,0:T(8,128)S(1)}, f32[64,32]{1,0:T(8,128)S(1)}, u32[]{:S(2)}, u32[]{:S(2)}) collective-permute-start(f32[64,32]{1,0:T(8,128)S(1)} %get-tuple-element.46), channel_id=1, source_target_pairs={{0,4},{4,0},{8,12},{12,8},{16,20},{20,16},{24,28},{28,24},{32,36},... | collective-permute-start | bytes 24584 | tf_op jit(solution)/shard_map/ppermute | solution.py:328
  36.9 1.9 %collective-permute-start.3 = (f32[64,32]{1,0:T(8,128)S(1)}, f32[64,32]{1,0:T(8,128)S(1)}, u32[]{:S(2)}, u32[]{:S(2)}) collective-permute-start(f32[64,32]{1,0:T(8,128)S(1)} %get-tuple-element.47), channel_id=1, source_target_pairs={{0,508},{4,8},{8,4},{12,16},{16,12},{20,24},{24,20},{28,32},{32,28... | collective-permute-start | bytes 24584 | tf_op jit(solution)/shard_map/ppermute | solution.py:332
  38.8 0.1 pad.1.clone
  38.9 0.0 collective-permute-done.4.recv_ref
  38.9 0.2 pair_stage.1
  39.0 0.7 %reshape.31 = bf16[64,2,384]{2,1,0:T(2,128)(2,1)} reshape(bf16[128,384]{1,0:T(8,128)(2,1)S(1)} %pair_stage.1) | data formatting | bytes 196608 | tf_op jit(solution)/shard_map/reshape | solution.py:371
  39.7 7.0 %all-to-all-start.1 = ((bf16[64,2,384]{2,1,0:T(2,128)(2,1)}), bf16[64,2,384]{2,1,0:T(2,128)(2,1)S(1)}, u32[]{:S(2)}, u32[]{:S(2)}) async-start(bf16[64,2,384]{2,1,0:T(2,128)(2,1)} %reshape.31), calls=%async_computation.1 | async-start | bytes 196608 | tf_op jit(solution)/shard_map/all_to_all | solution.py:372
  46.7 0.0 collective-permute-done.2
  46.7 0.0 collective-permute-done.3
  46.7 0.7 %fusion.2 = bf16[256,64]{0,1:T(8,128)(2,1)} fusion(f32[64,32]{1,0:T(8,128)S(1)} %get-tuple-element.49, f32[64,32]{1,0:T(8,128)S(1)} %get-tuple-element.48, f32[64,256]{1,0:T(8,128)S(1)} %get-tuple-element.30.cot_live_ref, f32[64,320]{1,0:T(8,128)S(1)} %convert_reduce_fusion, f32[256]{0:T(256)S(1)} %pad.1.clone), kind=kLoop, calls=%fused_computation.4 | loop fusion | flops 81920 | bytes 181248 | tf_op jit(solution)/shard_map/transpose | solution.py:383
  47.4 11.0 %all-to-all-done.1.slots_ref = bf16[64,2,384]{2,1,0:T(2,128)(2,1)S(1)} async-done(((bf16[64,2,384]{2,1,0:T(2,128)(2,1)}), bf16[64,2,384]{2,1,0:T(2,128)(2,1)S(1)}, u32[]{:S(2)}, u32[]{:S(2)}) %all-to-all-start.1) | async-done | bytes 98336 | tf_op jit(solution)/shard_map/all_to_all | solution.py:372
  58.4 0.7 %last_stage.1 = (f32[2,64]{1,0:T(2,128)}, f32[2,64]{1,0:T(2,128)}, f32[2,64]{1,0:T(2,128)}, f32[2,64]{1,0:T(2,128)}, f32[1,64]{1,0:T(1,128)}) custom-call(bf16[64,2,384]{2,1,0:T(2,128)(2,1)S(1)} %all-to-all-done.1.slots_ref), custom_call_target="tpu_custom_call" | custom-call | tf_op jit(solution)/shard_map/last_stage/pallas_call | solution.py:317
  (3 shorter events, 0.0 us)
Async XLA Ops:
  1.4 13.6 %collective-permute-start = (bf16[32,256]{1,0:T(8,128)(2,1)S(1)}, bf16[32,256]{1,0:T(8,128)(2,1)S(1)}, u32[]{:S(2)}, u32[]{:S(2)}) collective-permute-start(bf16[32,256]{1,0:T(8,128)(2,1)S(1)} %get-tuple-element.45), channel_id=1, source_target_pairs={{0,4},{4,0},{8,12},{12,8},{16,20},{20,16},{24,28},{28,24},{32,36},... | collective-permute-start | bytes 49160 | tf_op jit(solution)/shard_map/ppermute | solution.py:328
  10.1 5.1 %collective-permute-start.1 = (bf16[32,256]{1,0:T(8,128)(2,1)S(1)}, bf16[32,256]{1,0:T(8,128)(2,1)S(1)}, u32[]{:S(2)}, u32[]{:S(2)}) collective-permute-start(bf16[32,256]{1,0:T(8,128)(2,1)S(1)} %get-tuple-element.44), channel_id=1, source_target_pairs={{0,508},{4,8},{8,4},{12,16},{16,12},{20,24},{24,20},{28,32},{32,28... | collective-permute-start | bytes 49160 | tf_op jit(solution)/shard_map/ppermute | solution.py:332
  17.8 13.1 %all-to-all-start = ((bf16[4,64,320]{2,1,0:T(8,128)(2,1)}), bf16[4,64,320]{2,1,0:T(8,128)(2,1)S(1)}, u32[]{:S(2)}, u32[]{:S(2)}) async-start(bf16[4,64,320]{2,1,0:T(8,128)(2,1)} %bitcast.9), calls=%async_computation | async-start | bytes 393216 | tf_op jit(solution)/shard_map/all_to_all | solution.py:368
  21.6 17.3 %collective-permute-start.4 = (bf16[144,256]{1,0:T(8,128)(2,1)S(1)}, bf16[144,256]{1,0:T(8,128)(2,1)S(1)}, u32[]{:S(2)}, u32[]{:S(2)}) collective-permute-start(bf16[144,256]{1,0:T(8,128)(2,1)S(1)} %get-tuple-element.38), channel_id=1, source_target_pairs={{0,4},{4,0},{8,12},{12,8},{16,20},{20,16},{24,28},{28,24},{32,36},... | collective-permute-start | bytes 221192 | tf_op jit(solution)/shard_map/ppermute | solution.py:328
  31.0 15.7 %collective-permute-start.2 = (f32[64,32]{1,0:T(8,128)S(1)}, f32[64,32]{1,0:T(8,128)S(1)}, u32[]{:S(2)}, u32[]{:S(2)}) collective-permute-start(f32[64,32]{1,0:T(8,128)S(1)} %get-tuple-element.46), channel_id=1, source_target_pairs={{0,4},{4,0},{8,12},{12,8},{16,20},{20,16},{24,28},{28,24},{32,36},... | collective-permute-start | bytes 24584 | tf_op jit(solution)/shard_map/ppermute | solution.py:328
  36.9 9.8 %collective-permute-start.3 = (f32[64,32]{1,0:T(8,128)S(1)}, f32[64,32]{1,0:T(8,128)S(1)}, u32[]{:S(2)}, u32[]{:S(2)}) collective-permute-start(f32[64,32]{1,0:T(8,128)S(1)} %get-tuple-element.47), channel_id=1, source_target_pairs={{0,508},{4,8},{8,4},{12,16},{16,12},{20,24},{24,20},{28,32},{32,28... | collective-permute-start | bytes 24584 | tf_op jit(solution)/shard_map/ppermute | solution.py:332
  39.7 18.7 %all-to-all-start.1 = ((bf16[64,2,384]{2,1,0:T(2,128)(2,1)}), bf16[64,2,384]{2,1,0:T(2,128)(2,1)S(1)}, u32[]{:S(2)}, u32[]{:S(2)}) async-start(bf16[64,2,384]{2,1,0:T(2,128)(2,1)} %reshape.31), calls=%async_computation.1 | async-start | bytes 196608 | tf_op jit(solution)/shard_map/all_to_all | solution.py:372

commit v5 on v4

--- a/solution.py
+++ b/solution.py
@@ -93,7 +93,7 @@
     for copy in first + copies:
         copy.start()
     odd = odd_ref[0]
-    for copy in first:
+    for copy in first + copies:
         copy.wait()
     src, cos = by_slot(src_ref, cos_ref)
     cos_t_ref[...] = cos
@@ -109,8 +109,6 @@
     near_id = lax.broadcasted_iota(jnp.int32, (CAP, CAP), 0).astype(F32).astype(BF16)
     far_id = lax.broadcasted_iota(jnp.int32, (2 * GHOST, CAP), 0).astype(F32).astype(BF16)
     one, zero = jnp.ones((), BF16), jnp.zeros((), BF16)
-    for copy in copies:
-        copy.wait()
     live = live_row(count_ref[0])
     live_ref[...] = jnp.broadcast_to(live, (8, CAP))
     cot_live_ref[...] = cot_ref[...].astype(F32) * live
@@ -284,17 +282,18 @@
 
 
 def pair_kernel(keep_ref, recv_ref, out_ref):
-    out_ref[:, :256] = (keep_ref[0:128] + recv_ref[0:128].astype(F32)).astype(BF16)
     row = recv_ref[128:144].astype(F32)[0:8]
     gate = keep_ref[128:136][:, 0:64] + row[:, 0:64] + row[:, 64:128]
     high, low = two_parts(gate)
-    out_ref[:, 256:] = jnp.broadcast_to(jnp.concatenate([high, low], axis=1)[0:1], (128, 128))
+    tail = jnp.broadcast_to(jnp.concatenate([high, low], axis=1)[0:1], (128, 128))
+    total = (keep_ref[0:128] + recv_ref[0:128].astype(F32)).astype(BF16)
+    out_ref[...] = jnp.concatenate([total, tail], axis=1).reshape(out_ref.shape)
 
 
 def pair_stage(keep, recv):
     return pl.pallas_call(
         pair_kernel,
-        out_shape=jax.ShapeDtypeStruct((128, 384), BF16),
+        out_shape=stay((NDOM // 2, 256 // NDOM, 384), BF16),
         in_specs=[VMEM, VMEM],
         out_specs=VMEM,
         compiler_params=pltpu.CompilerParams(vmem_limit_bytes=24 << 20),
@@ -368,7 +367,7 @@
     tiles = lax.all_to_all(whole.reshape(4, 64, EXT), "wa", 0, 0, tiled=True)
     send, keep = grads_stage(odd, ghost_a, ghost_b, h_t, *found)
     recv = swap_core(send)
-    slots = pair_stage(keep, recv).reshape(NDOM // 2, 256 // NDOM, 384)
+    slots = pair_stage(keep, recv)
     slots = lax.all_to_all(slots, CHIP, 0, 0, tiled=True)
     summed = tiles.astype(F32).sum(axis=0)
     to_a, to_b = summed[:, CAP : CAP + GHOST], summed[:, CAP + GHOST :]

time: 59.7 us -> 59.9 us (level)
  Pallas kernels: 6.15 us -> 6.88 us
  local copies, waits for them, and re-layouts: 0.82 us -> 0.15 us
    reshape x1 -> x0, local copies, waits for them, and re-layouts: 0.67 us -> none  [per_device(): slots = pair_stage(keep, recv).reshape(NDOM // 2, 256 // NDOM, 384)]
    pallas_call x1, Pallas kernels: 0.15 us -> 0.79 us  [pair_stage(): pl.pallas_call(pair_kernel, out_shape=stay((NDOM // 2, 256 // NDOM, 384),...]
  transfers between devices with their start and end apart: 7 -> 7, of which waited for: 2 -> 2; matrix products, arithmetic and copies ran while one was open for 3% -> 2% of each run, Pallas kernels for 5% -> 6%
where the time goes in v5:
time: 59.9 us; the launch traced here: 59.4 us
  starting transfers between devices  38.2 us (64%)
  waiting for transfers between devices  11.3 us (19%)
  Pallas kernels  6.88 us (11%)
  other arithmetic  1.49 us (2%)
  between operations  1.41 us (2%)
    ppermute x3, starting transfers between devices, swap_core(): return lax.ppermute(x, DOM, [(i, i ^ 1) for i in range(NDOM)])  24 us
    all_to_all x1, waiting for transfers between devices, per_device(): slots = lax.all_to_all(slots, CHIP, 0, 0, tiled=True)  11.1 us
    all_to_all x1, starting transfers between devices, per_device(): slots = lax.all_to_all(slots, CHIP, 0, 0, tiled=True)  6.96 us
    ppermute x2, starting transfers between devices, swap_chip(): lax.ppermute(x, DOM, [(i, (i + 1) % NDOM if i % 2 else (i - 1) % NDOM) fo...  3.84 us
    all_to_all x1, starting transfers between devices, per_device(): tiles = lax.all_to_all(whole.reshape(4, 64, EXT), 'wa', 0, 0, tiled=True)  3.36 us
    pallas_call x1, Pallas kernels, angle_stage(): pl.pallas_call(angle_kernel, out_shape=(stay((256, EXT), BF16), stay((CAP...  2.58 us
    pallas_call x1, Pallas kernels, prep_stage(): pl.pallas_call(prep_kernel, out_shape=(stay((256, CAP), BF16), stay((256,...  2.33 us
  transfers between devices with their start and end apart: 7, of which 2 were waited for; matrix products, arithmetic and copies ran while one was open for 2% of the time, Pallas kernels for 6%

profile of v5, /device:TPU:1, one launch (start us, length us, event | category | flops | bytes accessed | tf_op | source)
XLA Modules:
  0.0 59.4 jit_solution(9787189231697395936)
XLA Ops:
  0.6 0.7 %broadcast_select_fusion.2 = (bf16[32,256]{1,0:T(8,128)(2,1)S(1)}, bf16[32,256]{1,0:T(8,128)(2,1)S(1)}) fusion(pred[]{:T(512)S(6)} %eq.3, bf16[256,256]{1,0:T(8,128)(2,1)} %h_hbm.1), kind=kLoop, calls=%fused_computation.7 | loop fusion | flops 16384 | bytes 65537 | tf_op jit(solution)/shard_map/jit(_where)/select_n | solution.py:349
  1.4 8.7 %collective-permute-start = (bf16[32,256]{1,0:T(8,128)(2,1)S(1)}, bf16[32,256]{1,0:T(8,128)(2,1)S(1)}, u32[]{:S(2)}, u32[]{:S(2)}) collective-permute-start(bf16[32,256]{1,0:T(8,128)(2,1)S(1)} %get-tuple-element.45), channel_id=1, source_target_pairs={{0,4},{4,0},{8,12},{12,8},{16,20},{20,16},{24,28},{28,24},{32,36},... | collective-permute-start | bytes 49160 | tf_op jit(solution)/shard_map/ppermute | solution.py:327
  10.1 1.9 %collective-permute-start.1 = (bf16[32,256]{1,0:T(8,128)(2,1)S(1)}, bf16[32,256]{1,0:T(8,128)(2,1)S(1)}, u32[]{:S(2)}, u32[]{:S(2)}) collective-permute-start(bf16[32,256]{1,0:T(8,128)(2,1)S(1)} %get-tuple-element.44), channel_id=1, source_target_pairs={{0,508},{4,8},{8,4},{12,16},{16,12},{20,24},{24,20},{28,32},{32,28... | collective-permute-start | bytes 49160 | tf_op jit(solution)/shard_map/ppermute | solution.py:331
  12.7 2.3 %prep_stage.1 = (bf16[256,256]{1,0:T(8,128)(2,1)S(1)}, bf16[256,256]{1,0:T(8,128)(2,1)S(1)}, f32[128,256]{1,0:T(8,128)S(1)}, bf16[320,3072]{1,0:T(8,128)(2,1)S(1...) custom-call(s32[1]{0:T(128)} %bitcast.odd_ref, ...), custom_call_target="tpu_custom_call" | custom-call | tf_op jit(solution)/shard_map/prep_stage/pallas_call | solution.py:135
  15.0 0.0 collective-permute-done.ga_ref
  15.0 0.1 collective-permute-done.1.gb_ref
  15.2 2.6 %angle_stage.1 = (bf16[256,320]{1,0:T(8,128)(2,1)}, bf16[256,256]{1,0:T(8,128)(2,1)S(1)}, bf16[64,128]{1,0:T(8,128)(2,1)S(1)}, f32[64,256]{1,0:T(8,128)S(1)}) custom-call(bf16[32,256]{1,0:T(8,128)(2,1)S(1)} %collective-permute-done.ga_ref, bf16[32,256]{1,0:T(8,128)(2,1)S(1)} %collective-permute-done.1.gb_ref, bf16[256,256]{1,0:T(8,128)(2,1)S(1)} %get-tuple-element.25.w_ref, ...), custom_call_target="tpu_custom_call" | custom-call | tf_op jit(solution)/shard_map/angle_stage/pallas_call | solution.py:227
  17.8 3.4 %all-to-all-start = ((bf16[4,64,320]{2,1,0:T(8,128)(2,1)}), bf16[4,64,320]{2,1,0:T(8,128)(2,1)S(1)}, u32[]{:S(2)}, u32[]{:S(2)}) async-start(bf16[4,64,320]{2,1,0:T(8,128)(2,1)} %bitcast.9), calls=%async_computation | async-start | bytes 393216 | tf_op jit(solution)/shard_map/all_to_all | solution.py:367
  21.1 0.4 grads_stage.1
  21.6 9.4 %collective-permute-start.4 = (bf16[144,256]{1,0:T(8,128)(2,1)S(1)}, bf16[144,256]{1,0:T(8,128)(2,1)S(1)}, u32[]{:S(2)}, u32[]{:S(2)}) collective-permute-start(bf16[144,256]{1,0:T(8,128)(2,1)S(1)} %get-tuple-element.38), channel_id=1, source_target_pairs={{0,4},{4,0},{8,12},{12,8},{16,20},{20,16},{24,28},{28,24},{32,36},... | collective-permute-start | bytes 221192 | tf_op jit(solution)/shard_map/ppermute | solution.py:327
  31.0 0.0 all-to-all-done
  31.0 0.1 fusion.3
  31.1 5.9 %collective-permute-start.2 = (f32[64,32]{1,0:T(8,128)S(1)}, f32[64,32]{1,0:T(8,128)S(1)}, u32[]{:S(2)}, u32[]{:S(2)}) collective-permute-start(f32[64,32]{1,0:T(8,128)S(1)} %get-tuple-element.46), channel_id=1, source_target_pairs={{0,4},{4,0},{8,12},{12,8},{16,20},{20,16},{24,28},{28,24},{32,36},... | collective-permute-start | bytes 24584 | tf_op jit(solution)/shard_map/ppermute | solution.py:327
  37.0 1.9 %collective-permute-start.3 = (f32[64,32]{1,0:T(8,128)S(1)}, f32[64,32]{1,0:T(8,128)S(1)}, u32[]{:S(2)}, u32[]{:S(2)}) collective-permute-start(f32[64,32]{1,0:T(8,128)S(1)} %get-tuple-element.47), channel_id=1, source_target_pairs={{0,508},{4,8},{8,4},{12,16},{16,12},{20,24},{24,20},{28,32},{32,28... | collective-permute-start | bytes 24584 | tf_op jit(solution)/shard_map/ppermute | solution.py:331
  38.9 0.1 pad.1.clone
  39.0 0.0 collective-permute-done.4.recv_ref
  39.0 0.8 %pair_stage.1 = bf16[64,2,384]{2,1,0:T(2,128)(2,1)} custom-call(f32[136,256]{1,0:T(8,128)S(1)} %get-tuple-element.37.keep_ref, bf16[144,256]{1,0:T(8,128)(2,1)S(1)} %collective-permute-done.4.recv_ref), custom_call_target="tpu_custom_call" | custom-call | tf_op jit(solution)/shard_map/pair_stage/pallas_call | solution.py:294
  39.8 7.0 %all-to-all-start.1 = ((bf16[64,2,384]{2,1,0:T(2,128)(2,1)}), bf16[64,2,384]{2,1,0:T(2,128)(2,1)S(1)}, u32[]{:S(2)}, u32[]{:S(2)}) async-start(bf16[64,2,384]{2,1,0:T(2,128)(2,1)} %pair_stage.1), calls=%async_computation.1 | async-start | bytes 196608 | tf_op jit(solution)/shard_map/all_to_all | solution.py:371
  46.8 0.0 collective-permute-done.2
  46.8 0.0 collective-permute-done.3
  46.8 0.7 %fusion.2 = bf16[256,64]{0,1:T(8,128)(2,1)} fusion(f32[64,32]{1,0:T(8,128)S(1)} %get-tuple-element.49, f32[64,32]{1,0:T(8,128)S(1)} %get-tuple-element.48, f32[64,256]{1,0:T(8,128)S(1)} %get-tuple-element.30.cot_live_ref, f32[64,320]{1,0:T(8,128)S(1)} %convert_reduce_fusion, f32[256]{0:T(256)S(1)} %pad.1.clone), kind=kLoop, calls=%fused_computation.4 | loop fusion | flops 81920 | bytes 181248 | tf_op jit(solution)/shard_map/transpose | solution.py:382
  47.5 11.1 %all-to-all-done.1.slots_ref = bf16[64,2,384]{2,1,0:T(2,128)(2,1)S(1)} async-done(((bf16[64,2,384]{2,1,0:T(2,128)(2,1)}), bf16[64,2,384]{2,1,0:T(2,128)(2,1)S(1)}, u32[]{:S(2)}, u32[]{:S(2)}) %all-to-all-start.1) | async-done | bytes 98336 | tf_op jit(solution)/shard_map/all_to_all | solution.py:371
  58.6 0.7 %last_stage.1 = (f32[2,64]{1,0:T(2,128)}, f32[2,64]{1,0:T(2,128)}, f32[2,64]{1,0:T(2,128)}, f32[2,64]{1,0:T(2,128)}, f32[1,64]{1,0:T(1,128)}) custom-call(bf16[64,2,384]{2,1,0:T(2,128)(2,1)S(1)} %all-to-all-done.1.slots_ref), custom_call_target="tpu_custom_call" | custom-call | tf_op jit(solution)/shard_map/last_stage/pallas_call | solution.py:316
  (3 shorter events, 0.0 us)
Async XLA Ops:
  1.4 13.7 %collective-permute-start = (bf16[32,256]{1,0:T(8,128)(2,1)S(1)}, bf16[32,256]{1,0:T(8,128)(2,1)S(1)}, u32[]{:S(2)}, u32[]{:S(2)}) collective-permute-start(bf16[32,256]{1,0:T(8,128)(2,1)S(1)} %get-tuple-element.45), channel_id=1, source_target_pairs={{0,4},{4,0},{8,12},{12,8},{16,20},{20,16},{24,28},{28,24},{32,36},... | collective-permute-start | bytes 49160 | tf_op jit(solution)/shard_map/ppermute | solution.py:327
  10.1 5.1 %collective-permute-start.1 = (bf16[32,256]{1,0:T(8,128)(2,1)S(1)}, bf16[32,256]{1,0:T(8,128)(2,1)S(1)}, u32[]{:S(2)}, u32[]{:S(2)}) collective-permute-start(bf16[32,256]{1,0:T(8,128)(2,1)S(1)} %get-tuple-element.44), channel_id=1, source_target_pairs={{0,508},{4,8},{8,4},{12,16},{16,12},{20,24},{24,20},{28,32},{32,28... | collective-permute-start | bytes 49160 | tf_op jit(solution)/shard_map/ppermute | solution.py:331
  17.8 13.2 %all-to-all-start = ((bf16[4,64,320]{2,1,0:T(8,128)(2,1)}), bf16[4,64,320]{2,1,0:T(8,128)(2,1)S(1)}, u32[]{:S(2)}, u32[]{:S(2)}) async-start(bf16[4,64,320]{2,1,0:T(8,128)(2,1)} %bitcast.9), calls=%async_computation | async-start | bytes 393216 | tf_op jit(solution)/shard_map/all_to_all | solution.py:367
  21.6 17.4 %collective-permute-start.4 = (bf16[144,256]{1,0:T(8,128)(2,1)S(1)}, bf16[144,256]{1,0:T(8,128)(2,1)S(1)}, u32[]{:S(2)}, u32[]{:S(2)}) collective-permute-start(bf16[144,256]{1,0:T(8,128)(2,1)S(1)} %get-tuple-element.38), channel_id=1, source_target_pairs={{0,4},{4,0},{8,12},{12,8},{16,20},{20,16},{24,28},{28,24},{32,36},... | collective-permute-start | bytes 221192 | tf_op jit(solution)/shard_map/ppermute | solution.py:327
  31.1 15.6 %collective-permute-start.2 = (f32[64,32]{1,0:T(8,128)S(1)}, f32[64,32]{1,0:T(8,128)S(1)}, u32[]{:S(2)}, u32[]{:S(2)}) collective-permute-start(f32[64,32]{1,0:T(8,128)S(1)} %get-tuple-element.46), channel_id=1, source_target_pairs={{0,4},{4,0},{8,12},{12,8},{16,20},{20,16},{24,28},{28,24},{32,36},... | collective-permute-start | bytes 24584 | tf_op jit(solution)/shard_map/ppermute | solution.py:327
  37.0 9.8 %collective-permute-start.3 = (f32[64,32]{1,0:T(8,128)S(1)}, f32[64,32]{1,0:T(8,128)S(1)}, u32[]{:S(2)}, u32[]{:S(2)}) collective-permute-start(f32[64,32]{1,0:T(8,128)S(1)} %get-tuple-element.47), channel_id=1, source_target_pairs={{0,508},{4,8},{8,4},{12,16},{16,12},{20,24},{24,20},{28,32},{32,28... | collective-permute-start | bytes 24584 | tf_op jit(solution)/shard_map/ppermute | solution.py:331
  39.8 18.8 %all-to-all-start.1 = ((bf16[64,2,384]{2,1,0:T(2,128)(2,1)}), bf16[64,2,384]{2,1,0:T(2,128)(2,1)S(1)}, u32[]{:S(2)}, u32[]{:S(2)}) async-start(bf16[64,2,384]{2,1,0:T(2,128)(2,1)} %pair_stage.1), calls=%async_computation.1 | async-start | bytes 196608 | tf_op jit(solution)/shard_map/all_to_all | solution.py:371

commit v6 on v4

--- a/solution.py
+++ b/solution.py
@@ -51,6 +51,53 @@
 def live_row(count):
     bond = lax.broadcasted_iota(jnp.int32, (1, CAP), 1)
     return ((bond < count - GHOST) | (bond >= CAP - GHOST)).astype(F32)
+
+
+def front_kernel(
+    odd_ref, src_hbm, cos_hbm, h_hbm, ws_hbm, wm_hbm, wt_hbm, wf_hbm, gate_w_hbm, cot_hbm,
+    to_a_ref, to_b_ref, src_ref, cos_ref, h_ref, w_ref, gate_w_ref, cot_ref,
+    sems,
+):
+    odd = odd_ref[0]
+    at_a = pl.multiple_of((1 - odd) * (CAP - GHOST), GHOST)
+    at_b = pl.multiple_of(odd * (CAP - GHOST), GHOST)
+    pairs = [
+        (h_hbm.at[pl.ds(at_b, GHOST)], to_b_ref),
+        (h_hbm.at[pl.ds(at_a, GHOST)], to_a_ref),
+        (src_hbm, src_ref),
+        (cos_hbm, cos_ref),
+        (h_hbm, h_ref),
+        (gate_w_hbm, gate_w_ref),
+        (cot_hbm, cot_ref),
+    ]
+    for n, ref in enumerate((ws_hbm, wm_hbm, wt_hbm, wf_hbm)):
+        pairs.append((ref, w_ref.at[pl.ds(64 * n, 64)]))
+    copies = [pltpu.make_async_copy(a, b, sems.at[n]) for n, (a, b) in enumerate(pairs)]
+    for copy in copies:
+        copy.start()
+    for copy in copies:
+        copy.wait()
+
+
+def front_stage(odd, *held):
+    return pl.pallas_call(
+        front_kernel,
+        out_shape=(
+            stay((GHOST, 256), BF16),
+            stay((GHOST, 256), BF16),
+            stay((24, 128), jnp.int32),
+            stay((24, 128), F32),
+            stay((CAP, 256), BF16),
+            stay((256, 256), BF16),
+            stay((1, 64), F32),
+            stay((64, CAP), BF16),
+        ),
+        in_specs=[SMEM] + [HBM] * 9,
+        out_specs=(VMEM,) * 8,
+        scratch_shapes=[pltpu.SemaphoreType.DMA((11,))],
+        compiler_params=pltpu.CompilerParams(vmem_limit_bytes=24 << 20),
+        name="front_stage",
+    )(odd, *(in_hbm(x) for x in held))
 
 
 def by_slot(src_ref, cos_ref):
@@ -78,23 +125,10 @@
 
 
 def prep_kernel(
-    odd_ref, count_ref, src_hbm, cos_hbm, h_hbm, ws_hbm, wm_hbm, wt_hbm, wf_hbm, gate_w_hbm, cot_hbm,
-    h_t_ref, w_ref, own_ref, hot_ref, part_ref, live_ref, cot_live_ref, cos_t_ref,
-    h_ref, gate_w_ref, cot_ref, src_ref, cos_ref, sems,
+    odd_ref, count_ref, src_ref, cos_ref, h_ref, w_ref, gate_w_ref, cot_ref,
+    h_t_ref, own_ref, hot_ref, part_ref, live_ref, cot_live_ref, cos_t_ref,
 ):
-    first = [pltpu.make_async_copy(src_hbm, src_ref, sems.at[7]), pltpu.make_async_copy(cos_hbm, cos_ref, sems.at[8])]
-    copies = [
-        pltpu.make_async_copy(ref, w_ref.at[pl.ds(64 * n, 64)], sems.at[n])
-        for n, ref in enumerate((ws_hbm, wm_hbm, wt_hbm, wf_hbm))
-    ]
-    copies.append(pltpu.make_async_copy(h_hbm, h_ref, sems.at[4]))
-    copies.append(pltpu.make_async_copy(gate_w_hbm, gate_w_ref, sems.at[5]))
-    copies.append(pltpu.make_async_copy(cot_hbm, cot_ref, sems.at[6]))
-    for copy in first + copies:
-        copy.start()
     odd = odd_ref[0]
-    for copy in first:
-        copy.wait()
     src, cos = by_slot(src_ref, cos_ref)
     cos_t_ref[...] = cos
     low_base = jnp.where(odd == 1, CAP, CAP + GHOST)
@@ -109,8 +143,6 @@
     near_id = lax.broadcasted_iota(jnp.int32, (CAP, CAP), 0).astype(F32).astype(BF16)
     far_id = lax.broadcasted_iota(jnp.int32, (2 * GHOST, CAP), 0).astype(F32).astype(BF16)
     one, zero = jnp.ones((), BF16), jnp.zeros((), BF16)
-    for copy in copies:
-        copy.wait()
     live = live_row(count_ref[0])
     live_ref[...] = jnp.broadcast_to(live, (8, CAP))
     cot_live_ref[...] = cot_ref[...].astype(F32) * live
@@ -138,7 +170,6 @@
         prep_kernel,
         out_shape=(
             stay((256, CAP), BF16),
-            stay((256, 256), BF16),
             stay((128, CAP), F32),
             stay((EXT, ARITY * CAP), BF16),
             stay((ARITY, 128, CAP), F32),
@@ -146,19 +177,11 @@
             stay((64, CAP), F32),
             stay((16, CAP), F32),
         ),
-        in_specs=[SMEM, SMEM] + [HBM] * 9,
-        out_specs=(VMEM,) * 8,
-        scratch_shapes=[
-            pltpu.VMEM((CAP, 256), BF16),
-            pltpu.VMEM((1, 64), F32),
-            pltpu.VMEM((64, CAP), BF16),
-            pltpu.VMEM((24, 128), jnp.int32),
-            pltpu.VMEM((24, 128), F32),
-            pltpu.SemaphoreType.DMA((9,)),
-        ],
+        in_specs=[SMEM, SMEM] + [VMEM] * 6,
+        out_specs=(VMEM,) * 7,
         compiler_params=pltpu.CompilerParams(vmem_limit_bytes=24 << 20),
         name="prep_stage",
-    )(odd, count, *(in_hbm(x) for x in held))
+    )(odd, count, *(in_vmem(x) for x in held))
 
 
 def angle_kernel(
@@ -346,14 +369,9 @@
 ):
     odd = lax.axis_index("dom_2").astype(jnp.int32)
     is_odd = odd == 1
-    first, last = bond_feats[:GHOST], bond_feats[CAP - GHOST :]
-    to_b, to_a = jnp.where(is_odd, last, first), jnp.where(is_odd, first, last)
-    ghost_b = swap_chip(to_b)
-    ghost_a = swap_core(to_a)
     odd = odd.reshape(1)
-    h_t, *prepared = prep_stage(
+    to_a, to_b, src, cos, own_h, w_t, *rest = front_stage(
         odd,
-        bond_count,
         source.reshape(24, 128),
         cosine.reshape(24, 128),
         bond_feats,
@@ -364,6 +382,10 @@
         gate_angle[None, :],
         cotangent.T,
     )
+    ghost_b = swap_chip(to_b)
+    ghost_a = swap_core(to_a)
+    h_t, *prepared = prep_stage(odd, bond_count, src, cos, own_h, w_t, *rest)
+    prepared.insert(0, w_t)
     whole, *found = angle_stage(ghost_a, ghost_b, *prepared)
     tiles = lax.all_to_all(whole.reshape(4, 64, EXT), "wa", 0, 0, tiled=True)
     send, keep = grads_stage(odd, ghost_a, ghost_b, h_t, *found)

time: 59.7 us -> 58.5 us (0.980)
  starting transfers between devices: 38.1 us -> 37.1 us
  other arithmetic: 1.48 us -> 0.74 us
  waiting for transfers between devices: 11.2 us -> 11.9 us
    ppermute x2, waiting for transfers between devices: 0.23 us -> 1.26 us  [swap_chip(): lax.ppermute(x, DOM, [(i, (i + 1) % NDOM if i % 2 else (i - 1) % NDOM) fo...]
    ppermute x3, starting transfers between devices: 23.9 us -> 22.9 us  [swap_core(): return lax.ppermute(x, DOM, [(i, i ^ 1) for i in range(NDOM)])]
    select_n x1 -> x0, other arithmetic: 0.74 us -> none  [per_device(): jnp.where(is_odd, last, first)]
    pallas_call x1 -> x2, Pallas kernels: 2.23 us -> 2.31 us  [the longest x1 1.21 us: prep_stage(): pl.pallas_call(prep_kernel, out_shape=(stay((256, CAP), BF16), stay((128,...]
  transfers between devices with their start and end apart: 7 -> 7, of which waited for: 2 -> 2; matrix products, arithmetic and copies ran while one was open for 3% -> 3% of each run, Pallas kernels for 5% -> 3%
where the time goes in v6:
time: 58.5 us; the launch traced here: 58.1 us
  starting transfers between devices  37.1 us (63%)
  waiting for transfers between devices  11.9 us (20%)
  Pallas kernels  6.2 us (11%)
  between operations  1.42 us (2%)
  local copies, waits for them, and re-layouts  0.82 us (1%)
  other arithmetic  0.74 us (1%)
    ppermute x3, starting transfers between devices, swap_core(): return lax.ppermute(x, DOM, [(i, i ^ 1) for i in range(NDOM)])  22.9 us
    all_to_all x1, waiting for transfers between devices, per_device(): slots = lax.all_to_all(slots, CHIP, 0, 0, tiled=True)  10.6 us
    all_to_all x1, starting transfers between devices, per_device(): slots = lax.all_to_all(slots, CHIP, 0, 0, tiled=True)  6.96 us
    ppermute x2, starting transfers between devices, swap_chip(): lax.ppermute(x, DOM, [(i, (i + 1) % NDOM if i % 2 else (i - 1) % NDOM) fo...  3.84 us
    all_to_all x1, starting transfers between devices, per_device(): tiles = lax.all_to_all(whole.reshape(4, 64, EXT), 'wa', 0, 0, tiled=True)  3.36 us
    pallas_call x1, Pallas kernels, angle_stage(): pl.pallas_call(angle_kernel, out_shape=(stay((256, EXT), BF16), stay((CAP...  2.55 us
    ppermute x2, waiting for transfers between devices, swap_chip(): lax.ppermute(x, DOM, [(i, (i + 1) % NDOM if i % 2 else (i - 1) % NDOM) fo...  1.26 us
    pallas_call x1, Pallas kernels, prep_stage(): pl.pallas_call(prep_kernel, out_shape=(stay((256, CAP), BF16), stay((128,...  1.21 us
  transfers between devices with their start and end apart: 7, of which 2 were waited for; matrix products, arithmetic and copies ran while one was open for 3% of the time, Pallas kernels for 3%

profile of v6, /device:TPU:1, one launch (start us, length us, event | category | flops | bytes accessed | tf_op | source)
XLA Modules:
  0.0 58.1 jit_solution(2953105790885191994)
XLA Ops:
  0.6 1.1 %front_stage.1 = (bf16[32,256]{1,0:T(8,128)(2,1)S(1)}, bf16[32,256]{1,0:T(8,128)(2,1)S(1)}, s32[24,128]{1,0:T(8,128)S(1)}, f32[24,128]{1,0:T(8,128)S(1)}, bf16[2...) custom-call(s32[1]{0:T(128)} %bitcast.odd_ref, ...), custom_call_target="tpu_custom_call" | custom-call | tf_op jit(solution)/shard_map/front_stage/pallas_call | solution.py:83
  1.8 8.7 %collective-permute-start = (bf16[32,256]{1,0:T(8,128)(2,1)S(1)}, bf16[32,256]{1,0:T(8,128)(2,1)S(1)}, u32[]{:S(2)}, u32[]{:S(2)}) collective-permute-start(bf16[32,256]{1,0:T(8,128)(2,1)S(1)} %get-tuple-element.32), channel_id=1, source_target_pairs={{0,4},{4,0},{8,12},{12,8},{16,20},{20,16},{24,28},{28,24},{32,36},... | collective-permute-start | bytes 49160 | tf_op jit(solution)/shard_map/ppermute | solution.py:351
  10.5 1.9 %collective-permute-start.1 = (bf16[32,256]{1,0:T(8,128)(2,1)S(1)}, bf16[32,256]{1,0:T(8,128)(2,1)S(1)}, u32[]{:S(2)}, u32[]{:S(2)}) collective-permute-start(bf16[32,256]{1,0:T(8,128)(2,1)S(1)} %get-tuple-element.33), channel_id=1, source_target_pairs={{0,508},{4,8},{8,4},{12,16},{16,12},{20,24},{24,20},{28,32},{32,28... | collective-permute-start | bytes 49160 | tf_op jit(solution)/shard_map/ppermute | solution.py:355
  13.1 1.2 %prep_stage.1 = (bf16[256,256]{1,0:T(8,128)(2,1)S(1)}, f32[128,256]{1,0:T(8,128)S(1)}, bf16[320,3072]{1,0:T(8,128)(2,1)S(1)}, f32[12,128,256]{2,1,0:T(8,128)S(1)...) custom-call(s32[1]{0:T(128)} %bitcast.odd_ref, s32[1]{0:T(128)S(6)} %copy.16.count_ref, ...), custom_call_target="tpu_custom_call" | custom-call | tf_op jit(solution)/shard_map/prep_stage/pallas_call | solution.py:169
  14.3 0.0 collective-permute-done.ga_ref
  14.3 1.3 %collective-permute-done.1.gb_ref = bf16[32,256]{1,0:T(8,128)(2,1)S(1)} collective-permute-done((bf16[32,256]{1,0:T(8,128)(2,1)S(1)}, bf16[32,256]{1,0:T(8,128)(2,1)S(1)}, u32[]{:S(2)}, u32[]{:S(2)}) %collective-permute-start.1) | collective-permute-done | bytes 16416 | tf_op jit(solution)/shard_map/ppermute | solution.py:355
  15.6 2.6 %angle_stage.1 = (bf16[256,320]{1,0:T(8,128)(2,1)}, bf16[256,256]{1,0:T(8,128)(2,1)S(1)}, bf16[64,128]{1,0:T(8,128)(2,1)S(1)}, f32[64,256]{1,0:T(8,128)S(1)}) custom-call(bf16[32,256]{1,0:T(8,128)(2,1)S(1)} %collective-permute-done.ga_ref, bf16[32,256]{1,0:T(8,128)(2,1)S(1)} %collective-permute-done.1.gb_ref, bf16[256,256]{1,0:T(8,128)(2,1)S(1)} %get-tuple-element.34.w_ref, ...), custom_call_target="tpu_custom_call" | custom-call | tf_op jit(solution)/shard_map/angle_stage/pallas_call | solution.py:252
  18.1 3.4 %all-to-all-start = ((bf16[4,64,320]{2,1,0:T(8,128)(2,1)}), bf16[4,64,320]{2,1,0:T(8,128)(2,1)S(1)}, u32[]{:S(2)}, u32[]{:S(2)}) async-start(bf16[4,64,320]{2,1,0:T(8,128)(2,1)} %bitcast.9), calls=%async_computation | async-start | bytes 393216 | tf_op jit(solution)/shard_map/all_to_all | solution.py:390
  21.5 0.4 grads_stage.1
  21.9 8.3 %collective-permute-start.4 = (bf16[144,256]{1,0:T(8,128)(2,1)S(1)}, bf16[144,256]{1,0:T(8,128)(2,1)S(1)}, u32[]{:S(2)}, u32[]{:S(2)}) collective-permute-start(bf16[144,256]{1,0:T(8,128)(2,1)S(1)} %get-tuple-element.52), channel_id=1, source_target_pairs={{0,4},{4,0},{8,12},{12,8},{16,20},{20,16},{24,28},{28,24},{32,36},... | collective-permute-start | bytes 221192 | tf_op jit(solution)/shard_map/ppermute | solution.py:351
  30.2 0.0 all-to-all-done
  30.3 0.1 fusion.3
  30.3 5.9 %collective-permute-start.2 = (f32[64,32]{1,0:T(8,128)S(1)}, f32[64,32]{1,0:T(8,128)S(1)}, u32[]{:S(2)}, u32[]{:S(2)}) collective-permute-start(f32[64,32]{1,0:T(8,128)S(1)} %get-tuple-element.58), channel_id=1, source_target_pairs={{0,4},{4,0},{8,12},{12,8},{16,20},{20,16},{24,28},{28,24},{32,36},... | collective-permute-start | bytes 24584 | tf_op jit(solution)/shard_map/ppermute | solution.py:351
  36.2 1.9 %collective-permute-start.3 = (f32[64,32]{1,0:T(8,128)S(1)}, f32[64,32]{1,0:T(8,128)S(1)}, u32[]{:S(2)}, u32[]{:S(2)}) collective-permute-start(f32[64,32]{1,0:T(8,128)S(1)} %get-tuple-element.59), channel_id=1, source_target_pairs={{0,508},{4,8},{8,4},{12,16},{16,12},{20,24},{24,20},{28,32},{32,28... | collective-permute-start | bytes 24584 | tf_op jit(solution)/shard_map/ppermute | solution.py:355
  38.2 0.1 pad.1.clone
  38.2 0.0 collective-permute-done.4.recv_ref
  38.2 0.2 pair_stage.1
  38.4 0.7 %reshape.31 = bf16[64,2,384]{2,1,0:T(2,128)(2,1)} reshape(bf16[128,384]{1,0:T(8,128)(2,1)S(1)} %pair_stage.1) | data formatting | bytes 196608 | tf_op jit(solution)/shard_map/reshape | solution.py:393
  39.1 7.0 %all-to-all-start.1 = ((bf16[64,2,384]{2,1,0:T(2,128)(2,1)}), bf16[64,2,384]{2,1,0:T(2,128)(2,1)S(1)}, u32[]{:S(2)}, u32[]{:S(2)}) async-start(bf16[64,2,384]{2,1,0:T(2,128)(2,1)} %reshape.31), calls=%async_computation.1 | async-start | bytes 196608 | tf_op jit(solution)/shard_map/all_to_all | solution.py:394
  46.0 0.0 collective-permute-done.2
  46.0 0.0 collective-permute-done.3
  46.1 0.7 %fusion.2 = bf16[256,64]{0,1:T(8,128)(2,1)} fusion(f32[64,32]{1,0:T(8,128)S(1)} %get-tuple-element.61, f32[64,32]{1,0:T(8,128)S(1)} %get-tuple-element.60, f32[64,256]{1,0:T(8,128)S(1)} %get-tuple-element.44.cot_live_ref, f32[64,320]{1,0:T(8,128)S(1)} %convert_reduce_fusion, f32[256]{0:T(256)S(1)} %pad.1.clone), kind=kLoop, calls=%fused_computation.4 | loop fusion | flops 81920 | bytes 181248 | tf_op jit(solution)/shard_map/transpose | solution.py:405
  46.8 10.6 %all-to-all-done.1.slots_ref = bf16[64,2,384]{2,1,0:T(2,128)(2,1)S(1)} async-done(((bf16[64,2,384]{2,1,0:T(2,128)(2,1)}), bf16[64,2,384]{2,1,0:T(2,128)(2,1)S(1)}, u32[]{:S(2)}, u32[]{:S(2)}) %all-to-all-start.1) | async-done | bytes 98336 | tf_op jit(solution)/shard_map/all_to_all | solution.py:394
  57.3 0.7 %last_stage.1 = (f32[2,64]{1,0:T(2,128)}, f32[2,64]{1,0:T(2,128)}, f32[2,64]{1,0:T(2,128)}, f32[2,64]{1,0:T(2,128)}, f32[1,64]{1,0:T(1,128)}) custom-call(bf16[64,2,384]{2,1,0:T(2,128)(2,1)S(1)} %all-to-all-done.1.slots_ref), custom_call_target="tpu_custom_call" | custom-call | tf_op jit(solution)/shard_map/last_stage/pallas_call | solution.py:340
  (3 shorter events, 0.0 us)
Async XLA Ops:
  1.8 12.5 %collective-permute-start = (bf16[32,256]{1,0:T(8,128)(2,1)S(1)}, bf16[32,256]{1,0:T(8,128)(2,1)S(1)}, u32[]{:S(2)}, u32[]{:S(2)}) collective-permute-start(bf16[32,256]{1,0:T(8,128)(2,1)S(1)} %get-tuple-element.32), channel_id=1, source_target_pairs={{0,4},{4,0},{8,12},{12,8},{16,20},{20,16},{24,28},{28,24},{32,36},... | collective-permute-start | bytes 49160 | tf_op jit(solution)/shard_map/ppermute | solution.py:351
  10.5 5.1 %collective-permute-start.1 = (bf16[32,256]{1,0:T(8,128)(2,1)S(1)}, bf16[32,256]{1,0:T(8,128)(2,1)S(1)}, u32[]{:S(2)}, u32[]{:S(2)}) collective-permute-start(bf16[32,256]{1,0:T(8,128)(2,1)S(1)} %get-tuple-element.33), channel_id=1, source_target_pairs={{0,508},{4,8},{8,4},{12,16},{16,12},{20,24},{24,20},{28,32},{32,28... | collective-permute-start | bytes 49160 | tf_op jit(solution)/shard_map/ppermute | solution.py:355
  18.1 12.1 %all-to-all-start = ((bf16[4,64,320]{2,1,0:T(8,128)(2,1)}), bf16[4,64,320]{2,1,0:T(8,128)(2,1)S(1)}, u32[]{:S(2)}, u32[]{:S(2)}) async-start(bf16[4,64,320]{2,1,0:T(8,128)(2,1)} %bitcast.9), calls=%async_computation | async-start | bytes 393216 | tf_op jit(solution)/shard_map/all_to_all | solution.py:390
  21.9 16.3 %collective-permute-start.4 = (bf16[144,256]{1,0:T(8,128)(2,1)S(1)}, bf16[144,256]{1,0:T(8,128)(2,1)S(1)}, u32[]{:S(2)}, u32[]{:S(2)}) collective-permute-start(bf16[144,256]{1,0:T(8,128)(2,1)S(1)} %get-tuple-element.52), channel_id=1, source_target_pairs={{0,4},{4,0},{8,12},{12,8},{16,20},{20,16},{24,28},{28,24},{32,36},... | collective-permute-start | bytes 221192 | tf_op jit(solution)/shard_map/ppermute | solution.py:351
  30.3 15.7 %collective-permute-start.2 = (f32[64,32]{1,0:T(8,128)S(1)}, f32[64,32]{1,0:T(8,128)S(1)}, u32[]{:S(2)}, u32[]{:S(2)}) collective-permute-start(f32[64,32]{1,0:T(8,128)S(1)} %get-tuple-element.58), channel_id=1, source_target_pairs={{0,4},{4,0},{8,12},{12,8},{16,20},{20,16},{24,28},{28,24},{32,36},... | collective-permute-start | bytes 24584 | tf_op jit(solution)/shard_map/ppermute | solution.py:351
  36.2 9.8 %collective-permute-start.3 = (f32[64,32]{1,0:T(8,128)S(1)}, f32[64,32]{1,0:T(8,128)S(1)}, u32[]{:S(2)}, u32[]{:S(2)}) collective-permute-start(f32[64,32]{1,0:T(8,128)S(1)} %get-tuple-element.59), channel_id=1, source_target_pairs={{0,508},{4,8},{8,4},{12,16},{16,12},{20,24},{24,20},{28,32},{32,28... | collective-permute-start | bytes 24584 | tf_op jit(solution)/shard_map/ppermute | solution.py:355
  39.1 18.3 %all-to-all-start.1 = ((bf16[64,2,384]{2,1,0:T(2,128)(2,1)}), bf16[64,2,384]{2,1,0:T(2,128)(2,1)S(1)}, u32[]{:S(2)}, u32[]{:S(2)}) async-start(bf16[64,2,384]{2,1,0:T(2,128)(2,1)} %reshape.31), calls=%async_computation.1 | async-start | bytes 196608 | tf_op jit(solution)/shard_map/all_to_all | solution.py:394

commit v7 on v6

--- a/solution.py
+++ b/solution.py
@@ -55,17 +55,17 @@
 
 def front_kernel(
     odd_ref, src_hbm, cos_hbm, h_hbm, ws_hbm, wm_hbm, wt_hbm, wf_hbm, gate_w_hbm, cot_hbm,
-    to_a_ref, to_b_ref, src_ref, cos_ref, h_ref, w_ref, gate_w_ref, cot_ref,
-    sems,
+    to_a_ref, to_b_ref, src_t_ref, cos_t_ref, h_ref, w_ref, gate_w_ref, cot_ref,
+    src_ref, cos_ref, sems,
 ):
     odd = odd_ref[0]
     at_a = pl.multiple_of((1 - odd) * (CAP - GHOST), GHOST)
     at_b = pl.multiple_of(odd * (CAP - GHOST), GHOST)
     pairs = [
+        (src_hbm, src_ref),
+        (cos_hbm, cos_ref),
         (h_hbm.at[pl.ds(at_b, GHOST)], to_b_ref),
         (h_hbm.at[pl.ds(at_a, GHOST)], to_a_ref),
-        (src_hbm, src_ref),
-        (cos_hbm, cos_ref),
         (h_hbm, h_ref),
         (gate_w_hbm, gate_w_ref),
         (cot_hbm, cot_ref),
@@ -75,7 +75,10 @@
     copies = [pltpu.make_async_copy(a, b, sems.at[n]) for n, (a, b) in enumerate(pairs)]
     for copy in copies:
         copy.start()
-    for copy in copies:
+    for copy in copies[:2]:
+        copy.wait()
+    src_t_ref[...], cos_t_ref[...] = by_slot(src_ref, cos_ref)
+    for copy in copies[2:]:
         copy.wait()
 
 
@@ -85,8 +88,8 @@
         out_shape=(
             stay((GHOST, 256), BF16),
             stay((GHOST, 256), BF16),
-            stay((24, 128), jnp.int32),
-            stay((24, 128), F32),
+            stay((16, CAP), jnp.int32),
+            stay((16, CAP), F32),
             stay((CAP, 256), BF16),
             stay((256, 256), BF16),
             stay((1, 64), F32),
@@ -94,7 +97,11 @@
         ),
         in_specs=[SMEM] + [HBM] * 9,
         out_specs=(VMEM,) * 8,
-        scratch_shapes=[pltpu.SemaphoreType.DMA((11,))],
+        scratch_shapes=[
+            pltpu.VMEM((24, 128), jnp.int32),
+            pltpu.VMEM((24, 128), F32),
+            pltpu.SemaphoreType.DMA((11,)),
+        ],
         compiler_params=pltpu.CompilerParams(vmem_limit_bytes=24 << 20),
         name="front_stage",
     )(odd, *(in_hbm(x) for x in held))
@@ -126,11 +133,10 @@
 
 def prep_kernel(
     odd_ref, count_ref, src_ref, cos_ref, h_ref, w_ref, gate_w_ref, cot_ref,
-    h_t_ref, own_ref, hot_ref, part_ref, live_ref, cot_live_ref, cos_t_ref,
+    h_t_ref, own_ref, hot_ref, part_ref, live_ref, cot_live_ref,
 ):
     odd = odd_ref[0]
-    src, cos = by_slot(src_ref, cos_ref)
-    cos_t_ref[...] = cos
+    src, cos = src_ref[...], cos_ref[...]
     low_base = jnp.where(odd == 1, CAP, CAP + GHOST)
     high_base = jnp.where(odd == 1, CAP + GHOST, CAP)
     row = jnp.where(
@@ -175,10 +181,9 @@
             stay((ARITY, 128, CAP), F32),
             stay((8, CAP), F32),
             stay((64, CAP), F32),
-            stay((16, CAP), F32),
         ),
         in_specs=[SMEM, SMEM] + [VMEM] * 6,
-        out_specs=(VMEM,) * 7,
+        out_specs=(VMEM,) * 6,
         compiler_params=pltpu.CompilerParams(vmem_limit_bytes=24 << 20),
         name="prep_stage",
     )(odd, count, *(in_vmem(x) for x in held))
@@ -385,7 +390,7 @@
     ghost_b = swap_chip(to_b)
     ghost_a = swap_core(to_a)
     h_t, *prepared = prep_stage(odd, bond_count, src, cos, own_h, w_t, *rest)
-    prepared.insert(0, w_t)
+    prepared = [w_t, *prepared, cos]
     whole, *found = angle_stage(ghost_a, ghost_b, *prepared)
     tiles = lax.all_to_all(whole.reshape(4, 64, EXT), "wa", 0, 0, tiled=True)
     send, keep = grads_stage(odd, ghost_a, ghost_b, h_t, *found)

time: 58.5 us -> 58.8 us (level)
  transfers between devices with their start and end apart: 7 -> 7, of which waited for: 2 -> 2; matrix products, arithmetic and copies ran while one was open for 3% -> 3% of each run, Pallas kernels for 3% -> 2%
where the time goes in v7:
time: 58.8 us; the launch traced here: 58.4 us
  starting transfers between devices  37 us (63%)
  waiting for transfers between devices  12.3 us (21%)
  Pallas kernels  6.17 us (10%)
  between operations  1.42 us (2%)
  local copies, waits for them, and re-layouts  0.82 us (1%)
  other arithmetic  0.74 us (1%)
    ppermute x3, starting transfers between devices, swap_core(): return lax.ppermute(x, DOM, [(i, i ^ 1) for i in range(NDOM)])  22.5 us
    all_to_all x1, waiting for transfers between devices, per_device(): slots = lax.all_to_all(slots, CHIP, 0, 0, tiled=True)  10.6 us
    all_to_all x1, starting transfers between devices, per_device(): slots = lax.all_to_all(slots, CHIP, 0, 0, tiled=True)  7.32 us
    ppermute x2, starting transfers between devices, swap_chip(): lax.ppermute(x, DOM, [(i, (i + 1) % NDOM if i % 2 else (i - 1) % NDOM) fo...  3.84 us
    all_to_all x1, starting transfers between devices, per_device(): tiles = lax.all_to_all(whole.reshape(4, 64, EXT), 'wa', 0, 0, tiled=True)  3.36 us
    pallas_call x1, Pallas kernels, angle_stage(): pl.pallas_call(angle_kernel, out_shape=(stay((256, EXT), BF16), stay((CAP...  2.58 us
    ppermute x2, waiting for transfers between devices, swap_chip(): lax.ppermute(x, DOM, [(i, (i + 1) % NDOM if i % 2 else (i - 1) % NDOM) fo...  1.69 us
    pallas_call x1, Pallas kernels, front_stage(): pl.pallas_call(front_kernel, out_shape=(stay((GHOST, 256), BF16), stay((G...  1.48 us
  transfers between devices with their start and end apart: 7, of which 2 were waited for; matrix products, arithmetic and copies ran while one was open for 3% of the time, Pallas kernels for 2%

profile of v7, /device:TPU:1, one launch (start us, length us, event | category | flops | bytes accessed | tf_op | source)
XLA Modules:
  0.0 58.4 jit_solution(8769378154105269487)
XLA Ops:
  0.6 1.5 %front_stage.1 = (bf16[32,256]{1,0:T(8,128)(2,1)S(1)}, bf16[32,256]{1,0:T(8,128)(2,1)S(1)}, s32[16,256]{1,0:T(8,128)S(1)}, f32[16,256]{1,0:T(8,128)S(1)}, bf16[2...) custom-call(s32[1]{0:T(128)} %bitcast.odd_ref, ...), custom_call_target="tpu_custom_call" | custom-call | tf_op jit(solution)/shard_map/front_stage/pallas_call | solution.py:86
  2.1 8.7 %collective-permute-start = (bf16[32,256]{1,0:T(8,128)(2,1)S(1)}, bf16[32,256]{1,0:T(8,128)(2,1)S(1)}, u32[]{:S(2)}, u32[]{:S(2)}) collective-permute-start(bf16[32,256]{1,0:T(8,128)(2,1)S(1)} %get-tuple-element.31), channel_id=1, source_target_pairs={{0,4},{4,0},{8,12},{12,8},{16,20},{20,16},{24,28},{28,24},{32,36},... | collective-permute-start | bytes 49160 | tf_op jit(solution)/shard_map/ppermute | solution.py:356
  10.9 1.9 %collective-permute-start.1 = (bf16[32,256]{1,0:T(8,128)(2,1)S(1)}, bf16[32,256]{1,0:T(8,128)(2,1)S(1)}, u32[]{:S(2)}, u32[]{:S(2)}) collective-permute-start(bf16[32,256]{1,0:T(8,128)(2,1)S(1)} %get-tuple-element.32), channel_id=1, source_target_pairs={{0,508},{4,8},{8,4},{12,16},{16,12},{20,24},{24,20},{28,32},{32,28... | collective-permute-start | bytes 49160 | tf_op jit(solution)/shard_map/ppermute | solution.py:360
  13.5 0.8 %prep_stage.1 = (bf16[256,256]{1,0:T(8,128)(2,1)S(1)}, f32[128,256]{1,0:T(8,128)S(1)}, bf16[320,3072]{1,0:T(8,128)(2,1)S(1)}, f32[12,128,256]{2,1,0:T(8,128)S(1)...) custom-call(s32[1]{0:T(128)} %bitcast.odd_ref, s32[1]{0:T(128)S(6)} %copy.16.count_ref, ...), custom_call_target="tpu_custom_call" | custom-call | tf_op jit(solution)/shard_map/prep_stage/pallas_call | solution.py:175
  14.2 0.0 collective-permute-done.ga_ref
  14.3 1.7 %collective-permute-done.1.gb_ref = bf16[32,256]{1,0:T(8,128)(2,1)S(1)} collective-permute-done((bf16[32,256]{1,0:T(8,128)(2,1)S(1)}, bf16[32,256]{1,0:T(8,128)(2,1)S(1)}, u32[]{:S(2)}, u32[]{:S(2)}) %collective-permute-start.1) | collective-permute-done | bytes 16416 | tf_op jit(solution)/shard_map/ppermute | solution.py:360
  15.9 2.6 %angle_stage.1 = (bf16[256,320]{1,0:T(8,128)(2,1)}, bf16[256,256]{1,0:T(8,128)(2,1)S(1)}, bf16[64,128]{1,0:T(8,128)(2,1)S(1)}, f32[64,256]{1,0:T(8,128)S(1)}) custom-call(bf16[32,256]{1,0:T(8,128)(2,1)S(1)} %collective-permute-done.ga_ref, bf16[32,256]{1,0:T(8,128)(2,1)S(1)} %collective-permute-done.1.gb_ref, bf16[256,256]{1,0:T(8,128)(2,1)S(1)} %get-tuple-element.33.w_ref, ...), custom_call_target="tpu_custom_call" | custom-call | tf_op jit(solution)/shard_map/angle_stage/pallas_call | solution.py:257
  18.5 3.4 %all-to-all-start = ((bf16[4,64,320]{2,1,0:T(8,128)(2,1)}), bf16[4,64,320]{2,1,0:T(8,128)(2,1)S(1)}, u32[]{:S(2)}, u32[]{:S(2)}) async-start(bf16[4,64,320]{2,1,0:T(8,128)(2,1)} %bitcast.9), calls=%async_computation | async-start | bytes 393216 | tf_op jit(solution)/shard_map/all_to_all | solution.py:395
  21.9 0.4 grads_stage.1
  22.3 7.9 %collective-permute-start.4 = (bf16[144,256]{1,0:T(8,128)(2,1)S(1)}, bf16[144,256]{1,0:T(8,128)(2,1)S(1)}, u32[]{:S(2)}, u32[]{:S(2)}) collective-permute-start(bf16[144,256]{1,0:T(8,128)(2,1)S(1)} %get-tuple-element.50), channel_id=1, source_target_pairs={{0,4},{4,0},{8,12},{12,8},{16,20},{20,16},{24,28},{28,24},{32,36},... | collective-permute-start | bytes 221192 | tf_op jit(solution)/shard_map/ppermute | solution.py:356
  30.2 0.0 all-to-all-done
  30.2 0.1 fusion.3
  30.3 5.9 %collective-permute-start.2 = (f32[64,32]{1,0:T(8,128)S(1)}, f32[64,32]{1,0:T(8,128)S(1)}, u32[]{:S(2)}, u32[]{:S(2)}) collective-permute-start(f32[64,32]{1,0:T(8,128)S(1)} %get-tuple-element.56), channel_id=1, source_target_pairs={{0,4},{4,0},{8,12},{12,8},{16,20},{20,16},{24,28},{28,24},{32,36},... | collective-permute-start | bytes 24584 | tf_op jit(solution)/shard_map/ppermute | solution.py:356
  36.2 1.9 %collective-permute-start.3 = (f32[64,32]{1,0:T(8,128)S(1)}, f32[64,32]{1,0:T(8,128)S(1)}, u32[]{:S(2)}, u32[]{:S(2)}) collective-permute-start(f32[64,32]{1,0:T(8,128)S(1)} %get-tuple-element.57), channel_id=1, source_target_pairs={{0,508},{4,8},{8,4},{12,16},{16,12},{20,24},{24,20},{28,32},{32,28... | collective-permute-start | bytes 24584 | tf_op jit(solution)/shard_map/ppermute | solution.py:360
  38.1 0.1 pad.1.clone
  38.2 0.0 collective-permute-done.4.recv_ref
  38.2 0.2 pair_stage.1
  38.4 0.7 %reshape.31 = bf16[64,2,384]{2,1,0:T(2,128)(2,1)} reshape(bf16[128,384]{1,0:T(8,128)(2,1)S(1)} %pair_stage.1) | data formatting | bytes 196608 | tf_op jit(solution)/shard_map/reshape | solution.py:398
  39.0 7.3 %all-to-all-start.1 = ((bf16[64,2,384]{2,1,0:T(2,128)(2,1)}), bf16[64,2,384]{2,1,0:T(2,128)(2,1)S(1)}, u32[]{:S(2)}, u32[]{:S(2)}) async-start(bf16[64,2,384]{2,1,0:T(2,128)(2,1)} %reshape.31), calls=%async_computation.1 | async-start | bytes 196608 | tf_op jit(solution)/shard_map/all_to_all | solution.py:399
  46.4 0.0 collective-permute-done.2
  46.4 0.0 collective-permute-done.3
  46.4 0.7 %fusion.2 = bf16[256,64]{0,1:T(8,128)(2,1)} fusion(f32[64,32]{1,0:T(8,128)S(1)} %get-tuple-element.59, f32[64,32]{1,0:T(8,128)S(1)} %get-tuple-element.58, f32[64,256]{1,0:T(8,128)S(1)} %get-tuple-element.43.cot_live_ref, f32[64,320]{1,0:T(8,128)S(1)} %convert_reduce_fusion, f32[256]{0:T(256)S(1)} %pad.1.clone), kind=kLoop, calls=%fused_computation.4 | loop fusion | flops 81920 | bytes 181248 | tf_op jit(solution)/shard_map/transpose | solution.py:410
  47.1 10.6 %all-to-all-done.1.slots_ref = bf16[64,2,384]{2,1,0:T(2,128)(2,1)S(1)} async-done(((bf16[64,2,384]{2,1,0:T(2,128)(2,1)}), bf16[64,2,384]{2,1,0:T(2,128)(2,1)S(1)}, u32[]{:S(2)}, u32[]{:S(2)}) %all-to-all-start.1) | async-done | bytes 98336 | tf_op jit(solution)/shard_map/all_to_all | solution.py:399
  57.7 0.7 %last_stage.1 = (f32[2,64]{1,0:T(2,128)}, f32[2,64]{1,0:T(2,128)}, f32[2,64]{1,0:T(2,128)}, f32[2,64]{1,0:T(2,128)}, f32[1,64]{1,0:T(1,128)}) custom-call(bf16[64,2,384]{2,1,0:T(2,128)(2,1)S(1)} %all-to-all-done.1.slots_ref), custom_call_target="tpu_custom_call" | custom-call | tf_op jit(solution)/shard_map/last_stage/pallas_call | solution.py:345
  (3 shorter events, 0.0 us)
Async XLA Ops:
  2.1 12.1 %collective-permute-start = (bf16[32,256]{1,0:T(8,128)(2,1)S(1)}, bf16[32,256]{1,0:T(8,128)(2,1)S(1)}, u32[]{:S(2)}, u32[]{:S(2)}) collective-permute-start(bf16[32,256]{1,0:T(8,128)(2,1)S(1)} %get-tuple-element.31), channel_id=1, source_target_pairs={{0,4},{4,0},{8,12},{12,8},{16,20},{20,16},{24,28},{28,24},{32,36},... | collective-permute-start | bytes 49160 | tf_op jit(solution)/shard_map/ppermute | solution.py:356
  10.9 5.1 %collective-permute-start.1 = (bf16[32,256]{1,0:T(8,128)(2,1)S(1)}, bf16[32,256]{1,0:T(8,128)(2,1)S(1)}, u32[]{:S(2)}, u32[]{:S(2)}) collective-permute-start(bf16[32,256]{1,0:T(8,128)(2,1)S(1)} %get-tuple-element.32), channel_id=1, source_target_pairs={{0,508},{4,8},{8,4},{12,16},{16,12},{20,24},{24,20},{28,32},{32,28... | collective-permute-start | bytes 49160 | tf_op jit(solution)/shard_map/ppermute | solution.py:360
  18.5 11.7 %all-to-all-start = ((bf16[4,64,320]{2,1,0:T(8,128)(2,1)}), bf16[4,64,320]{2,1,0:T(8,128)(2,1)S(1)}, u32[]{:S(2)}, u32[]{:S(2)}) async-start(bf16[4,64,320]{2,1,0:T(8,128)(2,1)} %bitcast.9), calls=%async_computation | async-start | bytes 393216 | tf_op jit(solution)/shard_map/all_to_all | solution.py:395
  22.3 15.9 %collective-permute-start.4 = (bf16[144,256]{1,0:T(8,128)(2,1)S(1)}, bf16[144,256]{1,0:T(8,128)(2,1)S(1)}, u32[]{:S(2)}, u32[]{:S(2)}) collective-permute-start(bf16[144,256]{1,0:T(8,128)(2,1)S(1)} %get-tuple-element.50), channel_id=1, source_target_pairs={{0,4},{4,0},{8,12},{12,8},{16,20},{20,16},{24,28},{28,24},{32,36},... | collective-permute-start | bytes 221192 | tf_op jit(solution)/shard_map/ppermute | solution.py:356
  30.3 16.0 %collective-permute-start.2 = (f32[64,32]{1,0:T(8,128)S(1)}, f32[64,32]{1,0:T(8,128)S(1)}, u32[]{:S(2)}, u32[]{:S(2)}) collective-permute-start(f32[64,32]{1,0:T(8,128)S(1)} %get-tuple-element.56), channel_id=1, source_target_pairs={{0,4},{4,0},{8,12},{12,8},{16,20},{20,16},{24,28},{28,24},{32,36},... | collective-permute-start | bytes 24584 | tf_op jit(solution)/shard_map/ppermute | solution.py:356
  36.2 10.2 %collective-permute-start.3 = (f32[64,32]{1,0:T(8,128)S(1)}, f32[64,32]{1,0:T(8,128)S(1)}, u32[]{:S(2)}, u32[]{:S(2)}) collective-permute-start(f32[64,32]{1,0:T(8,128)S(1)} %get-tuple-element.57), channel_id=1, source_target_pairs={{0,508},{4,8},{8,4},{12,16},{16,12},{20,24},{24,20},{28,32},{32,28... | collective-permute-start | bytes 24584 | tf_op jit(solution)/shard_map/ppermute | solution.py:360
  39.0 18.7 %all-to-all-start.1 = ((bf16[64,2,384]{2,1,0:T(2,128)(2,1)}), bf16[64,2,384]{2,1,0:T(2,128)(2,1)S(1)}, u32[]{:S(2)}, u32[]{:S(2)}) async-start(bf16[64,2,384]{2,1,0:T(2,128)(2,1)} %reshape.31), calls=%async_computation.1 | async-start | bytes 196608 | tf_op jit(solution)/shard_map/all_to_all | solution.py:399
